TPU v7x, 256 devices: a whole 4x4x8 slice. The times are simulated.
256 devices in a mesh: row: 32 (over z, y_lo, core), col: 8 (over x, y_hi).
Axes of the slice: x: 4, y: 4 (y_hi: 2, y_lo: 2; y = y_hi * 2 + y_lo), z: 8, core: 2. Of those that a mesh axis runs over, the one named last changes fastest.
Arguments:
- half_panel: bfloat16 [48, 2048, 2048], P(None, 'row', 'col'), may hold values from -6 to 6
- orbitals: bfloat16 [2048, 2048], replicated, may hold values from -0.125 to 0.125
Outputs:
- integrals: bfloat16 [48, 2048, 2048], P(None, 'row', 'col')
All inputs are finite; a program needn't handle non-finite values.
Results may differ from a plain program's by a relative error of at most 0.0049.
Values may be sent and summed in bfloat16 or wider, within the bound.
No kernel may reach another device: no remote copies, remote signals or barrier semaphores. Data moves between devices by JAX's collectives and lax.ppermute only.
A program may use at most 64 MiB of HBM per device.

v0:
```python
import jax
import jax.numpy as jnp
from jax import lax
from jax.sharding import PartitionSpec as P


def per_device(half_panel, orbitals):
    row_count = lax.axis_size("row")
    col_count = lax.axis_size("col")
    pair_count, block_rows, block_cols = half_panel.shape
    orbital_count = orbitals.shape[0]
    width = orbital_count // (row_count * col_count)
    ratio = row_count // col_count
    lanes = pair_count * width
    strip = lax.axis_index("row") * col_count + lax.axis_index("col")
    rows_out = jnp.transpose(
        half_panel.reshape(pair_count, col_count, width, block_cols), (3, 1, 0, 2)
    )
    rows_out = rows_out.reshape(block_cols, col_count, 1, lanes)
    cols_out = jnp.transpose(
        half_panel.reshape(pair_count, block_rows, ratio, col_count, width), (2, 3, 1, 0, 4)
    )
    cols_out = cols_out.reshape(ratio, col_count, block_rows, lanes)
    upper = lax.all_to_all(rows_out, "col", split_axis=1, concat_axis=0, tiled=True)
    lower = lax.all_to_all(cols_out, "col", split_axis=1, concat_axis=0, tiled=True)
    lower = lax.all_to_all(lower, "row", split_axis=0, concat_axis=2, tiled=True)
    upper = upper.reshape(orbital_count, pair_count, width)
    lower = lower.reshape(orbital_count, pair_count, width)
    position = strip * width + jnp.arange(width, dtype=jnp.int32)
    column_index = jnp.arange(orbital_count, dtype=jnp.int32)
    keep_upper = position[None, :] <= column_index[:, None]
    symmetric = jnp.where(keep_upper[:, None, :], upper, lower)
    target = orbitals.reshape(orbital_count, col_count, row_count, width)
    partial_value = jnp.einsum(
        "qka,qcrb->crakb", symmetric, target, preferred_element_type=jnp.float32
    ).astype(jnp.bfloat16)
    partial_value = partial_value.reshape(col_count, row_count, width, lanes)
    half_way = lax.all_to_all(partial_value, "col", split_axis=0, concat_axis=2, tiled=True)
    gathered = lax.all_to_all(half_way, "row", split_axis=1, concat_axis=2, tiled=True)
    gathered = gathered.reshape(orbital_count, lanes)
    result = lax.dot_general(
        orbitals, gathered, (((0,), (0,)), ((), ())), preferred_element_type=jnp.float32
    ).astype(jnp.bfloat16)
    result = result.reshape(row_count, block_rows, lanes)
    placed = lax.all_to_all(result, "row", split_axis=0, concat_axis=0, tiled=True)
    placed = placed.reshape(row_count, block_rows, pair_count, width)
    return jnp.transpose(placed, (2, 1, 0, 3)).reshape(pair_count, block_rows, block_cols)


def solution(mesh):
    return jax.shard_map(
        per_device,
        mesh=mesh,
        in_specs=(P(None, "row", "col"), P()),
        out_specs=P(None, "row", "col"),
        check_vma=False,
    )
```

profile of v0, /device:TPU:2, one launch (start us, length us, event | category | flops | bytes accessed | tf_op | source)
XLA Modules:
  0.0 275.5 jit_solution(13273540249739405776)
XLA Ops:
  0.0 4.1 %copy.32 = bf16[48,64,256]{1,2,0:T(8,128)(2,1)} copy(bf16[48,64,256]{2,1,0:T(8,128)(2,1)} %param.2) | data formatting | bytes 3145728 | tf_op args[0]
  4.1 2.7 copy.62
  6.8 2.4 copy.34
  9.2 28.4 %all_to_all.74 = bf16[4,8,64,384]{3,2,0,1:T(8,128)(2,1)} all-to-all(bf16[4,8,64,384]{3,2,0,1:T(8,128)(2,1)} %copy.34), channel_id=1, replica_groups=mesh['row'=32,'col'=8] {'col'}, dimensions={1} | all-to-all | bytes 3145728 | tf_op jit(solution)/shard_map/all_to_all | solution.py:25
  37.6 0.0 copy-start
  37.6 9.1 %all-to-all-start.2 = ((bf16[32,1,64,384]{3,2,1,0:T(8,128)(2,1)}), bf16[32,1,64,384]{3,2,1,0:T(8,128)(2,1)S(1)}, u32[]{:S(2)}, u32[]{:S(2)}) async-start(bf16[32,1,64,384]{3,2,1,0:T(8,128)(2,1)} %bitcast.12), calls=%async_computation.2 | async-start | bytes 3145728 | tf_op jit(solution)/shard_map/all_to_all | solution.py:26
  46.7 0.0 copy-done
  46.8 1.3 copy_bitcast_fusion.4
  48.1 38.1 %all-to-all-done.2 = bf16[32,1,64,384]{3,2,1,0:T(8,128)(2,1)S(1)} async-done(((bf16[32,1,64,384]{3,2,1,0:T(8,128)(2,1)}), bf16[32,1,64,384]{3,2,1,0:T(8,128)(2,1)S(1)}, u32[]{:S(2)}, u32[]{:S(2)}) %all-to-all-start.2) | async-done | bytes 1572896 | tf_op jit(solution)/shard_map/all_to_all | solution.py:26
  86.2 5.5 %all-to-all-start = ((bf16[256,8,1,384]{0,3,2,1:T(8,128)(2,1)}), bf16[256,8,1,384]{0,3,2,1:T(8,128)(2,1)S(1)}, u32[]{:S(2)}, u32[]{:S(2)}) async-start(bf16[256,8,1,384]{0,3,2,1:T(8,128)(2,1)} %copy_bitcast_fusion.4), calls=%async_computation | async-start | bytes 3145728 | tf_op jit(solution)/shard_map/all_to_all | solution.py:24
  91.7 0.1 iota_compare_fusion
  91.8 0.4 broadcast_in_dim.13
  92.2 1.4 copy.48
  93.5 12.3 %copy.37 = bf16[2048,2048]{0,1:T(8,128)(2,1)} copy(bf16[2048,2048]{1,0:T(8,128)(2,1)} %param.3) | data formatting | bytes 16777216 | tf_op args[1]
  105.8 2.0 copy.36
  107.8 5.6 %all-to-all-done = bf16[256,8,1,384]{0,3,2,1:T(8,128)(2,1)S(1)} async-done(((bf16[256,8,1,384]{0,3,2,1:T(8,128)(2,1)}), bf16[256,8,1,384]{0,3,2,1:T(8,128)(2,1)S(1)}, u32[]{:S(2)}, u32[]{:S(2)}) %all-to-all-start) | async-done | bytes 1572896 | tf_op jit(solution)/shard_map/all_to_all | solution.py:24
  113.4 2.6 bitcast_select_fusion
  116.0 0.8 reshape.80
  116.8 15.9 %convert_bitcast_fusion = bf16[8,32,8,48,8]{1,2,4,0,3:T(8,128)(2,1)S(1)} fusion(bf16[2048,8,32,8]{0,3,2,1:T(8,128)(2,1)} %bitcast.76, bf16[2048,48,8,1,1]{0,2,1,3,4:T(8,128)(2,1)S(1)} %reshape.80), kind=kOutput, calls=%fused_computation.4 | convolution fusion | flops 3222011904 | bytes 11534336 | tf_op jit(solution)/shard_map/qka,qcrb->crakb/dot_general | solution.py:34
  132.7 4.3 %copy.61 = bf16[8,32,8,48,8]{1,4,3,2,0:T(8,128)(2,1)} copy(bf16[8,32,8,48,8]{1,2,4,0,3:T(8,128)(2,1)S(1)} %convert_bitcast_fusion) | data formatting | bytes 3145728 | tf_op jit(solution)/shard_map/convert_element_type | solution.py:36
  137.0 5.4 %copy.40 = bf16[8,32,8,384]{3,2,1,0:T(8,128)(2,1)S(1)} copy(bf16[8,32,8,384]{1,3,2,0:T(8,128)(2,1)} %bitcast.73) | data formatting | bytes 3145728 | tf_op jit(solution)/shard_map/reshape | solution.py:37
  142.4 25.2 %all_to_all.75 = bf16[8,32,8,384]{3,2,1,0:T(8,128)(2,1)S(1)} all-to-all(bf16[8,32,8,384]{3,2,1,0:T(8,128)(2,1)S(1)} %copy.40), channel_id=1, replica_groups=mesh['row'=32,'col'=8] {'col'}, dimensions={0} | all-to-all | bytes 3145728 | tf_op jit(solution)/shard_map/all_to_all | solution.py:38
  167.6 0.3 copy.63
  167.9 45.9 %all_to_all.76 = bf16[1,32,64,384]{3,2,0,1:T(8,128)(2,1)S(1)} all-to-all(bf16[1,32,64,384]{3,2,0,1:T(8,128)(2,1)S(1)} %bitcast.78), channel_id=1, replica_groups=mesh['row'=32,'col'=8] {'row'}, dimensions={1} | all-to-all | bytes 3145728 | tf_op jit(solution)/shard_map/all_to_all | solution.py:39
  213.8 6.9 %fusion.5 = bf16[2048,384]{0,1:T(8,128)(2,1)S(1)} fusion(bf16[2048,384]{1,0:T(8,128)(2,1)S(1)} %bitcast.82, bf16[2048,2048]{1,0:T(8,128)(2,1)} %param.3), kind=kOutput, calls=%fused_computation.8 | convolution fusion | flops 3222011904 | bytes 11534336 | tf_op jit(solution)/shard_map/dot_general | solution.py:41
  220.6 0.9 copy.43
  221.5 44.1 %all_to_all.77 = bf16[32,64,384]{2,1,0:T(8,128)(2,1)} all-to-all(bf16[32,64,384]{2,1,0:T(8,128)(2,1)S(1)} %bitcast.79), channel_id=1, replica_groups=mesh['row'=32,'col'=8] {'row'}, dimensions={0} | all-to-all | bytes 3145728 | tf_op jit(solution)/shard_map/all_to_all | solution.py:45
  265.6 3.1 %copy.44 = bf16[32,64,384]{1,2,0:T(8,128)(2,1)S(1)} copy(bf16[32,64,384]{2,1,0:T(8,128)(2,1)} %all_to_all.77) | data formatting | bytes 3145728 | tf_op jit(solution)/shard_map/all_to_all | solution.py:45
  268.7 2.5 copy_bitcast_fusion.1
  271.2 4.3 %copy.46 = bf16[48,64,256]{2,1,0:T(8,128)(2,1)} copy(bf16[48,64,256]{1,2,0:T(8,128)(2,1)} %copy_bitcast_fusion.1) | data formatting | bytes 3145728 | tf_op jit(solution)/shard_map/reshape | solution.py:47
  (1 shorter events, 0.0 us)
Async XLA Ops:
  37.6 9.1 %copy-start = (bf16[48,64,256]{2,1,0:T(8,128)(2,1)S(1)}, bf16[48,64,256]{2,1,0:T(8,128)(2,1)}, u32[]{:S(2)}) copy-start(bf16[48,64,256]{2,1,0:T(8,128)(2,1)} %param.2) | copy-start | bytes 4718596
  37.6 48.6 %all-to-all-start.2 = ((bf16[32,1,64,384]{3,2,1,0:T(8,128)(2,1)}), bf16[32,1,64,384]{3,2,1,0:T(8,128)(2,1)S(1)}, u32[]{:S(2)}, u32[]{:S(2)}) async-start(bf16[32,1,64,384]{3,2,1,0:T(8,128)(2,1)} %bitcast.12), calls=%async_computation.2 | async-start | bytes 3145728 | tf_op jit(solution)/shard_map/all_to_all | solution.py:26
  86.2 27.2 %all-to-all-start = ((bf16[256,8,1,384]{0,3,2,1:T(8,128)(2,1)}), bf16[256,8,1,384]{0,3,2,1:T(8,128)(2,1)S(1)}, u32[]{:S(2)}, u32[]{:S(2)}) async-start(bf16[256,8,1,384]{0,3,2,1:T(8,128)(2,1)} %copy_bitcast_fusion.4), calls=%async_computation | async-start | bytes 3145728 | tf_op jit(solution)/shard_map/all_to_all | solution.py:24
where the time goes:
time: 278 us; the launch traced here: 275 us
  blocking collectives  144 us (52%)
  local copies, waits for them, and re-layouts  48 us (17%)
  waiting for transfers between devices  43.7 us (16%)
  matrix products  22.8 us (8%)
  starting transfers between devices  14.6 us (5%)
    all_to_all x1, blocking collectives, per_device(): lax.all_to_all(half_way, 'row', split_axis=1, concat_axis=2, tiled=True)  45.9 us
    all_to_all x1, blocking collectives, per_device(): lax.all_to_all(result, 'row', split_axis=0, concat_axis=0, tiled=True)  44.1 us
    all_to_all x1, waiting for transfers between devices, per_device(): lax.all_to_all(lower, 'row', split_axis=0, concat_axis=2, tiled=True)  38.1 us
    all_to_all x1, blocking collectives, per_device(): lax.all_to_all(cols_out, 'col', split_axis=1, concat_axis=0, tiled=True)  28.4 us
    all_to_all x1, blocking collectives, per_device(): lax.all_to_all(partial_value, 'col', split_axis=0, concat_axis=2, tiled=T...  25.2 us
    unnamed x5, local copies, waits for them, and re-layouts  17.8 us
    dot_general x1, matrix products, per_device(): jnp.einsum('qka,qcrb->crakb', symmetric, target, preferred_element_type=j...  15.9 us
    all_to_all x1, starting transfers between devices, per_device(): lax.all_to_all(lower, 'row', split_axis=0, concat_axis=2, tiled=True)  9.1 us
  transfers between devices with their start and end apart: 2, of which 2 were waited for; matrix products, arithmetic and copies ran while one was open for 6% of the time, Pallas kernels for 0%

commit v1 on v0

v1 whole, which is shorter than its diff:
```python
import jax
import jax.numpy as jnp
from jax import lax
from jax.experimental import pallas as pl
from jax.experimental.pallas import tpu as pltpu
from jax.sharding import Mesh, PartitionSpec as P

Z, YLO, CORE, X, YHI = 8, 2, 2, 4, 2
COLS = X * YHI
PLANE = ("x", "yhi", "ylo")
F32 = jnp.float32
BF16 = jnp.bfloat16


def transposed(block):
    size = block.shape[1]
    row = lax.broadcasted_iota(jnp.int32, (size, size), 0)
    column = lax.broadcasted_iota(jnp.int32, (size, size), 1)
    eye = (row == column).astype(F32).astype(BF16)
    return lax.dot_general(
        eye, block, (((1,), (1,)), ((), ())), preferred_element_type=F32
    ).astype(BF16)


def pick_kernel(core_ref, c_ref, out_ref):
    half = c_ref.shape[1] // 4
    row = lax.broadcasted_iota(jnp.int32, (4 * half, 2 * half), 0)
    column = lax.broadcasted_iota(jnp.int32, (4 * half, 2 * half), 1)
    wanted = jnp.where(column < half, column, column + half) + core_ref[0] * half
    choose = (row == wanted).astype(F32).astype(BF16)
    out_ref[...] = jnp.dot(c_ref[...], choose, preferred_element_type=F32).astype(BF16)


def pick_columns(core, orbitals):
    size = orbitals.shape[0]
    block = size // Z
    return pl.pallas_call(
        pick_kernel,
        out_shape=jax.ShapeDtypeStruct((size, size // CORE), BF16),
        grid_spec=pltpu.PrefetchScalarGridSpec(
            num_scalar_prefetch=1,
            grid=(Z,),
            in_specs=[pl.BlockSpec((size, block), lambda g, s: (0, g))],
            out_specs=pl.BlockSpec((size, block // CORE), lambda g, s: (0, g)),
        ),
        name="pick_columns",
    )(core, orbitals)


def first_kernel(place, own, other, own_low, other_low, c_ref, t_ref, sym, turn):
    depth, rows = own.shape[2], own.shape[3]
    block = own.shape[4]
    z, core = place[0], place[1]

    @pl.when(pl.program_id(0) == 0)
    def _():
        def build(step, carry):
            k = step // Z
            b = step % Z
            base = pl.multiple_of(k * block, block)
            cols = pl.ds(pl.multiple_of(b * block, block), block)

            @pl.when(b >= z)
            def _():
                for y in range(YLO):
                    at = base + y * CORE * rows
                    sym[pl.ds(pl.multiple_of(at + core * rows, rows), rows), cols] = own[b, y, k]
                    sym[pl.ds(pl.multiple_of(at + (1 - core) * rows, rows), rows), cols] = other[b, y, k]

            @pl.when(b == z)
            def _():
                upper = sym[pl.ds(base, block), cols]
                lower = transposed(upper)
                row = lax.broadcasted_iota(jnp.int32, (block, block), 0)
                column = lax.broadcasted_iota(jnp.int32, (block, block), 1)
                sym[pl.ds(base, block), cols] = jnp.where(row <= column, upper, lower)

            @pl.when(b < z)
            def _():
                for y in range(YLO):
                    at = y * CORE * rows
                    turn[pl.ds(pl.multiple_of(at + core * rows, rows), rows), :] = own_low[b, y, k]
                    turn[pl.ds(pl.multiple_of(at + (1 - core) * rows, rows), rows), :] = other_low[b, y, k]
                sym[pl.ds(base, block), cols] = transposed(turn[...])

            return carry

        lax.fori_loop(0, depth * Z, build, 0)

    product = jnp.dot(sym[...], c_ref[...], preferred_element_type=F32).astype(BF16)
    lanes = t_ref.shape[3]
    for part in range(t_ref.shape[0]):
        for k in range(depth):
            t_ref[part, k] = product[k * block:(k + 1) * block, part * lanes:(part + 1) * lanes]


def first_half(place, own, other, own_low, other_low, picked):
    depth = own.shape[2]
    block = own.shape[4]
    size = picked.shape[0]
    lanes = picked.shape[1] // Z
    step = 2
    whole = pl.BlockSpec(own.shape, lambda g, s: (0, 0, 0, 0, 0))
    return pl.pallas_call(
        first_kernel,
        out_shape=jax.ShapeDtypeStruct((Z, depth, block, lanes), BF16),
        grid_spec=pltpu.PrefetchScalarGridSpec(
            num_scalar_prefetch=1,
            grid=(Z // step,),
            in_specs=[whole, whole, whole, whole,
                      pl.BlockSpec((size, step * lanes), lambda g, s: (0, g))],
            out_specs=pl.BlockSpec((step, depth, block, lanes), lambda g, s: (g, 0, 0, 0)),
            scratch_shapes=[pltpu.VMEM((depth * block, size), BF16),
                            pltpu.VMEM((block, block), BF16)],
        ),
        compiler_params=pltpu.CompilerParams(vmem_limit_bytes=48 * 2**20),
        name="first_half",
    )(place, own, other, own_low, other_low, picked)


def second_kernel(t_ref, c_ref, out_ref, left):
    count, depth, block, lanes = t_ref.shape
    rows = lanes // YLO

    @pl.when(pl.program_id(0) == 0)
    def _():
        for k in range(depth):
            for b in range(count):
                left[k * lanes:(k + 1) * lanes, b * block:(b + 1) * block] = transposed(t_ref[b, k])

    product = jnp.dot(left[...], c_ref[...], preferred_element_type=F32).astype(BF16)
    for k in range(depth):
        for y in range(YLO):
            at = k * lanes + y * rows
            out_ref[0, y, k] = product[at:at + rows]


def second_half(partial_value, orbitals):
    count, depth, block, lanes = partial_value.shape
    size = orbitals.shape[0]
    rows = lanes // YLO
    return pl.pallas_call(
        second_kernel,
        out_shape=jax.ShapeDtypeStruct((COLS, YLO, depth, rows, block), BF16),
        grid=(COLS,),
        in_specs=[pl.BlockSpec(partial_value.shape, lambda g: (0, 0, 0, 0)),
                  pl.BlockSpec((size, block), lambda g: (0, g))],
        out_specs=pl.BlockSpec((1, YLO, depth, rows, block), lambda g: (g, 0, 0, 0, 0)),
        scratch_shapes=[pltpu.VMEM((depth * lanes, size), BF16)],
        compiler_params=pltpu.CompilerParams(vmem_limit_bytes=48 * 2**20),
        name="second_half",
    )(partial_value, orbitals)


def swap_cores(value):
    return lax.ppermute(value, "core", [(0, 1), (1, 0)])


def per_device(half_panel, orbitals):
    pairs, rows, block = half_panel.shape
    depth = pairs // (COLS * YLO)
    place = jnp.stack([lax.axis_index("z"), lax.axis_index("core")]).astype(jnp.int32)
    picked = pick_columns(place[1:], orbitals)
    with jax.named_scope("panels_in"):
        own = half_panel.reshape(COLS * YLO, depth, rows, block)
        own = lax.all_to_all(own, PLANE, 0, 0, tiled=True)
        own = own.reshape(COLS, YLO, depth, rows, block)
    other = swap_cores(own)
    with jax.named_scope("mirror"):
        own_low = lax.all_to_all(own, "z", 0, 0, tiled=True)
    other_low = swap_cores(own_low)
    partial_value = first_half(place, own, other, own_low, other_low, picked)
    with jax.named_scope("partial"):
        partial_value = lax.all_to_all(partial_value, "z", 0, 0, tiled=True)
    result = second_half(partial_value, orbitals)
    with jax.named_scope("panels_out"):
        result = result.reshape(COLS * YLO, depth, rows, block)
        result = lax.all_to_all(result, PLANE, 0, 0, tiled=True)
    return result.reshape(pairs, rows, block)


def solution(mesh):
    fine = Mesh(mesh.devices.reshape(Z, YLO, CORE, X, YHI), ("z", "ylo", "core", "x", "yhi"))
    spec = P(None, ("z", "ylo", "core"), ("x", "yhi"))
    return jax.shard_map(
        per_device, mesh=fine, in_specs=(spec, P()), out_specs=spec, check_vma=False
    )
```

time: 278 us -> 175 us (0.63)
  local copies, waits for them, and re-layouts: 48 us -> 1.15 us
  blocking collectives: 144 us -> 98.8 us
  Pallas kernels: 0 us -> 27.4 us
  matrix products: 22.8 us -> 0 us
  starting transfers between devices: 14.6 us -> 8.49 us
  waiting for transfers between devices: 43.7 us -> 38.1 us
    all_to_all x4 -> x3, blocking collectives: 144 us -> 98.8 us  [the longest x1 45.3 us: per_device(): partial_value = lax.all_to_all(partial_value, 'z', 0, 0, tiled=True)]
    pallas_call x0 -> x3, Pallas kernels: none -> 27.4 us  [the longest x1 9.63 us: pick_columns(): pl.pallas_call(pick_kernel, out_shape=jax.ShapeDtypeStruct((size, size //...]
    dot_general x2 -> x0, matrix products: 22.8 us -> none  [the longest x1 15.9 us: per_device(): jnp.einsum('qka,qcrb->crakb', symmetric, target, preferred_element_type=j...]
    reshape x6 -> x0, local copies, waits for them, and re-layouts: 17.9 us -> none  [the longest x2 6.8 us: per_device(): jnp.transpose(placed, (2, 1, 0, 3))]
    unnamed x5 -> x3, local copies, waits for them, and re-layouts: 17.8 us -> 1.15 us
    all_to_all x2 -> x1, starting transfers between devices: 14.6 us -> 8.47 us  [per_device(): own_low = lax.all_to_all(own, 'z', 0, 0, tiled=True)]
    all_to_all x2 -> x1, waiting for transfers between devices: 43.7 us -> 38.1 us  [per_device(): own_low = lax.all_to_all(own, 'z', 0, 0, tiled=True)]
    convert_element_type x2 -> x0, local copies, waits for them, and re-layouts: 5.15 us -> none  [the longest x1 4.28 us: per_device(): partial_value = jnp.einsum('qka,qcrb->crakb', symmetric, target, preferre...]
  transfers between devices with their start and end apart: 2 -> 3, of which waited for: 2 -> 1; matrix products, arithmetic and copies ran while one was open for 6% -> 0% of each run, Pallas kernels for 0% -> 6%
where the time goes in v1:
time: 175 us; the launch traced here: 174 us
  blocking collectives  98.8 us (56%)
  waiting for transfers between devices  38.1 us (22%)
  Pallas kernels  27.4 us (16%)
  starting transfers between devices  8.49 us (5%)
    all_to_all x1, blocking collectives, per_device(): partial_value = lax.all_to_all(partial_value, 'z', 0, 0, tiled=True)  45.3 us
    all_to_all x1, waiting for transfers between devices, per_device(): own_low = lax.all_to_all(own, 'z', 0, 0, tiled=True)  38.1 us
    all_to_all x1, blocking collectives, per_device(): own = lax.all_to_all(own, PLANE, 0, 0, tiled=True)  28.4 us
    all_to_all x1, blocking collectives, per_device(): result = lax.all_to_all(result, PLANE, 0, 0, tiled=True)  25.1 us
    pallas_call x1, Pallas kernels, pick_columns(): pl.pallas_call(pick_kernel, out_shape=jax.ShapeDtypeStruct((size, size //...  9.63 us
    pallas_call x1, Pallas kernels, first_half(): pl.pallas_call(first_kernel, out_shape=jax.ShapeDtypeStruct((Z, depth, bl...  9.11 us
    pallas_call x1, Pallas kernels, second_half(): pl.pallas_call(second_kernel, out_shape=jax.ShapeDtypeStruct((COLS, YLO,...  8.63 us
    all_to_all x1, starting transfers between devices, per_device(): own_low = lax.all_to_all(own, 'z', 0, 0, tiled=True)  8.47 us
  transfers between devices with their start and end apart: 3, of which 1 were waited for; matrix products, arithmetic and copies ran while one was open for 0% of the time, Pallas kernels for 6%

profile of v1, /device:TPU:2, one launch (start us, length us, event | category | flops | bytes accessed | tf_op | source)
XLA Modules:
  0.0 174.0 jit_solution(14369160026460286555)
XLA Ops:
  0.0 28.4 %all_to_all.20 = bf16[16,3,64,256]{3,2,1,0:T(8,128)(2,1)} all-to-all(bf16[16,3,64,256]{3,2,1,0:T(8,128)(2,1)} %bitcast.8), channel_id=1, replica_groups=mesh['z'=8,'ylo'=2,'core'=2,'x'=4,'yhi'=2] {'x','yhi','ylo'}, dimensions={0} | all-to-all | bytes 3145728 | tf_op jit(solution)/shard_map/panels_in/all_to_all | solution.py:166
  28.4 8.5 %all-to-all-start.1 = ((bf16[8,2,3,64,256]{4,3,2,1,0:T(8,128)(2,1)}), bf16[8,2,3,64,256]{4,3,2,1,0:T(8,128)(2,1)S(1)}, u32[]{:S(2)}, u32[]{:S(2)}) async-start(bf16[8,2,3,64,256]{4,3,2,1,0:T(8,128)(2,1)} %bitcast.3.own), calls=%async_computation.1 | async-start | bytes 3145728 | tf_op jit(solution)/shard_map/mirror/all_to_all | solution.py:170
  36.8 0.0 collective-permute-start
  36.8 38.1 %all-to-all-done.1.own_low = bf16[8,2,3,64,256]{4,3,2,1,0:T(8,128)(2,1)S(1)} async-done(((bf16[8,2,3,64,256]{4,3,2,1,0:T(8,128)(2,1)}), bf16[8,2,3,64,256]{4,3,2,1,0:T(8,128)(2,1)S(1)}, u32[]{:S(2)}, u32[]{:S(2)}) %all-to-all-start.1) | async-done | bytes 1572896 | tf_op jit(solution)/shard_map/mirror/all_to_all | solution.py:170
  75.0 0.0 copy-start
  75.0 0.0 collective-permute-start.1
  75.0 9.6 %pick_columns.1.c_ref = bf16[2048,1024]{1,0:T(8,128)(2,1)} custom-call(s32[1]{0:T(128)} %bitcast.1.core_ref, bf16[2048,2048]{1,0:T(8,128)(2,1)} %c_ref.3), custom_call_target="tpu_custom_call" | custom-call | tf_op jit(solution)/shard_map/pick_columns/pallas_call | solution.py:37
  84.6 0.0 copy-done
  84.6 0.1 pad_add_fusion.place
  84.7 0.0 collective-permute-done.other
  84.7 0.0 collective-permute-done.1.other_low
  84.7 9.1 %first_half.1 = bf16[8,3,256,128]{3,2,1,0:T(8,128)(2,1)S(1)} custom-call(s32[2]{0:T(128)S(1)} %pad_add_fusion.place, bf16[8,2,3,64,256]{4,3,2,1,0:T(8,128)(2,1)} %bitcast.3.own, bf16[8,2,3,64,256]{4,3,2,1,0:T(8,128)(2,1)S(1)} %collective-permute-done.other, bf16[8,2,3,64,256]{4,3,2,1,0:T(8,128)(2,1)} %copy-done, ...), custom_call_target="tpu_custom_call" | custom-call | tf_op jit(solution)/shard_map/first_half/pallas_call | solution.py:104
  93.8 45.3 %all_to_all.21.t_ref = bf16[8,3,256,128]{3,2,1,0:T(8,128)(2,1)S(1)} all-to-all(bf16[8,3,256,128]{3,2,1,0:T(8,128)(2,1)S(1)} %first_half.1), channel_id=1, replica_groups=mesh['z'=8,'ylo'=2,'core'=2,'x'=4,'yhi'=2] {'z'}, dimensions={0} | all-to-all | bytes 3145728 | tf_op jit(solution)/shard_map/partial/all_to_all | solution.py:174
  139.1 8.6 %second_half.1 = bf16[8,2,3,64,256]{4,3,2,1,0:T(8,128)(2,1)S(1)} custom-call(bf16[8,3,256,128]{3,2,1,0:T(8,128)(2,1)S(1)} %all_to_all.21.t_ref, bf16[2048,2048]{1,0:T(8,128)(2,1)} %c_ref.3), custom_call_target="tpu_custom_call" | custom-call | tf_op jit(solution)/shard_map/second_half/pallas_call | solution.py:142
  147.8 25.1 %all_to_all.22 = bf16[16,3,64,256]{3,2,1,0:T(8,128)(2,1)S(1)} all-to-all(bf16[16,3,64,256]{3,2,1,0:T(8,128)(2,1)S(1)} %bitcast.6), channel_id=1, replica_groups=mesh['z'=8,'ylo'=2,'core'=2,'x'=4,'yhi'=2] {'x','yhi','ylo'}, dimensions={0} | all-to-all | bytes 3145728 | tf_op jit(solution)/shard_map/panels_out/all_to_all | solution.py:178
  172.9 1.1 copy.4
Async XLA Ops:
  28.4 46.6 %all-to-all-start.1 = ((bf16[8,2,3,64,256]{4,3,2,1,0:T(8,128)(2,1)}), bf16[8,2,3,64,256]{4,3,2,1,0:T(8,128)(2,1)S(1)}, u32[]{:S(2)}, u32[]{:S(2)}) async-start(bf16[8,2,3,64,256]{4,3,2,1,0:T(8,128)(2,1)} %bitcast.3.own), calls=%async_computation.1 | async-start | bytes 3145728 | tf_op jit(solution)/shard_map/mirror/all_to_all | solution.py:170
  36.8 47.9 %collective-permute-start = (bf16[8,2,3,64,256]{4,3,2,1,0:T(8,128)(2,1)}, bf16[8,2,3,64,256]{4,3,2,1,0:T(8,128)(2,1)S(1)}, u32[]{:S(2)}, u32[]{:S(2)}) collective-permute-start(bf16[8,2,3,64,256]{4,3,2,1,0:T(8,128)(2,1)} %bitcast.3.own), channel_id=1, source_target_pairs={{0,8},{8,0},{1,9},{9,1},{2,10},{10,2},{3,11},{11,3},{4,12},{12,4},... | collective-permute-start | bytes 4718600 | tf_op jit(solution)/shard_map/ppermute | solution.py:156
  75.0 9.7 %copy-start = (bf16[8,2,3,64,256]{4,3,2,1,0:T(8,128)(2,1)}, bf16[8,2,3,64,256]{4,3,2,1,0:T(8,128)(2,1)S(1)}, u32[]{:S(2)}) copy-start(bf16[8,2,3,64,256]{4,3,2,1,0:T(8,128)(2,1)S(1)} %all-to-all-done.1.own_low) | copy-start | bytes 4718596
  75.0 9.7 %collective-permute-start.1 = (bf16[8,2,3,64,256]{4,3,2,1,0:T(8,128)(2,1)S(1)}, bf16[8,2,3,64,256]{4,3,2,1,0:T(8,128)(2,1)}, u32[]{:S(2)}, u32[]{:S(2)}) collective-permute-start(bf16[8,2,3,64,256]{4,3,2,1,0:T(8,128)(2,1)S(1)} %all-to-all-done.1.own_low), channel_id=1, source_target_pairs={{0,8},{8,0},{1,9},{9,1},{2,10},{10,2},{3,11},{11,3},{4,12},{12,4},... | collective-permute-start | bytes 4718600 | tf_op jit(solution)/shard_map/ppermute | solution.py:156

commit v2 on v1

v2 whole, which is shorter than its diff:
```python
import jax
import jax.numpy as jnp
from jax import lax
from jax.experimental import pallas as pl
from jax.experimental.pallas import tpu as pltpu
from jax.sharding import Mesh, PartitionSpec as P

Z, YLO, CORE, X, YHI = 8, 2, 2, 4, 2
COLS = X * YHI
BLOCKS = 8
PLANE = ("x", "yhi", "ylo")
SIDE = ("x", "yhi")
F32 = jnp.float32
BF16 = jnp.bfloat16
PARAMS = pltpu.CompilerParams(vmem_limit_bytes=16 * 2**20)
SMALL = pltpu.CompilerParams(vmem_limit_bytes=4 * 2**20)


def transposed(block):
    size = block.shape[1]
    row = lax.broadcasted_iota(jnp.int32, (size, size), 0)
    column = lax.broadcasted_iota(jnp.int32, (size, size), 1)
    eye = (row == column).astype(F32).astype(BF16)
    return lax.dot_general(
        eye, block, (((1,), (1,)), ((), ())), preferred_element_type=F32
    ).astype(BF16)


def pick_kernel(core_ref, c_ref, out_ref):
    block = c_ref.shape[1] // BLOCKS
    lanes = block // CORE
    half = lanes // 2
    row = lax.broadcasted_iota(jnp.int32, (block, lanes), 0)
    column = lax.broadcasted_iota(jnp.int32, (block, lanes), 1)
    wanted = jnp.where(column < half, column, column + half) + core_ref[0] * half
    choose = (row == wanted).astype(F32).astype(BF16)
    for b in range(BLOCKS):
        out_ref[:, b * lanes:(b + 1) * lanes] = jnp.dot(
            c_ref[:, b * block:(b + 1) * block], choose, preferred_element_type=F32
        ).astype(BF16)


def pick_columns(core, orbitals):
    size = orbitals.shape[0]
    block = size // BLOCKS
    return pl.pallas_call(
        pick_kernel,
        out_shape=jax.ShapeDtypeStruct((size, size // CORE), BF16),
        grid_spec=pltpu.PrefetchScalarGridSpec(
            num_scalar_prefetch=1,
            grid=(BLOCKS,),
            in_specs=[pl.BlockSpec((block, size), lambda g, s: (g, 0))],
            out_specs=pl.BlockSpec((block, size // CORE), lambda g, s: (g, 0)),
        ),
        name="pick_columns",
    )(core, orbitals)


def accumulate(total, product):
    step = pl.program_id(0)

    @pl.when(step == 0)
    def _():
        total[...] = product

    @pl.when(step > 0)
    def _():
        total[...] += product


def first_kernel(place, direct, direct_other, turned, turned_other, c_ref, t_ref, sym, turn, total):
    per_step, _, depth, rows, block = direct.shape
    mine, core = place[0], place[1]
    step = pl.program_id(0)

    for u in range(per_step):
        b = step * per_step + u
        cols = slice(u * block, (u + 1) * block)

        @pl.when(b >= mine)
        def _():
            for k in range(depth):
                for y in range(YLO):
                    at = k * block + y * CORE * rows
                    sym[pl.ds(pl.multiple_of(at + core * rows, rows), rows), cols] = direct[u, y, k]
                    sym[pl.ds(pl.multiple_of(at + (1 - core) * rows, rows), rows), cols] = direct_other[u, y, k]

        @pl.when(b == mine)
        def _():
            row = lax.broadcasted_iota(jnp.int32, (block, block), 0)
            column = lax.broadcasted_iota(jnp.int32, (block, block), 1)
            for k in range(depth):
                upper = sym[k * block:(k + 1) * block, cols]
                sym[k * block:(k + 1) * block, cols] = jnp.where(row <= column, upper, transposed(upper))

        @pl.when(b < mine)
        def _():
            for k in range(depth):
                for y in range(YLO):
                    at = k * block + y * CORE * rows
                    turn[pl.ds(pl.multiple_of(at + core * rows, rows), rows), :] = turned[u, y, k]
                    turn[pl.ds(pl.multiple_of(at + (1 - core) * rows, rows), rows), :] = turned_other[u, y, k]
            for k in range(depth):
                sym[k * block:(k + 1) * block, cols] = transposed(turn[k * block:(k + 1) * block])

    accumulate(total, jnp.dot(sym[...], c_ref[...], preferred_element_type=F32))

    @pl.when(step == pl.num_programs(0) - 1)
    def _():
        lanes = t_ref.shape[3]
        for part in range(t_ref.shape[0]):
            for k in range(depth):
                t_ref[part, k] = total[k * block:(k + 1) * block, part * lanes:(part + 1) * lanes].astype(BF16)


def first_half(place, direct, direct_other, turned, turned_other, picked, name):
    _, _, depth, rows, block = direct.shape
    size, width = picked.shape
    per_step = 2
    piece = pl.BlockSpec((per_step, YLO, depth, rows, block), lambda g, s: (g, 0, 0, 0, 0))
    out = (BLOCKS, depth, block, width // BLOCKS)
    return pl.pallas_call(
        first_kernel,
        out_shape=jax.ShapeDtypeStruct(out, BF16),
        grid_spec=pltpu.PrefetchScalarGridSpec(
            num_scalar_prefetch=1,
            grid=(BLOCKS // per_step,),
            in_specs=[piece, piece, piece, piece,
                      pl.BlockSpec((per_step * block, width), lambda g, s: (g, 0))],
            out_specs=pl.BlockSpec(out, lambda g, s: (0, 0, 0, 0)),
            scratch_shapes=[pltpu.VMEM((depth * block, per_step * block), BF16),
                            pltpu.VMEM((depth * block, block), BF16),
                            pltpu.VMEM((depth * block, width), F32)],
        ),
        compiler_params=PARAMS,
        name=name,
    )(place, direct, direct_other, turned, turned_other, picked)


def second_kernel(t_ref, c_ref, out_ref, left, total):
    per_step, depth, block, lanes = t_ref.shape
    rows = lanes // YLO
    for u in range(per_step):
        for k in range(depth):
            left[k * lanes:(k + 1) * lanes, u * block:(u + 1) * block] = transposed(t_ref[u, k])
    accumulate(total, jnp.dot(left[...], c_ref[...], preferred_element_type=F32))

    @pl.when(pl.program_id(0) == pl.num_programs(0) - 1)
    def _():
        for c in range(COLS):
            for y in range(YLO):
                for k in range(depth):
                    at = k * lanes + y * rows
                    out_ref[c, y, k] = total[at:at + rows, c * block:(c + 1) * block].astype(BF16)


def second_half(partial_value, orbitals):
    _, depth, block, lanes = partial_value.shape
    size = orbitals.shape[0]
    rows = lanes // YLO
    per_step = 2
    out = (COLS, YLO, depth, rows, block)
    return pl.pallas_call(
        second_kernel,
        out_shape=jax.ShapeDtypeStruct(out, BF16),
        grid=(BLOCKS // per_step,),
        in_specs=[pl.BlockSpec((per_step, depth, block, lanes), lambda g: (g, 0, 0, 0)),
                  pl.BlockSpec((per_step * block, size), lambda g: (g, 0))],
        out_specs=pl.BlockSpec(out, lambda g: (0, 0, 0, 0, 0)),
        scratch_shapes=[pltpu.VMEM((depth * lanes, per_step * block), BF16),
                        pltpu.VMEM((depth * lanes, size), F32)],
        compiler_params=PARAMS,
        name="second_half",
    )(partial_value, orbitals)


def second_side_kernel(place, t_ref, other_ref, c_ref, keep, send, left, total, final):
    per_step, _, block, lanes = t_ref.shape
    rows = lanes // YLO
    ylo, core = place[0], place[1]
    for u in range(per_step):
        cols = slice(u * block, (u + 1) * block)
        own = transposed(t_ref[u, 0])
        other = transposed(other_ref[u, 0])
        for y in range(YLO):
            at = y * CORE * rows
            left[pl.ds(pl.multiple_of(at + core * rows, rows), rows), cols] = own[y * rows:(y + 1) * rows]
            left[pl.ds(pl.multiple_of(at + (1 - core) * rows, rows), rows), cols] = other[y * rows:(y + 1) * rows]
    accumulate(total, jnp.dot(left[...], c_ref[...], preferred_element_type=F32))

    @pl.when(pl.program_id(0) == pl.num_programs(0) - 1)
    def _():
        for part in range(total.shape[1] // block):
            cols = slice(part * block, (part + 1) * block)
            final[cols] = transposed(total[:, cols].astype(BF16))
        for z in range(Z):
            at = z * YLO * rows
            keep[z] = final[pl.ds(pl.multiple_of(at + ylo * rows, rows), rows)]
            send[z] = final[pl.ds(pl.multiple_of(at + (1 - ylo) * rows, rows), rows)]


def second_half_side(place, own, other, picked):
    _, _, block, lanes = own.shape
    size, width = picked.shape
    per_step = 2
    piece = pl.BlockSpec((per_step, 1, block, lanes), lambda g, s: (g, 0, 0, 0))
    out = jax.ShapeDtypeStruct((Z, lanes // YLO, block), BF16)
    whole = pl.BlockSpec(out.shape, lambda g, s: (0, 0, 0))
    return pl.pallas_call(
        second_side_kernel,
        out_shape=[out, out],
        grid_spec=pltpu.PrefetchScalarGridSpec(
            num_scalar_prefetch=1,
            grid=(BLOCKS // per_step,),
            in_specs=[piece, piece, pl.BlockSpec((per_step * block, width), lambda g, s: (g, 0))],
            out_specs=[whole, whole],
            scratch_shapes=[pltpu.VMEM((block, per_step * block), BF16),
                            pltpu.VMEM((block, width), F32),
                            pltpu.VMEM((width, block), BF16)],
        ),
        compiler_params=PARAMS,
        name="second_half_side",
    )(place, own, other, picked)


def spread_kernel(place, x_ref, *out_refs):
    for d in range(BLOCKS):
        out_refs[d][...] = x_ref[(place[0] + d) % BLOCKS]


def spread(mine, value):
    vmem = pl.BlockSpec(memory_space=pltpu.VMEM)
    return pl.pallas_call(
        spread_kernel,
        out_shape=[jax.ShapeDtypeStruct(value.shape[1:], BF16)] * BLOCKS,
        in_specs=[pl.BlockSpec(memory_space=pltpu.SMEM), vmem],
        out_specs=[vmem] * BLOCKS,
        compiler_params=SMALL,
        name="spread",
    )(mine, value)


def join_kernel(place, keep, got, *out_refs):
    z, ylo = place[0], place[1]
    for d in range(BLOCKS):
        out_refs[d][ylo] = keep[(z + d) % BLOCKS]
        out_refs[d][1 - ylo] = got[(z + d) % BLOCKS]


def join_and_spread(place, keep, got):
    vmem = pl.BlockSpec(memory_space=pltpu.VMEM)
    return pl.pallas_call(
        join_kernel,
        out_shape=[jax.ShapeDtypeStruct((YLO,) + keep.shape[1:], BF16)] * BLOCKS,
        in_specs=[pl.BlockSpec(memory_space=pltpu.SMEM), vmem, vmem],
        out_specs=[vmem] * BLOCKS,
        compiler_params=SMALL,
        name="join_and_spread",
    )(place, keep, got)


def collect_kernel(place, *refs):
    out_ref = refs[BLOCKS]
    for d in range(BLOCKS):
        out_ref[(place[0] + BLOCKS - d) % BLOCKS] = refs[d][...]


def collect(mine, parts):
    vmem = pl.BlockSpec(memory_space=pltpu.VMEM)
    return pl.pallas_call(
        collect_kernel,
        out_shape=jax.ShapeDtypeStruct((BLOCKS,) + parts[0].shape, BF16),
        in_specs=[pl.BlockSpec(memory_space=pltpu.SMEM)] + [vmem] * BLOCKS,
        out_specs=vmem,
        compiler_params=SMALL,
        name="collect",
    )(mine, *parts)


def collect_last_kernel(place, *refs):
    out_ref = refs[BLOCKS]
    for d in range(BLOCKS):
        for y in range(YLO):
            out_ref[y, (place[0] + BLOCKS - d) % BLOCKS] = refs[d][y]


def collect_last(mine, parts):
    vmem = pl.BlockSpec(memory_space=pltpu.VMEM)
    return pl.pallas_call(
        collect_last_kernel,
        out_shape=jax.ShapeDtypeStruct((YLO, BLOCKS) + parts[0].shape[1:], BF16),
        in_specs=[pl.BlockSpec(memory_space=pltpu.SMEM)] + [vmem] * BLOCKS,
        out_specs=vmem,
        compiler_params=SMALL,
        name="collect_last",
    )(mine, *parts)


def rotate(parts, axes):
    out = [parts[0]]
    for d in range(1, BLOCKS):
        out.append(lax.ppermute(parts[d], axes, [(i, (i + d) % BLOCKS) for i in range(BLOCKS)]))
    return out


def swap(value, axis):
    return lax.ppermute(value, axis, [(0, 1), (1, 0)])


def per_device(half_panel, orbitals):
    pairs, rows, block = half_panel.shape
    side_pairs = Z * YLO
    main_pairs = pairs - side_pairs
    depth = main_pairs // (COLS * YLO)
    z, ylo, core = lax.axis_index("z"), lax.axis_index("ylo"), lax.axis_index("core")
    c = lax.axis_index("x") * YHI + lax.axis_index("yhi")

    def scalars(*values):
        return jnp.stack(values).astype(jnp.int32)

    def deep(value):
        return value.reshape(BLOCKS, YLO, 1, rows, block)

    together = lax.optimization_barrier

    side = half_panel[main_pairs:].reshape(YLO, Z, rows, block)
    with jax.named_scope("panels_in"):
        own = half_panel[:main_pairs].reshape(COLS * YLO, depth, rows, block)
        own = lax.all_to_all(own, PLANE, 0, 0, tiled=True)
        own = own.reshape(COLS, YLO, depth, rows, block)
    with jax.named_scope("side_in"):
        got = swap(lax.dynamic_index_in_dim(side, 1 - ylo, 0, keepdims=False), "ylo")
        keep = lax.dynamic_index_in_dim(side, ylo, 0, keepdims=False)
        parts = rotate(join_and_spread(scalars(z, ylo), keep, got), "z")
        side_own = collect(scalars(z), parts)
    picked = pick_columns(scalars(core), orbitals)
    own, side_own, picked = together((own, side_own, picked))

    with jax.named_scope("mirror"):
        own_low = lax.all_to_all(own, "z", 0, 0, tiled=True)
    other = swap(own, "core")
    with jax.named_scope("side_mirror"):
        side_other = swap(side_own, "core")
        parts = rotate(spread(scalars(c), side_own), SIDE)
        side_low = collect(scalars(c), parts)
        side_other_low = swap(side_low, "core")
        side_partial = first_half(
            scalars(c, core), deep(side_low), deep(side_other_low), deep(side_own), deep(side_other),
            picked, "first_half_side"
        )
    own_low, other, side_partial = together((own_low, other, side_partial))

    other_low = swap(own_low, "core")
    partial_value = first_half(scalars(z, core), own, other, own_low, other_low, picked, "first_half")
    with jax.named_scope("partial"):
        partial_value = lax.all_to_all(partial_value, "z", 0, 0, tiled=True)
    with jax.named_scope("side_partial"):
        parts = rotate(spread(scalars(c), side_partial), SIDE)
        side_partial = collect(scalars(c), parts)
        side_partial_other = swap(side_partial, "core")
        keep, send = second_half_side(scalars(ylo, core), side_partial, side_partial_other, picked)
    partial_value, keep, send = together((partial_value, keep, send))

    got = swap(send, "ylo")
    result = second_half(partial_value, orbitals)
    with jax.named_scope("panels_out"):
        result = result.reshape(COLS * YLO, depth, rows, block)
        result = lax.all_to_all(result, PLANE, 0, 0, tiled=True)
        result = result.reshape(main_pairs, rows, block)
    with jax.named_scope("side_out"):
        parts = rotate(join_and_spread(scalars(z, ylo), keep, got), "z")
        side_result = collect_last(scalars(z), parts).reshape(side_pairs, rows, block)
    return jnp.concatenate([result, side_result], axis=0)


def solution(mesh):
    fine = Mesh(mesh.devices.reshape(Z, YLO, CORE, X, YHI), ("z", "ylo", "core", "x", "yhi"))
    spec = P(None, ("z", "ylo", "core"), ("x", "yhi"))
    return jax.shard_map(
        per_device, mesh=fine, in_specs=(spec, P()), out_specs=spec, check_vma=False
    )
```

time: 175 us -> 193 us (1.10)
  blocking collectives: 98.8 us -> 0 us
  starting transfers between devices: 8.49 us -> 89.4 us
  waiting for transfers between devices: 38.1 us -> 58.7 us
  local copies, waits for them, and re-layouts: 1.15 us -> 12.3 us
  Pallas kernels: 27.4 us -> 29.9 us
    all_to_all x3 -> x0, blocking collectives: 98.8 us -> none  [the longest x1 45.3 us: per_device(): partial_value = lax.all_to_all(partial_value, 'z', 0, 0, tiled=True)]
    ppermute x2 -> x35, starting transfers between devices: 0.02 us -> 63.5 us  [the longest x28 60 us: rotate(): lax.ppermute(parts[d], axes, [(i, (i + d) % BLOCKS) for i in range(BLOCKS)])]
    ppermute x2 -> x35, waiting for transfers between devices: 0.01 us -> 56.9 us  [the longest x7 40.5 us: swap(): return lax.ppermute(value, axis, [(0, 1), (1, 0)])]
    all_to_all x1, waiting for transfers between devices: 38.1 us -> 0.01 us  [per_device(): own_low = lax.all_to_all(own, 'z', 0, 0, tiled=True)]
    all_to_all x0 -> x3, starting transfers between devices: none -> 22.2 us  [the longest x1 8.04 us: per_device(): partial_value = lax.all_to_all(partial_value, 'z', 0, 0, tiled=True)]
    unnamed x3 -> x8, local copies, waits for them, and re-layouts: 1.15 us -> 9.95 us
    all_to_all x1, starting transfers between devices: 8.47 us -> 3.57 us  [per_device(): own_low = lax.all_to_all(own, 'z', 0, 0, tiled=True)]
    pallas_call x2 -> x12, Pallas kernels: 17.7 us -> 21 us  [the longest x2 10.4 us: first_half(): pl.pallas_call(first_kernel, out_shape=jax.ShapeDtypeStruct(out, BF16), g...]
  transfers between devices with their start and end apart: 3 -> 39, of which waited for: 1 -> 15; matrix products, arithmetic and copies ran while one was open for 0% -> 0% of each run, Pallas kernels for 6% -> 9%
where the time goes in v2:
time: 193 us; the launch traced here: 192 us
  starting transfers between devices  89.4 us (46%)
  waiting for transfers between devices  58.7 us (30%)
  Pallas kernels  29.9 us (15%)
  local copies, waits for them, and re-layouts  12.3 us (6%)
    ppermute x28, starting transfers between devices, rotate(): lax.ppermute(parts[d], axes, [(i, (i + d) % BLOCKS) for i in range(BLOCKS)])  60 us
    ppermute x7, waiting for transfers between devices, swap(): return lax.ppermute(value, axis, [(0, 1), (1, 0)])  40.5 us
    ppermute x28, waiting for transfers between devices, rotate(): lax.ppermute(parts[d], axes, [(i, (i + d) % BLOCKS) for i in range(BLOCKS)])  16.4 us
    pallas_call x2, Pallas kernels, first_half(): pl.pallas_call(first_kernel, out_shape=jax.ShapeDtypeStruct(out, BF16), g...  10.4 us
    unnamed x8, local copies, waits for them, and re-layouts  9.95 us
    pallas_call x1, Pallas kernels, pick_columns(): pl.pallas_call(pick_kernel, out_shape=jax.ShapeDtypeStruct((size, size //...  8.9 us
    all_to_all x1, starting transfers between devices, per_device(): partial_value = lax.all_to_all(partial_value, 'z', 0, 0, tiled=True)  8.04 us
    all_to_all x1, starting transfers between devices, per_device(): own = lax.all_to_all(own, PLANE, 0, 0, tiled=True)  7.61 us
  transfers between devices with their start and end apart: 39, of which 15 were waited for; matrix products, arithmetic and copies ran while one was open for 0% of the time, Pallas kernels for 9%

profile of v2, /device:TPU:2, one launch (start us, length us, event | category | flops | bytes accessed | tf_op | source)
XLA Modules:
  0.0 192.0 jit_solution(6069637014043380002)
XLA Ops:
  0.0 2.3 %slice.6 = bf16[32,64,256]{2,1,0:T(8,128)(2,1)} slice(bf16[48,64,256]{2,1,0:T(8,128)(2,1)} %param.2), slice={[0:32], [0:64], [0:256]} | slice | bytes 2097152 | tf_op jit(solution)/shard_map/panels_in/slice | solution.py:328
  2.3 7.6 %all-to-all-start = ((bf16[16,2,64,256]{3,2,1,0:T(8,128)(2,1)}), bf16[16,2,64,256]{3,2,1,0:T(8,128)(2,1)}, u32[]{:S(2)}, u32[]{:S(2)}) async-start(bf16[16,2,64,256]{3,2,1,0:T(8,128)(2,1)} %bitcast.2), calls=%async_computation | async-start | bytes 2097152 | tf_op jit(solution)/shard_map/panels_in/all_to_all | solution.py:329
  10.0 1.6 collective-permute-start
  11.6 17.0 %collective-permute-done.got = bf16[8,64,256]{2,1,0:T(8,128)(2,1)S(1)} collective-permute-done((bf16[8,64,256]{2,1,0:T(8,128)(2,1)S(1)}, bf16[8,64,256]{2,1,0:T(8,128)(2,1)S(1)}, u32[]{:S(2)}, u32[]{:S(2)}) %collective-permute-start) | collective-permute-done | bytes 262176 | tf_op jit(solution)/shard_map/side_in/ppermute | solution.py:307
  28.6 0.6 join_and_spread.2
  29.2 2.0 %collective-permute-start.1 = (bf16[2,64,256]{2,1,0:T(8,128)(2,1)S(1)}, bf16[2,64,256]{2,1,0:T(8,128)(2,1)S(1)}, u32[]{:S(2)}, u32[]{:S(2)}) collective-permute-start(bf16[2,64,256]{2,1,0:T(8,128)(2,1)S(1)} %get-tuple-element.49), channel_id=1, source_target_pairs={{0,32},{32,64},{64,96},{96,128},{128,160},{160,192},{192,224},{224... | collective-permute-start | bytes 196616 | tf_op jit(solution)/shard_map/side_in/ppermute | solution.py:302
  31.2 3.3 %collective-permute-start.2 = (bf16[2,64,256]{2,1,0:T(8,128)(2,1)S(1)}, bf16[2,64,256]{2,1,0:T(8,128)(2,1)S(1)}, u32[]{:S(2)}, u32[]{:S(2)}) collective-permute-start(bf16[2,64,256]{2,1,0:T(8,128)(2,1)S(1)} %get-tuple-element.50), channel_id=1, source_target_pairs={{0,64},{32,96},{64,128},{96,160},{128,192},{160,224},{192,0},{224,... | collective-permute-start | bytes 196616 | tf_op jit(solution)/shard_map/side_in/ppermute | solution.py:302
  34.4 4.0 %collective-permute-start.3 = (bf16[2,64,256]{2,1,0:T(8,128)(2,1)S(1)}, bf16[2,64,256]{2,1,0:T(8,128)(2,1)S(1)}, u32[]{:S(2)}, u32[]{:S(2)}) collective-permute-start(bf16[2,64,256]{2,1,0:T(8,128)(2,1)S(1)} %get-tuple-element.51), channel_id=1, source_target_pairs={{0,96},{32,128},{64,160},{96,192},{128,224},{160,0},{192,32},{224,... | collective-permute-start | bytes 196616 | tf_op jit(solution)/shard_map/side_in/ppermute | solution.py:302
  38.5 0.5 collective-permute-start.4
  39.0 4.9 %collective-permute-start.5 = (bf16[2,64,256]{2,1,0:T(8,128)(2,1)S(1)}, bf16[2,64,256]{2,1,0:T(8,128)(2,1)S(1)}, u32[]{:S(2)}, u32[]{:S(2)}) collective-permute-start(bf16[2,64,256]{2,1,0:T(8,128)(2,1)S(1)} %get-tuple-element.53), channel_id=1, source_target_pairs={{0,160},{32,192},{64,224},{96,0},{128,32},{160,64},{192,96},{224,1... | collective-permute-start | bytes 196616 | tf_op jit(solution)/shard_map/side_in/ppermute | solution.py:302
  44.0 2.7 %collective-permute-start.6 = (bf16[2,64,256]{2,1,0:T(8,128)(2,1)S(1)}, bf16[2,64,256]{2,1,0:T(8,128)(2,1)S(1)}, u32[]{:S(2)}, u32[]{:S(2)}) collective-permute-start(bf16[2,64,256]{2,1,0:T(8,128)(2,1)S(1)} %get-tuple-element.54), channel_id=1, source_target_pairs={{0,192},{32,224},{64,0},{96,32},{128,64},{160,96},{192,128},{224,1... | collective-permute-start | bytes 196616 | tf_op jit(solution)/shard_map/side_in/ppermute | solution.py:302
  46.6 1.0 collective-permute-start.7
  47.6 8.9 %pick_columns.1.c_ref = bf16[2048,1024]{1,0:T(8,128)(2,1)} custom-call(s32[1]{0:T(128)} %bitcast.1.core_ref, bf16[2048,2048]{1,0:T(8,128)(2,1)} %c_ref.3), custom_call_target="tpu_custom_call" | custom-call | tf_op jit(solution)/shard_map/pick_columns/pallas_call | solution.py:46
  56.7 3.6 %all-to-all-start.1 = ((bf16[8,2,2,64,256]{4,3,2,1,0:T(8,128)(2,1)}), bf16[8,2,2,64,256]{4,3,2,1,0:T(8,128)(2,1)S(1)}, u32[]{:S(2)}, u32[]{:S(2)}) async-start(bf16[8,2,2,64,256]{4,3,2,1,0:T(8,128)(2,1)} %bitcast.3.direct), calls=%async_computation.1 | async-start | bytes 2097152 | tf_op jit(solution)/shard_map/mirror/all_to_all | solution.py:340
  60.2 0.1 collective-permute-start.8
  60.4 2.8 %collective-permute-start.9 = (bf16[2,64,256]{2,1,0:T(8,128)(2,1)S(1)}, bf16[2,64,256]{2,1,0:T(8,128)(2,1)S(1)}, u32[]{:S(2)}, u32[]{:S(2)}) collective-permute-start(bf16[2,64,256]{2,1,0:T(8,128)(2,1)S(1)} %get-tuple-element.59), channel_id=1, source_target_pairs={{0,1},{1,2},{2,3},{3,4},{4,5},{5,6},{6,7},{7,0},{8,9},{9,10},{10,1... | collective-permute-start | bytes 196616 | tf_op jit(solution)/shard_map/side_mirror/ppermute | solution.py:302
  63.1 1.5 collective-permute-start.10
  64.6 1.5 collective-permute-start.11
  66.1 2.4 %collective-permute-start.12 = (bf16[2,64,256]{2,1,0:T(8,128)(2,1)S(1)}, bf16[2,64,256]{2,1,0:T(8,128)(2,1)S(1)}, u32[]{:S(2)}, u32[]{:S(2)}) collective-permute-start(bf16[2,64,256]{2,1,0:T(8,128)(2,1)S(1)} %get-tuple-element.62), channel_id=1, source_target_pairs={{0,4},{1,5},{2,6},{3,7},{4,0},{5,1},{6,2},{7,3},{8,12},{9,13},{10,... | collective-permute-start | bytes 196616 | tf_op jit(solution)/shard_map/side_mirror/ppermute | solution.py:302
  68.5 3.2 %collective-permute-start.13 = (bf16[2,64,256]{2,1,0:T(8,128)(2,1)S(1)}, bf16[2,64,256]{2,1,0:T(8,128)(2,1)S(1)}, u32[]{:S(2)}, u32[]{:S(2)}) collective-permute-start(bf16[2,64,256]{2,1,0:T(8,128)(2,1)S(1)} %get-tuple-element.63), channel_id=1, source_target_pairs={{0,5},{1,6},{2,7},{3,0},{4,1},{5,2},{6,3},{7,4},{8,13},{9,14},{10,... | collective-permute-start | bytes 196616 | tf_op jit(solution)/shard_map/side_mirror/ppermute | solution.py:302
  71.8 2.1 %collective-permute-start.14 = (bf16[2,64,256]{2,1,0:T(8,128)(2,1)S(1)}, bf16[2,64,256]{2,1,0:T(8,128)(2,1)S(1)}, u32[]{:S(2)}, u32[]{:S(2)}) collective-permute-start(bf16[2,64,256]{2,1,0:T(8,128)(2,1)S(1)} %get-tuple-element.64), channel_id=1, source_target_pairs={{0,6},{1,7},{2,0},{3,1},{4,2},{5,3},{6,4},{7,5},{8,14},{9,15},{10,... | collective-permute-start | bytes 196616 | tf_op jit(solution)/shard_map/side_mirror/ppermute | solution.py:302
  73.9 1.0 collective-permute-start.15
  74.9 1.3 collective-permute-done.13.refs_5_
  76.2 0.8 collective-permute-done.14.refs_6_
  76.9 2.7 %collective-permute-done.15.refs_7_ = bf16[2,64,256]{2,1,0:T(8,128)(2,1)S(1)} collective-permute-done((bf16[2,64,256]{2,1,0:T(8,128)(2,1)S(1)}, bf16[2,64,256]{2,1,0:T(8,128)(2,1)S(1)}, u32[]{:S(2)}, u32[]{:S(2)}) %collective-permute-start.15) | collective-permute-done | bytes 65568 | tf_op jit(solution)/shard_map/side_mirror/ppermute | solution.py:302
  79.7 0.1 collective-permute-start.16
  79.9 1.8 collective-permute-done.16
  81.7 2.2 %copy-done = bf16[2048,1024]{1,0:T(8,128)(2,1)S(1)} copy-done((bf16[2048,1024]{1,0:T(8,128)(2,1)S(1)}, bf16[2048,1024]{1,0:T(8,128)(2,1)}, u32[]{:S(2)}) %copy-start) | copy-done | bytes 4194328
  83.9 3.6 %first_half_side.1.x_ref = bf16[8,1,256,128]{3,2,1,0:T(8,128)(2,1)S(1)} custom-call(s32[2]{0:T(128)S(1)} %pad_add_fusion.1.place, bf16[8,2,1,64,256]{4,3,2,1,0:T(8,128)(2,1)S(1)} %bitcast.20, bf16[8,2,1,64,256]{4,3,2,1,0:T(8,128)(2,1)S(1)} %bitcast.22, bf16[8,2,1,64,256]{4,3,2,1,0:T(8,128)(2,1)S(1)} %bitcast.18, bf16[8,2,1,64,256]{4,3,2,1,0:T(8,128)(2,1)S(1)} %bitcast.21, ...), custom_call_target="tpu_custom_call" | custom-call | tf_op jit(solution)/shard_map/side_mirror/first_half_side/pallas_call | solution.py:122
  87.6 0.2 collective-permute-start.18
  87.9 2.4 %collective-permute-done.18.turned_other = bf16[8,2,2,64,256]{4,3,2,1,0:T(8,128)(2,1)S(1)} collective-permute-done((bf16[8,2,2,64,256]{4,3,2,1,0:T(8,128)(2,1)S(1)}, bf16[8,2,2,64,256]{4,3,2,1,0:T(8,128)(2,1)S(1)}, u32[]{:S(2)}, u32[]{:S(2)}) %collective-permute-start.18) | collective-permute-done | bytes 1048608 | tf_op jit(solution)/shard_map/ppermute | solution.py:307
  90.3 2.2 %copy-done.1 = bf16[2048,1024]{1,0:T(8,128)(2,1)S(1)} copy-done((bf16[2048,1024]{1,0:T(8,128)(2,1)S(1)}, bf16[2048,1024]{1,0:T(8,128)(2,1)}, u32[]{:S(2)}) %copy-start.1) | copy-done | bytes 4194328
  92.5 6.8 %first_half.1 = bf16[8,2,256,128]{3,2,1,0:T(8,128)(2,1)} custom-call(s32[2]{0:T(128)S(1)} %pad_add_fusion.3.place, bf16[8,2,2,64,256]{4,3,2,1,0:T(8,128)(2,1)} %bitcast.3.direct, bf16[8,2,2,64,256]{4,3,2,1,0:T(8,128)(2,1)S(1)} %collective-permute-done.8.direct_other, bf16[8,2,2,64,256]{4,3,2,1,0:T(8,128)(2,1)S(1)} %all-to-all-done.1.turned, ...), custom_call_target="tpu_custom_call" | custom-call | tf_op jit(solution)/shard_map/first_half/pallas_call | solution.py:122
  99.3 8.0 %all-to-all-start.2 = ((bf16[8,2,256,128]{3,2,1,0:T(8,128)(2,1)}), bf16[8,2,256,128]{3,2,1,0:T(8,128)(2,1)S(1)}, u32[]{:S(2)}, u32[]{:S(2)}) async-start(bf16[8,2,256,128]{3,2,1,0:T(8,128)(2,1)} %first_half.1), calls=%async_computation.2 | async-start | bytes 2097152 | tf_op jit(solution)/shard_map/partial/all_to_all | solution.py:356
  107.4 1.3 collective-permute-start.19
  108.7 1.5 collective-permute-start.20
  110.2 3.2 %collective-permute-start.21 = (bf16[1,256,128]{2,1,0:T(8,128)(2,1)S(1)}, bf16[1,256,128]{2,1,0:T(8,128)(2,1)S(1)}, u32[]{:S(2)}, u32[]{:S(2)}) collective-permute-start(bf16[1,256,128]{2,1,0:T(8,128)(2,1)S(1)} %get-tuple-element.73), channel_id=1, source_target_pairs={{0,3},{1,4},{2,5},{3,6},{4,7},{5,0},{6,1},{7,2},{8,11},{9,12},{10,... | collective-permute-start | bytes 196616 | tf_op jit(solution)/shard_map/side_partial/ppermute | solution.py:302
  113.4 1.7 collective-permute-start.22
  115.1 3.0 %collective-permute-start.23 = (bf16[1,256,128]{2,1,0:T(8,128)(2,1)S(1)}, bf16[1,256,128]{2,1,0:T(8,128)(2,1)S(1)}, u32[]{:S(2)}, u32[]{:S(2)}) collective-permute-start(bf16[1,256,128]{2,1,0:T(8,128)(2,1)S(1)} %get-tuple-element.75), channel_id=1, source_target_pairs={{0,5},{1,6},{2,7},{3,0},{4,1},{5,2},{6,3},{7,4},{8,13},{9,14},{10,... | collective-permute-start | bytes 196616 | tf_op jit(solution)/shard_map/side_partial/ppermute | solution.py:302
  118.1 2.6 %collective-permute-start.24 = (bf16[1,256,128]{2,1,0:T(8,128)(2,1)S(1)}, bf16[1,256,128]{2,1,0:T(8,128)(2,1)S(1)}, u32[]{:S(2)}, u32[]{:S(2)}) collective-permute-start(bf16[1,256,128]{2,1,0:T(8,128)(2,1)S(1)} %get-tuple-element.76), channel_id=1, source_target_pairs={{0,6},{1,7},{2,0},{3,1},{4,2},{5,3},{6,4},{7,5},{8,14},{9,15},{10,... | collective-permute-start | bytes 196616 | tf_op jit(solution)/shard_map/side_partial/ppermute | solution.py:302
  120.8 1.1 collective-permute-done.23.refs_5_
  121.9 1.4 collective-permute-done.24.refs_6_
  123.3 3.2 %collective-permute-done.25.refs_7_ = bf16[1,256,128]{2,1,0:T(8,128)(2,1)S(1)} collective-permute-done((bf16[1,256,128]{2,1,0:T(8,128)(2,1)S(1)}, bf16[1,256,128]{2,1,0:T(8,128)(2,1)S(1)}, u32[]{:S(2)}, u32[]{:S(2)}) %collective-permute-start.25) | collective-permute-done | bytes 65568 | tf_op jit(solution)/shard_map/side_partial/ppermute | solution.py:302
  126.6 0.1 collective-permute-start.26
  126.7 1.8 collective-permute-done.26.other_ref
  128.6 2.2 %copy-done.2 = bf16[2048,1024]{1,0:T(8,128)(2,1)S(1)} copy-done((bf16[2048,1024]{1,0:T(8,128)(2,1)S(1)}, bf16[2048,1024]{1,0:T(8,128)(2,1)}, u32[]{:S(2)}) %copy-start.2) | copy-done | bytes 4194328
  130.7 3.9 %second_half_side.1 = (bf16[8,64,256]{2,1,0:T(8,128)(2,1)S(1)}, bf16[8,64,256]{2,1,0:T(8,128)(2,1)S(1)}) custom-call(s32[2]{0:T(128)S(1)} %pad_add_fusion.2.place, bf16[8,1,256,128]{3,2,1,0:T(8,128)(2,1)S(1)} %collect.5.t_ref, bf16[8,1,256,128]{3,2,1,0:T(8,128)(2,1)S(1)} %collective-permute-done.26.other_ref, bf16[2048,1024]{1,0:T(8,128)(2,1)S(1)} %copy-done.2), custom_call_target="tpu_custom_call" | custom-call | tf_op jit(solution)/shard_map/side_partial/second_half_side/pallas_call | solution.py:209
  134.6 1.8 all-to-all-done.2.t_ref
  136.4 3.4 %copy-done.3 = bf16[2048,2048]{1,0:T(8,128)(2,1)S(1)} copy-done((bf16[2048,2048]{1,0:T(8,128)(2,1)S(1)}, bf16[2048,2048]{1,0:T(8,128)(2,1)}, u32[]{:S(2)}) %copy-start.3) | copy-done | bytes 8388632
  139.8 5.2 %second_half.1 = bf16[8,2,2,64,256]{4,3,2,1,0:T(8,128)(2,1)} custom-call(bf16[8,2,256,128]{3,2,1,0:T(8,128)(2,1)S(1)} %all-to-all-done.2.t_ref, bf16[2048,2048]{1,0:T(8,128)(2,1)S(1)} %copy-done.3), custom_call_target="tpu_custom_call" | custom-call | tf_op jit(solution)/shard_map/second_half/pallas_call | solution.py:163
  145.0 6.6 %all-to-all-start.3 = ((bf16[16,2,64,256]{3,2,1,0:T(8,128)(2,1)}), bf16[16,2,64,256]{3,2,1,0:T(8,128)(2,1)S(1)}, u32[]{:S(2)}, u32[]{:S(2)}) async-start(bf16[16,2,64,256]{3,2,1,0:T(8,128)(2,1)} %bitcast.13), calls=%async_computation.3 | async-start | bytes 2097152 | tf_op jit(solution)/shard_map/panels_out/all_to_all | solution.py:368
  151.6 1.5 collective-permute-start.27
  153.1 17.4 %collective-permute-done.27.got = bf16[8,64,256]{2,1,0:T(8,128)(2,1)S(1)} collective-permute-done((bf16[8,64,256]{2,1,0:T(8,128)(2,1)S(1)}, bf16[8,64,256]{2,1,0:T(8,128)(2,1)S(1)}, u32[]{:S(2)}, u32[]{:S(2)}) %collective-permute-start.27) | collective-permute-done | bytes 262176 | tf_op jit(solution)/shard_map/ppermute | solution.py:307
  170.5 0.6 join_and_spread.3
  171.2 0.9 collective-permute-start.29
  172.1 2.7 %collective-permute-start.30 = (bf16[2,64,256]{2,1,0:T(8,128)(2,1)S(1)}, bf16[2,64,256]{2,1,0:T(8,128)(2,1)S(1)}, u32[]{:S(2)}, u32[]{:S(2)}) collective-permute-start(bf16[2,64,256]{2,1,0:T(8,128)(2,1)S(1)} %get-tuple-element.86), channel_id=1, source_target_pairs={{0,96},{32,128},{64,160},{96,192},{128,224},{160,0},{192,32},{224,... | collective-permute-start | bytes 196616 | tf_op jit(solution)/shard_map/side_out/ppermute | solution.py:302
  174.7 2.9 %collective-permute-start.31 = (bf16[2,64,256]{2,1,0:T(8,128)(2,1)S(1)}, bf16[2,64,256]{2,1,0:T(8,128)(2,1)S(1)}, u32[]{:S(2)}, u32[]{:S(2)}) collective-permute-start(bf16[2,64,256]{2,1,0:T(8,128)(2,1)S(1)} %get-tuple-element.87), channel_id=1, source_target_pairs={{0,128},{32,160},{64,192},{96,224},{128,0},{160,32},{192,64},{224,... | collective-permute-start | bytes 196616 | tf_op jit(solution)/shard_map/side_out/ppermute | solution.py:302
  177.7 2.1 %collective-permute-start.32 = (bf16[2,64,256]{2,1,0:T(8,128)(2,1)S(1)}, bf16[2,64,256]{2,1,0:T(8,128)(2,1)S(1)}, u32[]{:S(2)}, u32[]{:S(2)}) collective-permute-start(bf16[2,64,256]{2,1,0:T(8,128)(2,1)S(1)} %get-tuple-element.88), channel_id=1, source_target_pairs={{0,160},{32,192},{64,224},{96,0},{128,32},{160,64},{192,96},{224,1... | collective-permute-start | bytes 196616 | tf_op jit(solution)/shard_map/side_out/ppermute | solution.py:302
  179.8 3.6 %collective-permute-start.33 = (bf16[2,64,256]{2,1,0:T(8,128)(2,1)S(1)}, bf16[2,64,256]{2,1,0:T(8,128)(2,1)S(1)}, u32[]{:S(2)}, u32[]{:S(2)}) collective-permute-start(bf16[2,64,256]{2,1,0:T(8,128)(2,1)S(1)} %get-tuple-element.89), channel_id=1, source_target_pairs={{0,192},{32,224},{64,0},{96,32},{128,64},{160,96},{192,128},{224,1... | collective-permute-start | bytes 196616 | tf_op jit(solution)/shard_map/side_out/ppermute | solution.py:302
  183.4 1.5 collective-permute-start.34
  184.8 1.6 collective-permute-done.32.refs_5_
  186.4 3.4 %collective-permute-done.33.refs_6_ = bf16[2,64,256]{2,1,0:T(8,128)(2,1)S(1)} collective-permute-done((bf16[2,64,256]{2,1,0:T(8,128)(2,1)S(1)}, bf16[2,64,256]{2,1,0:T(8,128)(2,1)S(1)}, u32[]{:S(2)}, u32[]{:S(2)}) %collective-permute-start.33) | collective-permute-done | bytes 65568 | tf_op jit(solution)/shard_map/side_out/ppermute | solution.py:302
  189.8 0.8 collective-permute-done.34.refs_7_
  190.7 1.3 pad_maximum_fusion
  (44 shorter events, 0.8 us)
Async XLA Ops:
  2.3 7.6 %slice-start = ((bf16[48,64,256]{2,1,0:T(8,128)(2,1)}), bf16[16,64,256]{2,1,0:T(8,128)(2,1)S(1)}, s32[]{:S(2)}) async-start(bf16[48,64,256]{2,1,0:T(8,128)(2,1)} %param.2), calls=%async_computation.4 | async-start | bytes 1048576 | tf_op jit(solution)/shard_map/slice | solution.py:326
  2.3 54.3 %all-to-all-start = ((bf16[16,2,64,256]{3,2,1,0:T(8,128)(2,1)}), bf16[16,2,64,256]{3,2,1,0:T(8,128)(2,1)}, u32[]{:S(2)}, u32[]{:S(2)}) async-start(bf16[16,2,64,256]{3,2,1,0:T(8,128)(2,1)} %bitcast.2), calls=%async_computation | async-start | bytes 2097152 | tf_op jit(solution)/shard_map/panels_in/all_to_all | solution.py:329
  10.0 18.6 %collective-permute-start = (bf16[8,64,256]{2,1,0:T(8,128)(2,1)S(1)}, bf16[8,64,256]{2,1,0:T(8,128)(2,1)S(1)}, u32[]{:S(2)}, u32[]{:S(2)}) collective-permute-start(bf16[8,64,256]{2,1,0:T(8,128)(2,1)S(1)} %get-tuple-element.91), channel_id=1, source_target_pairs={{0,16},{16,0},{1,17},{17,1},{2,18},{18,2},{3,19},{19,3},{4,20},{20... | collective-permute-start | bytes 786440 | tf_op jit(solution)/shard_map/side_in/ppermute | solution.py:307
  29.2 14.8 %collective-permute-start.1 = (bf16[2,64,256]{2,1,0:T(8,128)(2,1)S(1)}, bf16[2,64,256]{2,1,0:T(8,128)(2,1)S(1)}, u32[]{:S(2)}, u32[]{:S(2)}) collective-permute-start(bf16[2,64,256]{2,1,0:T(8,128)(2,1)S(1)} %get-tuple-element.49), channel_id=1, source_target_pairs={{0,32},{32,64},{64,96},{96,128},{128,160},{160,192},{192,224},{224... | collective-permute-start | bytes 196616 | tf_op jit(solution)/shard_map/side_in/ppermute | solution.py:302
  31.2 15.5 %collective-permute-start.2 = (bf16[2,64,256]{2,1,0:T(8,128)(2,1)S(1)}, bf16[2,64,256]{2,1,0:T(8,128)(2,1)S(1)}, u32[]{:S(2)}, u32[]{:S(2)}) collective-permute-start(bf16[2,64,256]{2,1,0:T(8,128)(2,1)S(1)} %get-tuple-element.50), channel_id=1, source_target_pairs={{0,64},{32,96},{64,128},{96,160},{128,192},{160,224},{192,0},{224,... | collective-permute-start | bytes 196616 | tf_op jit(solution)/shard_map/side_in/ppermute | solution.py:302
  34.4 22.1 %collective-permute-start.3 = (bf16[2,64,256]{2,1,0:T(8,128)(2,1)S(1)}, bf16[2,64,256]{2,1,0:T(8,128)(2,1)S(1)}, u32[]{:S(2)}, u32[]{:S(2)}) collective-permute-start(bf16[2,64,256]{2,1,0:T(8,128)(2,1)S(1)} %get-tuple-element.51), channel_id=1, source_target_pairs={{0,96},{32,128},{64,160},{96,192},{128,224},{160,0},{192,32},{224,... | collective-permute-start | bytes 196616 | tf_op jit(solution)/shard_map/side_in/ppermute | solution.py:302
  38.5 18.1 %collective-permute-start.4 = (bf16[2,64,256]{2,1,0:T(8,128)(2,1)S(1)}, bf16[2,64,256]{2,1,0:T(8,128)(2,1)S(1)}, u32[]{:S(2)}, u32[]{:S(2)}) collective-permute-start(bf16[2,64,256]{2,1,0:T(8,128)(2,1)S(1)} %get-tuple-element.52), channel_id=1, source_target_pairs={{0,128},{32,160},{64,192},{96,224},{128,0},{160,32},{192,64},{224,... | collective-permute-start | bytes 196616 | tf_op jit(solution)/shard_map/side_in/ppermute | solution.py:302
  39.0 17.5 %collective-permute-start.5 = (bf16[2,64,256]{2,1,0:T(8,128)(2,1)S(1)}, bf16[2,64,256]{2,1,0:T(8,128)(2,1)S(1)}, u32[]{:S(2)}, u32[]{:S(2)}) collective-permute-start(bf16[2,64,256]{2,1,0:T(8,128)(2,1)S(1)} %get-tuple-element.53), channel_id=1, source_target_pairs={{0,160},{32,192},{64,224},{96,0},{128,32},{160,64},{192,96},{224,1... | collective-permute-start | bytes 196616 | tf_op jit(solution)/shard_map/side_in/ppermute | solution.py:302
  44.0 12.6 %collective-permute-start.6 = (bf16[2,64,256]{2,1,0:T(8,128)(2,1)S(1)}, bf16[2,64,256]{2,1,0:T(8,128)(2,1)S(1)}, u32[]{:S(2)}, u32[]{:S(2)}) collective-permute-start(bf16[2,64,256]{2,1,0:T(8,128)(2,1)S(1)} %get-tuple-element.54), channel_id=1, source_target_pairs={{0,192},{32,224},{64,0},{96,32},{128,64},{160,96},{192,128},{224,1... | collective-permute-start | bytes 196616 | tf_op jit(solution)/shard_map/side_in/ppermute | solution.py:302
  46.6 9.9 %collective-permute-start.7 = (bf16[2,64,256]{2,1,0:T(8,128)(2,1)S(1)}, bf16[2,64,256]{2,1,0:T(8,128)(2,1)S(1)}, u32[]{:S(2)}, u32[]{:S(2)}) collective-permute-start(bf16[2,64,256]{2,1,0:T(8,128)(2,1)S(1)} %get-tuple-element.55), channel_id=1, source_target_pairs={{0,224},{32,0},{64,32},{96,64},{128,96},{160,128},{192,160},{224,1... | collective-permute-start | bytes 196616 | tf_op jit(solution)/shard_map/side_in/ppermute | solution.py:302
  56.7 30.9 %all-to-all-start.1 = ((bf16[8,2,2,64,256]{4,3,2,1,0:T(8,128)(2,1)}), bf16[8,2,2,64,256]{4,3,2,1,0:T(8,128)(2,1)S(1)}, u32[]{:S(2)}, u32[]{:S(2)}) async-start(bf16[8,2,2,64,256]{4,3,2,1,0:T(8,128)(2,1)} %bitcast.3.direct), calls=%async_computation.1 | async-start | bytes 2097152 | tf_op jit(solution)/shard_map/mirror/all_to_all | solution.py:340
  60.2 27.3 %collective-permute-start.8 = (bf16[8,2,2,64,256]{4,3,2,1,0:T(8,128)(2,1)}, bf16[8,2,2,64,256]{4,3,2,1,0:T(8,128)(2,1)S(1)}, u32[]{:S(2)}, u32[]{:S(2)}) collective-permute-start(bf16[8,2,2,64,256]{4,3,2,1,0:T(8,128)(2,1)} %bitcast.3.direct), channel_id=1, source_target_pairs={{0,8},{8,0},{1,9},{9,1},{2,10},{10,2},{3,11},{11,3},{4,12},{12,4},... | collective-permute-start | bytes 3145736 | tf_op jit(solution)/shard_map/ppermute | solution.py:307
  60.4 8.1 %collective-permute-start.9 = (bf16[2,64,256]{2,1,0:T(8,128)(2,1)S(1)}, bf16[2,64,256]{2,1,0:T(8,128)(2,1)S(1)}, u32[]{:S(2)}, u32[]{:S(2)}) collective-permute-start(bf16[2,64,256]{2,1,0:T(8,128)(2,1)S(1)} %get-tuple-element.59), channel_id=1, source_target_pairs={{0,1},{1,2},{2,3},{3,4},{4,5},{5,6},{6,7},{7,0},{8,9},{9,10},{10,1... | collective-permute-start | bytes 196616 | tf_op jit(solution)/shard_map/side_mirror/ppermute | solution.py:302
  63.1 8.6 %collective-permute-start.10 = (bf16[2,64,256]{2,1,0:T(8,128)(2,1)S(1)}, bf16[2,64,256]{2,1,0:T(8,128)(2,1)S(1)}, u32[]{:S(2)}, u32[]{:S(2)}) collective-permute-start(bf16[2,64,256]{2,1,0:T(8,128)(2,1)S(1)} %get-tuple-element.60), channel_id=1, source_target_pairs={{0,2},{1,3},{2,4},{3,5},{4,6},{5,7},{6,0},{7,1},{8,10},{9,11},{10,... | collective-permute-start | bytes 196616 | tf_op jit(solution)/shard_map/side_mirror/ppermute | solution.py:302
  64.6 9.3 %collective-permute-start.11 = (bf16[2,64,256]{2,1,0:T(8,128)(2,1)S(1)}, bf16[2,64,256]{2,1,0:T(8,128)(2,1)S(1)}, u32[]{:S(2)}, u32[]{:S(2)}) collective-permute-start(bf16[2,64,256]{2,1,0:T(8,128)(2,1)S(1)} %get-tuple-element.61), channel_id=1, source_target_pairs={{0,3},{1,4},{2,5},{3,6},{4,7},{5,0},{6,1},{7,2},{8,11},{9,12},{10,... | collective-permute-start | bytes 196616 | tf_op jit(solution)/shard_map/side_mirror/ppermute | solution.py:302
  66.1 8.8 %collective-permute-start.12 = (bf16[2,64,256]{2,1,0:T(8,128)(2,1)S(1)}, bf16[2,64,256]{2,1,0:T(8,128)(2,1)S(1)}, u32[]{:S(2)}, u32[]{:S(2)}) collective-permute-start(bf16[2,64,256]{2,1,0:T(8,128)(2,1)S(1)} %get-tuple-element.62), channel_id=1, source_target_pairs={{0,4},{1,5},{2,6},{3,7},{4,0},{5,1},{6,2},{7,3},{8,12},{9,13},{10,... | collective-permute-start | bytes 196616 | tf_op jit(solution)/shard_map/side_mirror/ppermute | solution.py:302
  68.5 7.6 %collective-permute-start.13 = (bf16[2,64,256]{2,1,0:T(8,128)(2,1)S(1)}, bf16[2,64,256]{2,1,0:T(8,128)(2,1)S(1)}, u32[]{:S(2)}, u32[]{:S(2)}) collective-permute-start(bf16[2,64,256]{2,1,0:T(8,128)(2,1)S(1)} %get-tuple-element.63), channel_id=1, source_target_pairs={{0,5},{1,6},{2,7},{3,0},{4,1},{5,2},{6,3},{7,4},{8,13},{9,14},{10,... | collective-permute-start | bytes 196616 | tf_op jit(solution)/shard_map/side_mirror/ppermute | solution.py:302
  71.8 5.2 %collective-permute-start.14 = (bf16[2,64,256]{2,1,0:T(8,128)(2,1)S(1)}, bf16[2,64,256]{2,1,0:T(8,128)(2,1)S(1)}, u32[]{:S(2)}, u32[]{:S(2)}) collective-permute-start(bf16[2,64,256]{2,1,0:T(8,128)(2,1)S(1)} %get-tuple-element.64), channel_id=1, source_target_pairs={{0,6},{1,7},{2,0},{3,1},{4,2},{5,3},{6,4},{7,5},{8,14},{9,15},{10,... | collective-permute-start | bytes 196616 | tf_op jit(solution)/shard_map/side_mirror/ppermute | solution.py:302
  73.9 5.8 %collective-permute-start.15 = (bf16[2,64,256]{2,1,0:T(8,128)(2,1)S(1)}, bf16[2,64,256]{2,1,0:T(8,128)(2,1)S(1)}, u32[]{:S(2)}, u32[]{:S(2)}) collective-permute-start(bf16[2,64,256]{2,1,0:T(8,128)(2,1)S(1)} %get-tuple-element.65), channel_id=1, source_target_pairs={{0,7},{1,0},{2,1},{3,2},{4,3},{5,4},{6,5},{7,6},{8,15},{9,8},{10,9... | collective-permute-start | bytes 196616 | tf_op jit(solution)/shard_map/side_mirror/ppermute | solution.py:302
  74.9 5.1 %collective-permute-start.17 = (bf16[8,2,64,256]{3,2,1,0:T(8,128)(2,1)S(1)}, bf16[8,2,64,256]{3,2,1,0:T(8,128)(2,1)S(1)}, u32[]{:S(2)}, u32[]{:S(2)}) collective-permute-start(bf16[8,2,64,256]{3,2,1,0:T(8,128)(2,1)S(1)} %collect.3.x_ref), channel_id=1, source_target_pairs={{0,8},{8,0},{1,9},{9,1},{2,10},{10,2},{3,11},{11,3},{4,12},{12,4},... | collective-permute-start | bytes 1572872 | tf_op jit(solution)/shard_map/side_mirror/ppermute | solution.py:307
  79.7 2.0 %collective-permute-start.16 = (bf16[8,2,64,256]{3,2,1,0:T(8,128)(2,1)S(1)}, bf16[8,2,64,256]{3,2,1,0:T(8,128)(2,1)S(1)}, u32[]{:S(2)}, u32[]{:S(2)}) collective-permute-start(bf16[8,2,64,256]{3,2,1,0:T(8,128)(2,1)S(1)} %collect.4), channel_id=1, source_target_pairs={{0,8},{8,0},{1,9},{9,1},{2,10},{10,2},{3,11},{11,3},{4,12},{12,4},... | collective-permute-start | bytes 1572872 | tf_op jit(solution)/shard_map/side_mirror/ppermute | solution.py:307
  81.7 2.2 %copy-start = (bf16[2048,1024]{1,0:T(8,128)(2,1)S(1)}, bf16[2048,1024]{1,0:T(8,128)(2,1)}, u32[]{:S(2)}) copy-start(bf16[2048,1024]{1,0:T(8,128)(2,1)} %pick_columns.1.c_ref) | copy-start | bytes 12582916
  87.6 2.7 %collective-permute-start.18 = (bf16[8,2,2,64,256]{4,3,2,1,0:T(8,128)(2,1)S(1)}, bf16[8,2,2,64,256]{4,3,2,1,0:T(8,128)(2,1)S(1)}, u32[]{:S(2)}, u32[]{:S(2)}) collective-permute-start(bf16[8,2,2,64,256]{4,3,2,1,0:T(8,128)(2,1)S(1)} %all-to-all-done.1.turned), channel_id=1, source_target_pairs={{0,8},{8,0},{1,9},{9,1},{2,10},{10,2},{3,11},{11,3},{4,12},{12,4},... | collective-permute-start | bytes 3145736 | tf_op jit(solution)/shard_map/ppermute | solution.py:307
  90.3 2.2 %copy-start.1 = (bf16[2048,1024]{1,0:T(8,128)(2,1)S(1)}, bf16[2048,1024]{1,0:T(8,128)(2,1)}, u32[]{:S(2)}) copy-start(bf16[2048,1024]{1,0:T(8,128)(2,1)} %pick_columns.1.c_ref) | copy-start | bytes 12582916
  99.3 37.1 %all-to-all-start.2 = ((bf16[8,2,256,128]{3,2,1,0:T(8,128)(2,1)}), bf16[8,2,256,128]{3,2,1,0:T(8,128)(2,1)S(1)}, u32[]{:S(2)}, u32[]{:S(2)}) async-start(bf16[8,2,256,128]{3,2,1,0:T(8,128)(2,1)} %first_half.1), calls=%async_computation.2 | async-start | bytes 2097152 | tf_op jit(solution)/shard_map/partial/all_to_all | solution.py:356
  107.4 10.8 %collective-permute-start.19 = (bf16[1,256,128]{2,1,0:T(8,128)(2,1)S(1)}, bf16[1,256,128]{2,1,0:T(8,128)(2,1)S(1)}, u32[]{:S(2)}, u32[]{:S(2)}) collective-permute-start(bf16[1,256,128]{2,1,0:T(8,128)(2,1)S(1)} %get-tuple-element.71), channel_id=1, source_target_pairs={{0,1},{1,2},{2,3},{3,4},{4,5},{5,6},{6,7},{7,0},{8,9},{9,10},{10,1... | collective-permute-start | bytes 196616 | tf_op jit(solution)/shard_map/side_partial/ppermute | solution.py:302
  108.7 12.1 %collective-permute-start.20 = (bf16[1,256,128]{2,1,0:T(8,128)(2,1)S(1)}, bf16[1,256,128]{2,1,0:T(8,128)(2,1)S(1)}, u32[]{:S(2)}, u32[]{:S(2)}) collective-permute-start(bf16[1,256,128]{2,1,0:T(8,128)(2,1)S(1)} %get-tuple-element.72), channel_id=1, source_target_pairs={{0,2},{1,3},{2,4},{3,5},{4,6},{5,7},{6,0},{7,1},{8,10},{9,11},{10,... | collective-permute-start | bytes 196616 | tf_op jit(solution)/shard_map/side_partial/ppermute | solution.py:302
  110.2 10.6 %collective-permute-start.21 = (bf16[1,256,128]{2,1,0:T(8,128)(2,1)S(1)}, bf16[1,256,128]{2,1,0:T(8,128)(2,1)S(1)}, u32[]{:S(2)}, u32[]{:S(2)}) collective-permute-start(bf16[1,256,128]{2,1,0:T(8,128)(2,1)S(1)} %get-tuple-element.73), channel_id=1, source_target_pairs={{0,3},{1,4},{2,5},{3,6},{4,7},{5,0},{6,1},{7,2},{8,11},{9,12},{10,... | collective-permute-start | bytes 196616 | tf_op jit(solution)/shard_map/side_partial/ppermute | solution.py:302
  113.4 7.4 %collective-permute-start.22 = (bf16[1,256,128]{2,1,0:T(8,128)(2,1)S(1)}, bf16[1,256,128]{2,1,0:T(8,128)(2,1)S(1)}, u32[]{:S(2)}, u32[]{:S(2)}) collective-permute-start(bf16[1,256,128]{2,1,0:T(8,128)(2,1)S(1)} %get-tuple-element.74), channel_id=1, source_target_pairs={{0,4},{1,5},{2,6},{3,7},{4,0},{5,1},{6,2},{7,3},{8,12},{9,13},{10,... | collective-permute-start | bytes 196616 | tf_op jit(solution)/shard_map/side_partial/ppermute | solution.py:302
  115.1 6.8 %collective-permute-start.23 = (bf16[1,256,128]{2,1,0:T(8,128)(2,1)S(1)}, bf16[1,256,128]{2,1,0:T(8,128)(2,1)S(1)}, u32[]{:S(2)}, u32[]{:S(2)}) collective-permute-start(bf16[1,256,128]{2,1,0:T(8,128)(2,1)S(1)} %get-tuple-element.75), channel_id=1, source_target_pairs={{0,5},{1,6},{2,7},{3,0},{4,1},{5,2},{6,3},{7,4},{8,13},{9,14},{10,... | collective-permute-start | bytes 196616 | tf_op jit(solution)/shard_map/side_partial/ppermute | solution.py:302
  118.1 5.2 %collective-permute-start.24 = (bf16[1,256,128]{2,1,0:T(8,128)(2,1)S(1)}, bf16[1,256,128]{2,1,0:T(8,128)(2,1)S(1)}, u32[]{:S(2)}, u32[]{:S(2)}) collective-permute-start(bf16[1,256,128]{2,1,0:T(8,128)(2,1)S(1)} %get-tuple-element.76), channel_id=1, source_target_pairs={{0,6},{1,7},{2,0},{3,1},{4,2},{5,3},{6,4},{7,5},{8,14},{9,15},{10,... | collective-permute-start | bytes 196616 | tf_op jit(solution)/shard_map/side_partial/ppermute | solution.py:302
  120.7 5.8 %collective-permute-start.25 = (bf16[1,256,128]{2,1,0:T(8,128)(2,1)S(1)}, bf16[1,256,128]{2,1,0:T(8,128)(2,1)S(1)}, u32[]{:S(2)}, u32[]{:S(2)}) collective-permute-start(bf16[1,256,128]{2,1,0:T(8,128)(2,1)S(1)} %get-tuple-element.77), channel_id=1, source_target_pairs={{0,7},{1,0},{2,1},{3,2},{4,3},{5,4},{6,5},{7,6},{8,15},{9,8},{10,9... | collective-permute-start | bytes 196616 | tf_op jit(solution)/shard_map/side_partial/ppermute | solution.py:302
  126.6 2.0 %collective-permute-start.26 = (bf16[8,1,256,128]{3,2,1,0:T(8,128)(2,1)S(1)}, bf16[8,1,256,128]{3,2,1,0:T(8,128)(2,1)S(1)}, u32[]{:S(2)}, u32[]{:S(2)}) collective-permute-start(bf16[8,1,256,128]{3,2,1,0:T(8,128)(2,1)S(1)} %collect.5.t_ref), channel_id=1, source_target_pairs={{0,8},{8,0},{1,9},{9,1},{2,10},{10,2},{3,11},{11,3},{4,12},{12,4},... | collective-permute-start | bytes 1572872 | tf_op jit(solution)/shard_map/side_partial/ppermute | solution.py:307
  128.6 2.2 %copy-start.2 = (bf16[2048,1024]{1,0:T(8,128)(2,1)S(1)}, bf16[2048,1024]{1,0:T(8,128)(2,1)}, u32[]{:S(2)}) copy-start(bf16[2048,1024]{1,0:T(8,128)(2,1)} %pick_columns.1.c_ref) | copy-start | bytes 12582916
  136.4 3.4 %copy-start.3 = (bf16[2048,2048]{1,0:T(8,128)(2,1)S(1)}, bf16[2048,2048]{1,0:T(8,128)(2,1)}, u32[]{:S(2)}) copy-start(bf16[2048,2048]{1,0:T(8,128)(2,1)} %c_ref.3) | copy-start | bytes 25165828
  145.0 45.7 %all-to-all-start.3 = ((bf16[16,2,64,256]{3,2,1,0:T(8,128)(2,1)}), bf16[16,2,64,256]{3,2,1,0:T(8,128)(2,1)S(1)}, u32[]{:S(2)}, u32[]{:S(2)}) async-start(bf16[16,2,64,256]{3,2,1,0:T(8,128)(2,1)} %bitcast.13), calls=%async_computation.3 | async-start | bytes 2097152 | tf_op jit(solution)/shard_map/panels_out/all_to_all | solution.py:368
  151.6 18.9 %collective-permute-start.27 = (bf16[8,64,256]{2,1,0:T(8,128)(2,1)S(1)}, bf16[8,64,256]{2,1,0:T(8,128)(2,1)S(1)}, u32[]{:S(2)}, u32[]{:S(2)}) collective-permute-start(bf16[8,64,256]{2,1,0:T(8,128)(2,1)S(1)} %get-tuple-element.82), channel_id=1, source_target_pairs={{0,16},{16,0},{1,17},{17,1},{2,18},{18,2},{3,19},{19,3},{4,20},{20... | collective-permute-start | bytes 786440 | tf_op jit(solution)/shard_map/ppermute | solution.py:307
  171.1 8.7 %collective-permute-start.28 = (bf16[2,64,256]{2,1,0:T(8,128)(2,1)S(1)}, bf16[2,64,256]{2,1,0:T(8,128)(2,1)S(1)}, u32[]{:S(2)}, u32[]{:S(2)}) collective-permute-start(bf16[2,64,256]{2,1,0:T(8,128)(2,1)S(1)} %get-tuple-element.84), channel_id=1, source_target_pairs={{0,32},{32,64},{64,96},{96,128},{128,160},{160,192},{192,224},{224... | collective-permute-start | bytes 196616 | tf_op jit(solution)/shard_map/side_out/ppermute | solution.py:302
  171.2 12.2 %collective-permute-start.29 = (bf16[2,64,256]{2,1,0:T(8,128)(2,1)S(1)}, bf16[2,64,256]{2,1,0:T(8,128)(2,1)S(1)}, u32[]{:S(2)}, u32[]{:S(2)}) collective-permute-start(bf16[2,64,256]{2,1,0:T(8,128)(2,1)S(1)} %get-tuple-element.85), channel_id=1, source_target_pairs={{0,64},{32,96},{64,128},{96,160},{128,192},{160,224},{192,0},{224,... | collective-permute-start | bytes 196616 | tf_op jit(solution)/shard_map/side_out/ppermute | solution.py:302
  172.1 12.7 %collective-permute-start.30 = (bf16[2,64,256]{2,1,0:T(8,128)(2,1)S(1)}, bf16[2,64,256]{2,1,0:T(8,128)(2,1)S(1)}, u32[]{:S(2)}, u32[]{:S(2)}) collective-permute-start(bf16[2,64,256]{2,1,0:T(8,128)(2,1)S(1)} %get-tuple-element.86), channel_id=1, source_target_pairs={{0,96},{32,128},{64,160},{96,192},{128,224},{160,0},{192,32},{224,... | collective-permute-start | bytes 196616 | tf_op jit(solution)/shard_map/side_out/ppermute | solution.py:302
  174.7 10.1 %collective-permute-start.31 = (bf16[2,64,256]{2,1,0:T(8,128)(2,1)S(1)}, bf16[2,64,256]{2,1,0:T(8,128)(2,1)S(1)}, u32[]{:S(2)}, u32[]{:S(2)}) collective-permute-start(bf16[2,64,256]{2,1,0:T(8,128)(2,1)S(1)} %get-tuple-element.87), channel_id=1, source_target_pairs={{0,128},{32,160},{64,192},{96,224},{128,0},{160,32},{192,64},{224,... | collective-permute-start | bytes 196616 | tf_op jit(solution)/shard_map/side_out/ppermute | solution.py:302
  177.7 8.7 %collective-permute-start.32 = (bf16[2,64,256]{2,1,0:T(8,128)(2,1)S(1)}, bf16[2,64,256]{2,1,0:T(8,128)(2,1)S(1)}, u32[]{:S(2)}, u32[]{:S(2)}) collective-permute-start(bf16[2,64,256]{2,1,0:T(8,128)(2,1)S(1)} %get-tuple-element.88), channel_id=1, source_target_pairs={{0,160},{32,192},{64,224},{96,0},{128,32},{160,64},{192,96},{224,1... | collective-permute-start | bytes 196616 | tf_op jit(solution)/shard_map/side_out/ppermute | solution.py:302
  179.8 10.1 %collective-permute-start.33 = (bf16[2,64,256]{2,1,0:T(8,128)(2,1)S(1)}, bf16[2,64,256]{2,1,0:T(8,128)(2,1)S(1)}, u32[]{:S(2)}, u32[]{:S(2)}) collective-permute-start(bf16[2,64,256]{2,1,0:T(8,128)(2,1)S(1)} %get-tuple-element.89), channel_id=1, source_target_pairs={{0,192},{32,224},{64,0},{96,32},{128,64},{160,96},{192,128},{224,1... | collective-permute-start | bytes 196616 | tf_op jit(solution)/shard_map/side_out/ppermute | solution.py:302
  183.4 7.3 %collective-permute-start.34 = (bf16[2,64,256]{2,1,0:T(8,128)(2,1)S(1)}, bf16[2,64,256]{2,1,0:T(8,128)(2,1)S(1)}, u32[]{:S(2)}, u32[]{:S(2)}) collective-permute-start(bf16[2,64,256]{2,1,0:T(8,128)(2,1)S(1)} %get-tuple-element.90), channel_id=1, source_target_pairs={{0,224},{32,0},{64,32},{96,64},{128,96},{160,128},{192,160},{224,1... | collective-permute-start | bytes 196616 | tf_op jit(solution)/shard_map/side_out/ppermute | solution.py:302

commit v3 on v2

--- a/solution.py
+++ b/solution.py
@@ -12,8 +12,9 @@
 SIDE = ("x", "yhi")
 F32 = jnp.float32
 BF16 = jnp.bfloat16
-PARAMS = pltpu.CompilerParams(vmem_limit_bytes=16 * 2**20)
-SMALL = pltpu.CompilerParams(vmem_limit_bytes=4 * 2**20)
+WIDE = pltpu.CompilerParams(vmem_limit_bytes=56 * 2**20)
+NARROW = pltpu.CompilerParams(vmem_limit_bytes=60 * 2**20)
+SMALL = pltpu.CompilerParams(vmem_limit_bytes=8 * 2**20)
 
 
 def transposed(block):
@@ -30,14 +31,15 @@
     block = c_ref.shape[1] // BLOCKS
     lanes = block // CORE
     half = lanes // 2
-    row = lax.broadcasted_iota(jnp.int32, (block, lanes), 0)
-    column = lax.broadcasted_iota(jnp.int32, (block, lanes), 1)
-    wanted = jnp.where(column < half, column, column + half) + core_ref[0] * half
-    choose = (row == wanted).astype(F32).astype(BF16)
-    for b in range(BLOCKS):
-        out_ref[:, b * lanes:(b + 1) * lanes] = jnp.dot(
-            c_ref[:, b * block:(b + 1) * block], choose, preferred_element_type=F32
-        ).astype(BF16)
+    for core in range(CORE):
+        @pl.when(core_ref[0] == core)
+        def _():
+            for b in range(BLOCKS):
+                pieces = []
+                for y in range(YLO):
+                    tile = c_ref[:, b * block + y * lanes:b * block + (y + 1) * lanes]
+                    pieces.append(tile[:, core * half:(core + 1) * half])
+                out_ref[:, b * lanes:(b + 1) * lanes] = jnp.concatenate(pieces, axis=1)
 
 
 def pick_columns(core, orbitals):
@@ -132,7 +134,7 @@
                             pltpu.VMEM((depth * block, block), BF16),
                             pltpu.VMEM((depth * block, width), F32)],
         ),
-        compiler_params=PARAMS,
+        compiler_params=NARROW,
         name=name,
     )(place, direct, direct_other, turned, turned_other, picked)
 
@@ -169,7 +171,7 @@
         out_specs=pl.BlockSpec(out, lambda g: (0, 0, 0, 0, 0)),
         scratch_shapes=[pltpu.VMEM((depth * lanes, per_step * block), BF16),
                         pltpu.VMEM((depth * lanes, size), F32)],
-        compiler_params=PARAMS,
+        compiler_params=WIDE,
         name="second_half",
     )(partial_value, orbitals)
 
@@ -218,7 +220,7 @@
                             pltpu.VMEM((block, width), F32),
                             pltpu.VMEM((width, block), BF16)],
         ),
-        compiler_params=PARAMS,
+        compiler_params=NARROW,
         name="second_half_side",
     )(place, own, other, picked)
 
@@ -277,23 +279,26 @@
     )(mine, *parts)
 
 
-def collect_last_kernel(place, *refs):
-    out_ref = refs[BLOCKS]
+def finish_kernel(place, *refs):
+    main_ref, out_ref = refs[BLOCKS:]
+    main = main_ref.shape[0]
+    out_ref[:main] = main_ref[...]
     for d in range(BLOCKS):
         for y in range(YLO):
-            out_ref[y, (place[0] + BLOCKS - d) % BLOCKS] = refs[d][y]
-
-
-def collect_last(mine, parts):
+            out_ref[main + y * BLOCKS + (place[0] + BLOCKS - d) % BLOCKS] = refs[d][y]
+
+
+def finish(mine, parts, main):
+    pairs, rows, block = main.shape
     vmem = pl.BlockSpec(memory_space=pltpu.VMEM)
     return pl.pallas_call(
-        collect_last_kernel,
-        out_shape=jax.ShapeDtypeStruct((YLO, BLOCKS) + parts[0].shape[1:], BF16),
-        in_specs=[pl.BlockSpec(memory_space=pltpu.SMEM)] + [vmem] * BLOCKS,
+        finish_kernel,
+        out_shape=jax.ShapeDtypeStruct((pairs + YLO * BLOCKS, rows, block), BF16),
+        in_specs=[pl.BlockSpec(memory_space=pltpu.SMEM)] + [vmem] * (BLOCKS + 1),
         out_specs=vmem,
         compiler_params=SMALL,
-        name="collect_last",
-    )(mine, *parts)
+        name="finish",
+    )(mine, *parts, main)
 
 
 def rotate(parts, axes):
@@ -323,17 +328,20 @@
 
     together = lax.optimization_barrier
 
-    side = half_panel[main_pairs:].reshape(YLO, Z, rows, block)
+    with jax.named_scope("side_in"):
+        side = half_panel[main_pairs:].reshape(YLO, Z, rows, block)
+        got = swap(lax.dynamic_index_in_dim(side, 1 - ylo, 0, keepdims=False), "ylo")
+        keep = lax.dynamic_index_in_dim(side, ylo, 0, keepdims=False)
+    picked = pick_columns(scalars(core), orbitals)
+    own = half_panel[:main_pairs].reshape(COLS * YLO, depth, rows, block)
+    own, got, keep, picked = together((own, got, keep, picked))
+
     with jax.named_scope("panels_in"):
-        own = half_panel[:main_pairs].reshape(COLS * YLO, depth, rows, block)
         own = lax.all_to_all(own, PLANE, 0, 0, tiled=True)
         own = own.reshape(COLS, YLO, depth, rows, block)
     with jax.named_scope("side_in"):
-        got = swap(lax.dynamic_index_in_dim(side, 1 - ylo, 0, keepdims=False), "ylo")
-        keep = lax.dynamic_index_in_dim(side, ylo, 0, keepdims=False)
         parts = rotate(join_and_spread(scalars(z, ylo), keep, got), "z")
         side_own = collect(scalars(z), parts)
-    picked = pick_columns(scalars(core), orbitals)
     own, side_own, picked = together((own, side_own, picked))
 
     with jax.named_scope("mirror"):
@@ -363,14 +371,15 @@
 
     got = swap(send, "ylo")
     result = second_half(partial_value, orbitals)
+    result, got, keep = together((result, got, keep))
+
     with jax.named_scope("panels_out"):
         result = result.reshape(COLS * YLO, depth, rows, block)
         result = lax.all_to_all(result, PLANE, 0, 0, tiled=True)
         result = result.reshape(main_pairs, rows, block)
     with jax.named_scope("side_out"):
         parts = rotate(join_and_spread(scalars(z, ylo), keep, got), "z")
-        side_result = collect_last(scalars(z), parts).reshape(side_pairs, rows, block)
-    return jnp.concatenate([result, side_result], axis=0)
+    return finish(scalars(z), parts, result)
 
 
 def solution(mesh):

time: 193 us -> 166 us (0.86)
  waiting for transfers between devices: 58.7 us -> 26.6 us
  Pallas kernels: 29.9 us -> 40.5 us
  local copies, waits for them, and re-layouts: 12.3 us -> 5.47 us
    ppermute x7, waiting for transfers between devices: 40.5 us -> 4.4 us  [swap(): return lax.ppermute(value, axis, [(0, 1), (1, 0)])]
    unnamed x8 -> x22, local copies, waits for them, and re-layouts: 9.95 us -> 2.04 us
    ppermute x28, waiting for transfers between devices: 16.4 us -> 21.7 us  [rotate(): lax.ppermute(parts[d], axes, [(i, (i + d) % BLOCKS) for i in range(BLOCKS)])]
    pallas_call x2, Pallas kernels: 10.4 us -> 15.1 us  [first_half(): pl.pallas_call(first_kernel, out_shape=jax.ShapeDtypeStruct(out, BF16), g...]
    pallas_call x1, Pallas kernels: 3.88 us -> 6.84 us  [second_half_side(): pl.pallas_call(second_side_kernel, out_shape=[out, out], grid_spec=pltpu....]
    pallas_call x1, Pallas kernels: 5.24 us -> 7.74 us  [second_half(): pl.pallas_call(second_kernel, out_shape=jax.ShapeDtypeStruct(out, BF16),...]
  transfers between devices with their start and end apart: 39 -> 39, of which waited for: 15 -> 16; matrix products, arithmetic and copies ran while one was open for 0% -> 3% of each run, Pallas kernels for 9% -> 19%
where the time goes in v3:
time: 166 us; the launch traced here: 165 us
  starting transfers between devices  90.4 us (54%)
  Pallas kernels  40.5 us (24%)
  waiting for transfers between devices  26.6 us (16%)
  local copies, waits for them, and re-layouts  5.47 us (3%)
  other arithmetic  2.13 us (1%)
    ppermute x28, starting transfers between devices, rotate(): lax.ppermute(parts[d], axes, [(i, (i + d) % BLOCKS) for i in range(BLOCKS)])  61.7 us
    ppermute x28, waiting for transfers between devices, rotate(): lax.ppermute(parts[d], axes, [(i, (i + d) % BLOCKS) for i in range(BLOCKS)])  21.7 us
    pallas_call x2, Pallas kernels, first_half(): pl.pallas_call(first_kernel, out_shape=jax.ShapeDtypeStruct(out, BF16), g...  15.1 us
    pallas_call x1, Pallas kernels, pick_columns(): pl.pallas_call(pick_kernel, out_shape=jax.ShapeDtypeStruct((size, size //...  8.19 us
    all_to_all x1, starting transfers between devices, per_device(): partial_value = lax.all_to_all(partial_value, 'z', 0, 0, tiled=True)  7.83 us
    pallas_call x1, Pallas kernels, second_half(): pl.pallas_call(second_kernel, out_shape=jax.ShapeDtypeStruct(out, BF16),...  7.74 us
    all_to_all x1, starting transfers between devices, per_device(): own = lax.all_to_all(own, PLANE, 0, 0, tiled=True)  7.19 us
    pallas_call x1, Pallas kernels, second_half_side(): pl.pallas_call(second_side_kernel, out_shape=[out, out], grid_spec=pltpu....  6.84 us
  transfers between devices with their start and end apart: 39, of which 16 were waited for; matrix products, arithmetic and copies ran while one was open for 3% of the time, Pallas kernels for 19%

profile of v3, /device:TPU:2, one launch (start us, length us, event | category | flops | bytes accessed | tf_op | source)
XLA Modules:
  0.0 165.4 jit_solution(6332530748390750867)
XLA Ops:
  0.0 1.1 slice.7
  1.1 1.7 %collective-permute-start = (bf16[8,64,256]{2,1,0:T(8,128)(2,1)S(1)}, bf16[8,64,256]{2,1,0:T(8,128)(2,1)S(1)}, u32[]{:S(2)}, u32[]{:S(2)}) collective-permute-start(bf16[8,64,256]{2,1,0:T(8,128)(2,1)S(1)} %get-tuple-element.106), channel_id=1, source_target_pairs={{0,16},{16,0},{1,17},{17,1},{2,18},{18,2},{3,19},{19,3},{4,20},{20... | collective-permute-start | bytes 786440 | tf_op jit(solution)/shard_map/side_in/ppermute | solution.py:312
  2.8 2.3 %slice.6 = bf16[32,64,256]{2,1,0:T(8,128)(2,1)} slice(bf16[48,64,256]{2,1,0:T(8,128)(2,1)} %param.2), slice={[0:32], [0:64], [0:256]} | slice | bytes 2097152 | tf_op jit(solution)/shard_map/slice | solution.py:336
  5.1 8.2 %pick_columns.1.c_ref = bf16[2048,1024]{1,0:T(8,128)(2,1)} custom-call(s32[1]{0:T(128)} %bitcast.2.core_ref, bf16[2048,2048]{1,0:T(8,128)(2,1)} %c_ref.3), custom_call_target="tpu_custom_call" | custom-call | tf_op jit(solution)/shard_map/pick_columns/pallas_call | solution.py:48
  13.3 7.2 %all-to-all-start = ((bf16[16,2,64,256]{3,2,1,0:T(8,128)(2,1)}), bf16[16,2,64,256]{3,2,1,0:T(8,128)(2,1)}, u32[]{:S(2)}, u32[]{:S(2)}) async-start(bf16[16,2,64,256]{3,2,1,0:T(8,128)(2,1)} %bitcast.3), calls=%async_computation | async-start | bytes 2097152 | tf_op jit(solution)/shard_map/panels_in/all_to_all | solution.py:340
  20.6 0.6 join_and_spread.2
  21.2 2.0 %collective-permute-start.1 = (bf16[2,64,256]{2,1,0:T(8,128)(2,1)S(1)}, bf16[2,64,256]{2,1,0:T(8,128)(2,1)S(1)}, u32[]{:S(2)}, u32[]{:S(2)}) collective-permute-start(bf16[2,64,256]{2,1,0:T(8,128)(2,1)S(1)} %get-tuple-element.59), channel_id=1, source_target_pairs={{0,32},{32,64},{64,96},{96,128},{128,160},{160,192},{192,224},{224... | collective-permute-start | bytes 196616 | tf_op jit(solution)/shard_map/side_in/ppermute | solution.py:307
  23.2 3.3 %collective-permute-start.2 = (bf16[2,64,256]{2,1,0:T(8,128)(2,1)S(1)}, bf16[2,64,256]{2,1,0:T(8,128)(2,1)S(1)}, u32[]{:S(2)}, u32[]{:S(2)}) collective-permute-start(bf16[2,64,256]{2,1,0:T(8,128)(2,1)S(1)} %get-tuple-element.60), channel_id=1, source_target_pairs={{0,64},{32,96},{64,128},{96,160},{128,192},{160,224},{192,0},{224,... | collective-permute-start | bytes 196616 | tf_op jit(solution)/shard_map/side_in/ppermute | solution.py:307
  26.4 4.0 %collective-permute-start.3 = (bf16[2,64,256]{2,1,0:T(8,128)(2,1)S(1)}, bf16[2,64,256]{2,1,0:T(8,128)(2,1)S(1)}, u32[]{:S(2)}, u32[]{:S(2)}) collective-permute-start(bf16[2,64,256]{2,1,0:T(8,128)(2,1)S(1)} %get-tuple-element.61), channel_id=1, source_target_pairs={{0,96},{32,128},{64,160},{96,192},{128,224},{160,0},{192,32},{224,... | collective-permute-start | bytes 196616 | tf_op jit(solution)/shard_map/side_in/ppermute | solution.py:307
  30.5 0.5 collective-permute-start.4
  31.0 4.9 %collective-permute-start.5 = (bf16[2,64,256]{2,1,0:T(8,128)(2,1)S(1)}, bf16[2,64,256]{2,1,0:T(8,128)(2,1)S(1)}, u32[]{:S(2)}, u32[]{:S(2)}) collective-permute-start(bf16[2,64,256]{2,1,0:T(8,128)(2,1)S(1)} %get-tuple-element.63), channel_id=1, source_target_pairs={{0,160},{32,192},{64,224},{96,0},{128,32},{160,64},{192,96},{224,1... | collective-permute-start | bytes 196616 | tf_op jit(solution)/shard_map/side_in/ppermute | solution.py:307
  36.0 2.7 %collective-permute-start.6 = (bf16[2,64,256]{2,1,0:T(8,128)(2,1)S(1)}, bf16[2,64,256]{2,1,0:T(8,128)(2,1)S(1)}, u32[]{:S(2)}, u32[]{:S(2)}) collective-permute-start(bf16[2,64,256]{2,1,0:T(8,128)(2,1)S(1)} %get-tuple-element.64), channel_id=1, source_target_pairs={{0,192},{32,224},{64,0},{96,32},{128,64},{160,96},{192,128},{224,1... | collective-permute-start | bytes 196616 | tf_op jit(solution)/shard_map/side_in/ppermute | solution.py:307
  38.6 1.0 collective-permute-start.7
  39.6 4.0 %collective-permute-done.5.refs_5_ = bf16[2,64,256]{2,1,0:T(8,128)(2,1)S(1)} collective-permute-done((bf16[2,64,256]{2,1,0:T(8,128)(2,1)S(1)}, bf16[2,64,256]{2,1,0:T(8,128)(2,1)S(1)}, u32[]{:S(2)}, u32[]{:S(2)}) %collective-permute-start.5) | collective-permute-done | bytes 65568 | tf_op jit(solution)/shard_map/side_in/ppermute | solution.py:307
  43.6 0.7 collective-permute-done.6.refs_6_
  44.3 0.6 collective-permute-done.7.refs_7_
  45.1 4.5 %all-to-all-start.1 = ((bf16[8,2,2,64,256]{4,3,2,1,0:T(8,128)(2,1)}), bf16[8,2,2,64,256]{4,3,2,1,0:T(8,128)(2,1)S(1)}, u32[]{:S(2)}, u32[]{:S(2)}) async-start(bf16[8,2,2,64,256]{4,3,2,1,0:T(8,128)(2,1)} %bitcast.7.direct), calls=%async_computation.1 | async-start | bytes 2097152 | tf_op jit(solution)/shard_map/mirror/all_to_all | solution.py:348
  49.7 3.0 %collective-permute-start.9 = (bf16[2,64,256]{2,1,0:T(8,128)(2,1)S(1)}, bf16[2,64,256]{2,1,0:T(8,128)(2,1)S(1)}, u32[]{:S(2)}, u32[]{:S(2)}) collective-permute-start(bf16[2,64,256]{2,1,0:T(8,128)(2,1)S(1)} %get-tuple-element.70), channel_id=1, source_target_pairs={{0,1},{1,2},{2,3},{3,4},{4,5},{5,6},{6,7},{7,0},{8,9},{9,10},{10,1... | collective-permute-start | bytes 196616 | tf_op jit(solution)/shard_map/side_mirror/ppermute | solution.py:307
  52.7 1.5 collective-permute-start.10
  54.2 0.8 collective-permute-start.11
  54.9 2.8 %collective-permute-start.12 = (bf16[2,64,256]{2,1,0:T(8,128)(2,1)S(1)}, bf16[2,64,256]{2,1,0:T(8,128)(2,1)S(1)}, u32[]{:S(2)}, u32[]{:S(2)}) collective-permute-start(bf16[2,64,256]{2,1,0:T(8,128)(2,1)S(1)} %get-tuple-element.73), channel_id=1, source_target_pairs={{0,4},{1,5},{2,6},{3,7},{4,0},{5,1},{6,2},{7,3},{8,12},{9,13},{10,... | collective-permute-start | bytes 196616 | tf_op jit(solution)/shard_map/side_mirror/ppermute | solution.py:307
  57.7 3.6 %collective-permute-start.13 = (bf16[2,64,256]{2,1,0:T(8,128)(2,1)S(1)}, bf16[2,64,256]{2,1,0:T(8,128)(2,1)S(1)}, u32[]{:S(2)}, u32[]{:S(2)}) collective-permute-start(bf16[2,64,256]{2,1,0:T(8,128)(2,1)S(1)} %get-tuple-element.74), channel_id=1, source_target_pairs={{0,5},{1,6},{2,7},{3,0},{4,1},{5,2},{6,3},{7,4},{8,13},{9,14},{10,... | collective-permute-start | bytes 196616 | tf_op jit(solution)/shard_map/side_mirror/ppermute | solution.py:307
  61.3 2.1 %collective-permute-start.14 = (bf16[2,64,256]{2,1,0:T(8,128)(2,1)S(1)}, bf16[2,64,256]{2,1,0:T(8,128)(2,1)S(1)}, u32[]{:S(2)}, u32[]{:S(2)}) collective-permute-start(bf16[2,64,256]{2,1,0:T(8,128)(2,1)S(1)} %get-tuple-element.75), channel_id=1, source_target_pairs={{0,6},{1,7},{2,0},{3,1},{4,2},{5,3},{6,4},{7,5},{8,14},{9,15},{10,... | collective-permute-start | bytes 196616 | tf_op jit(solution)/shard_map/side_mirror/ppermute | solution.py:307
  63.3 0.7 collective-permute-start.15
  64.1 1.4 collective-permute-done.13.refs_5_
  65.5 0.7 collective-permute-done.14.refs_6_
  66.2 2.9 %collective-permute-done.15.refs_7_ = bf16[2,64,256]{2,1,0:T(8,128)(2,1)S(1)} collective-permute-done((bf16[2,64,256]{2,1,0:T(8,128)(2,1)S(1)}, bf16[2,64,256]{2,1,0:T(8,128)(2,1)S(1)}, u32[]{:S(2)}, u32[]{:S(2)}) %collective-permute-start.15) | collective-permute-done | bytes 65568 | tf_op jit(solution)/shard_map/side_mirror/ppermute | solution.py:307
  69.3 0.7 pad_add_fusion.1.place
  70.0 1.2 collective-permute-done.16
  71.2 0.8 copy-done.9
  72.0 6.9 %first_half_side.1.x_ref = bf16[8,1,256,128]{3,2,1,0:T(8,128)(2,1)} custom-call(s32[2]{0:T(128)} %pad_add_fusion.1.place, bf16[8,2,1,64,256]{4,3,2,1,0:T(8,128)(2,1)} %bitcast.19, bf16[8,2,1,64,256]{4,3,2,1,0:T(8,128)(2,1)} %bitcast.23, bf16[8,2,1,64,256]{4,3,2,1,0:T(8,128)(2,1)} %bitcast.17, bf16[8,2,1,64,256]{4,3,2,1,0:T(8,128)(2,1)} %bitcast.22, ...), custom_call_target="tpu_custom_call" | custom-call | tf_op jit(solution)/shard_map/side_mirror/first_half_side/pallas_call | solution.py:124
  79.2 0.7 pad_add_fusion.3.place
  79.9 1.9 %collective-permute-done.18.turned_other = bf16[8,2,2,64,256]{4,3,2,1,0:T(8,128)(2,1)} collective-permute-done((bf16[8,2,2,64,256]{4,3,2,1,0:T(8,128)(2,1)S(1)}, bf16[8,2,2,64,256]{4,3,2,1,0:T(8,128)(2,1)}, u32[]{:S(2)}, u32[]{:S(2)}) %collective-permute-start.18) | collective-permute-done | bytes 1048608 | tf_op jit(solution)/shard_map/ppermute | solution.py:312
  81.9 8.1 %first_half.1 = bf16[8,2,256,128]{3,2,1,0:T(8,128)(2,1)} custom-call(s32[2]{0:T(128)} %pad_add_fusion.3.place, bf16[8,2,2,64,256]{4,3,2,1,0:T(8,128)(2,1)} %bitcast.7.direct, bf16[8,2,2,64,256]{4,3,2,1,0:T(8,128)(2,1)} %copy-done.7, bf16[8,2,2,64,256]{4,3,2,1,0:T(8,128)(2,1)} %copy-done.5, bf16[8,2,2,64,256]{4,3,2,1,0:T(8,128)(2,1)} %collective-permute-done.18.turned_other, ...), custom_call_target="tpu_custom_call" | custom-call | tf_op jit(solution)/shard_map/first_half/pallas_call | solution.py:124
  90.0 7.8 %all-to-all-start.2 = ((bf16[8,2,256,128]{3,2,1,0:T(8,128)(2,1)}), bf16[8,2,256,128]{3,2,1,0:T(8,128)(2,1)S(1)}, u32[]{:S(2)}, u32[]{:S(2)}) async-start(bf16[8,2,256,128]{3,2,1,0:T(8,128)(2,1)} %first_half.1), calls=%async_computation.2 | async-start | bytes 2097152 | tf_op jit(solution)/shard_map/partial/all_to_all | solution.py:364
  97.9 1.3 collective-permute-start.19
  99.2 1.2 collective-permute-start.20
  100.4 3.7 %collective-permute-start.21 = (bf16[1,256,128]{2,1,0:T(8,128)(2,1)S(1)}, bf16[1,256,128]{2,1,0:T(8,128)(2,1)S(1)}, u32[]{:S(2)}, u32[]{:S(2)}) collective-permute-start(bf16[1,256,128]{2,1,0:T(8,128)(2,1)S(1)} %get-tuple-element.84), channel_id=1, source_target_pairs={{0,3},{1,4},{2,5},{3,6},{4,7},{5,0},{6,1},{7,2},{8,11},{9,12},{10,... | collective-permute-start | bytes 196616 | tf_op jit(solution)/shard_map/side_partial/ppermute | solution.py:307
  104.0 1.3 collective-permute-start.22
  105.3 2.9 %collective-permute-start.23 = (bf16[1,256,128]{2,1,0:T(8,128)(2,1)S(1)}, bf16[1,256,128]{2,1,0:T(8,128)(2,1)S(1)}, u32[]{:S(2)}, u32[]{:S(2)}) collective-permute-start(bf16[1,256,128]{2,1,0:T(8,128)(2,1)S(1)} %get-tuple-element.86), channel_id=1, source_target_pairs={{0,5},{1,6},{2,7},{3,0},{4,1},{5,2},{6,3},{7,4},{8,13},{9,14},{10,... | collective-permute-start | bytes 196616 | tf_op jit(solution)/shard_map/side_partial/ppermute | solution.py:307
  108.2 2.6 %collective-permute-start.24 = (bf16[1,256,128]{2,1,0:T(8,128)(2,1)S(1)}, bf16[1,256,128]{2,1,0:T(8,128)(2,1)S(1)}, u32[]{:S(2)}, u32[]{:S(2)}) collective-permute-start(bf16[1,256,128]{2,1,0:T(8,128)(2,1)S(1)} %get-tuple-element.87), channel_id=1, source_target_pairs={{0,6},{1,7},{2,0},{3,1},{4,2},{5,3},{6,4},{7,5},{8,14},{9,15},{10,... | collective-permute-start | bytes 196616 | tf_op jit(solution)/shard_map/side_partial/ppermute | solution.py:307
  111.2 1.0 collective-permute-done.23.refs_5_
  112.2 1.3 collective-permute-done.24.refs_6_
  113.5 3.2 %collective-permute-done.25.refs_7_ = bf16[1,256,128]{2,1,0:T(8,128)(2,1)S(1)} collective-permute-done((bf16[1,256,128]{2,1,0:T(8,128)(2,1)S(1)}, bf16[1,256,128]{2,1,0:T(8,128)(2,1)S(1)}, u32[]{:S(2)}, u32[]{:S(2)}) %collective-permute-start.25) | collective-permute-done | bytes 65568 | tf_op jit(solution)/shard_map/side_partial/ppermute | solution.py:307
  116.8 0.6 pad_add_fusion.2.place
  117.4 1.2 collective-permute-done.26.other_ref
  118.7 0.8 copy-done.10
  119.5 6.8 %second_half_side.1 = (bf16[8,64,256]{2,1,0:T(8,128)(2,1)}, bf16[8,64,256]{2,1,0:T(8,128)(2,1)}) custom-call(s32[2]{0:T(128)} %pad_add_fusion.2.place, bf16[8,1,256,128]{3,2,1,0:T(8,128)(2,1)} %copy-done.2, bf16[8,1,256,128]{3,2,1,0:T(8,128)(2,1)} %copy-done.10, bf16[2048,1024]{1,0:T(8,128)(2,1)} %pick_columns.1.c_ref), custom_call_target="tpu_custom_call" | custom-call | tf_op jit(solution)/shard_map/side_partial/second_half_side/pallas_call | solution.py:211
  126.3 0.6 all-to-all-done.2.t_ref
  126.9 0.6 collective-permute-start.27
  127.9 7.7 %second_half.1 = bf16[8,2,2,64,256]{4,3,2,1,0:T(8,128)(2,1)} custom-call(bf16[8,2,256,128]{3,2,1,0:T(8,128)(2,1)} %copy-done.6, bf16[2048,2048]{1,0:T(8,128)(2,1)} %c_ref.3), custom_call_target="tpu_custom_call" | custom-call | tf_op jit(solution)/shard_map/second_half/pallas_call | solution.py:165
  135.6 6.6 %all-to-all-start.3 = ((bf16[16,2,64,256]{3,2,1,0:T(8,128)(2,1)}), bf16[16,2,64,256]{3,2,1,0:T(8,128)(2,1)S(1)}, u32[]{:S(2)}, u32[]{:S(2)}) async-start(bf16[16,2,64,256]{3,2,1,0:T(8,128)(2,1)} %bitcast.20), calls=%async_computation.3 | async-start | bytes 2097152 | tf_op jit(solution)/shard_map/panels_out/all_to_all | solution.py:378
  142.2 0.6 join_and_spread.3
  142.8 0.6 collective-permute-start.28
  143.4 2.1 %collective-permute-start.29 = (bf16[2,64,256]{2,1,0:T(8,128)(2,1)S(1)}, bf16[2,64,256]{2,1,0:T(8,128)(2,1)S(1)}, u32[]{:S(2)}, u32[]{:S(2)}) collective-permute-start(bf16[2,64,256]{2,1,0:T(8,128)(2,1)S(1)} %get-tuple-element.98), channel_id=1, source_target_pairs={{0,64},{32,96},{64,128},{96,160},{128,192},{160,224},{192,0},{224,... | collective-permute-start | bytes 196616 | tf_op jit(solution)/shard_map/side_out/ppermute | solution.py:307
  145.5 2.7 %collective-permute-start.30 = (bf16[2,64,256]{2,1,0:T(8,128)(2,1)S(1)}, bf16[2,64,256]{2,1,0:T(8,128)(2,1)S(1)}, u32[]{:S(2)}, u32[]{:S(2)}) collective-permute-start(bf16[2,64,256]{2,1,0:T(8,128)(2,1)S(1)} %get-tuple-element.99), channel_id=1, source_target_pairs={{0,96},{32,128},{64,160},{96,192},{128,224},{160,0},{192,32},{224,... | collective-permute-start | bytes 196616 | tf_op jit(solution)/shard_map/side_out/ppermute | solution.py:307
  148.2 2.3 %collective-permute-start.31 = (bf16[2,64,256]{2,1,0:T(8,128)(2,1)S(1)}, bf16[2,64,256]{2,1,0:T(8,128)(2,1)S(1)}, u32[]{:S(2)}, u32[]{:S(2)}) collective-permute-start(bf16[2,64,256]{2,1,0:T(8,128)(2,1)S(1)} %get-tuple-element.100), channel_id=1, source_target_pairs={{0,128},{32,160},{64,192},{96,224},{128,0},{160,32},{192,64},{224,... | collective-permute-start | bytes 196616 | tf_op jit(solution)/shard_map/side_out/ppermute | solution.py:307
  150.6 2.7 %collective-permute-start.32 = (bf16[2,64,256]{2,1,0:T(8,128)(2,1)S(1)}, bf16[2,64,256]{2,1,0:T(8,128)(2,1)S(1)}, u32[]{:S(2)}, u32[]{:S(2)}) collective-permute-start(bf16[2,64,256]{2,1,0:T(8,128)(2,1)S(1)} %get-tuple-element.101), channel_id=1, source_target_pairs={{0,160},{32,192},{64,224},{96,0},{128,32},{160,64},{192,96},{224,1... | collective-permute-start | bytes 196616 | tf_op jit(solution)/shard_map/side_out/ppermute | solution.py:307
  153.2 3.6 %collective-permute-start.33 = (bf16[2,64,256]{2,1,0:T(8,128)(2,1)S(1)}, bf16[2,64,256]{2,1,0:T(8,128)(2,1)S(1)}, u32[]{:S(2)}, u32[]{:S(2)}) collective-permute-start(bf16[2,64,256]{2,1,0:T(8,128)(2,1)S(1)} %get-tuple-element.102), channel_id=1, source_target_pairs={{0,192},{32,224},{64,0},{96,32},{128,64},{160,96},{192,128},{224,1... | collective-permute-start | bytes 196616 | tf_op jit(solution)/shard_map/side_out/ppermute | solution.py:307
  156.8 1.5 collective-permute-start.34
  158.3 3.7 %collective-permute-done.32.refs_5_ = bf16[2,64,256]{2,1,0:T(8,128)(2,1)S(1)} collective-permute-done((bf16[2,64,256]{2,1,0:T(8,128)(2,1)S(1)}, bf16[2,64,256]{2,1,0:T(8,128)(2,1)S(1)}, u32[]{:S(2)}, u32[]{:S(2)}) %collective-permute-start.32) | collective-permute-done | bytes 65568 | tf_op jit(solution)/shard_map/side_out/ppermute | solution.py:307
  162.0 1.0 collective-permute-done.33.refs_6_
  163.0 1.1 collective-permute-done.34.refs_7_
  164.1 1.2 finish.1
  (56 shorter events, 1.6 us)
Async XLA Ops:
  1.1 12.2 %collective-permute-start = (bf16[8,64,256]{2,1,0:T(8,128)(2,1)S(1)}, bf16[8,64,256]{2,1,0:T(8,128)(2,1)S(1)}, u32[]{:S(2)}, u32[]{:S(2)}) collective-permute-start(bf16[8,64,256]{2,1,0:T(8,128)(2,1)S(1)} %get-tuple-element.106), channel_id=1, source_target_pairs={{0,16},{16,0},{1,17},{17,1},{2,18},{18,2},{3,19},{19,3},{4,20},{20... | collective-permute-start | bytes 786440 | tf_op jit(solution)/shard_map/side_in/ppermute | solution.py:312
  13.3 31.8 %all-to-all-start = ((bf16[16,2,64,256]{3,2,1,0:T(8,128)(2,1)}), bf16[16,2,64,256]{3,2,1,0:T(8,128)(2,1)}, u32[]{:S(2)}, u32[]{:S(2)}) async-start(bf16[16,2,64,256]{3,2,1,0:T(8,128)(2,1)} %bitcast.3), calls=%async_computation | async-start | bytes 2097152 | tf_op jit(solution)/shard_map/panels_in/all_to_all | solution.py:340
  21.2 14.8 %collective-permute-start.1 = (bf16[2,64,256]{2,1,0:T(8,128)(2,1)S(1)}, bf16[2,64,256]{2,1,0:T(8,128)(2,1)S(1)}, u32[]{:S(2)}, u32[]{:S(2)}) collective-permute-start(bf16[2,64,256]{2,1,0:T(8,128)(2,1)S(1)} %get-tuple-element.59), channel_id=1, source_target_pairs={{0,32},{32,64},{64,96},{96,128},{128,160},{160,192},{192,224},{224... | collective-permute-start | bytes 196616 | tf_op jit(solution)/shard_map/side_in/ppermute | solution.py:307
  23.2 15.5 %collective-permute-start.2 = (bf16[2,64,256]{2,1,0:T(8,128)(2,1)S(1)}, bf16[2,64,256]{2,1,0:T(8,128)(2,1)S(1)}, u32[]{:S(2)}, u32[]{:S(2)}) collective-permute-start(bf16[2,64,256]{2,1,0:T(8,128)(2,1)S(1)} %get-tuple-element.60), channel_id=1, source_target_pairs={{0,64},{32,96},{64,128},{96,160},{128,192},{160,224},{192,0},{224,... | collective-permute-start | bytes 196616 | tf_op jit(solution)/shard_map/side_in/ppermute | solution.py:307
  26.4 13.2 %collective-permute-start.3 = (bf16[2,64,256]{2,1,0:T(8,128)(2,1)S(1)}, bf16[2,64,256]{2,1,0:T(8,128)(2,1)S(1)}, u32[]{:S(2)}, u32[]{:S(2)}) collective-permute-start(bf16[2,64,256]{2,1,0:T(8,128)(2,1)S(1)} %get-tuple-element.61), channel_id=1, source_target_pairs={{0,96},{32,128},{64,160},{96,192},{128,224},{160,0},{192,32},{224,... | collective-permute-start | bytes 196616 | tf_op jit(solution)/shard_map/side_in/ppermute | solution.py:307
  30.5 9.2 %collective-permute-start.4 = (bf16[2,64,256]{2,1,0:T(8,128)(2,1)S(1)}, bf16[2,64,256]{2,1,0:T(8,128)(2,1)S(1)}, u32[]{:S(2)}, u32[]{:S(2)}) collective-permute-start(bf16[2,64,256]{2,1,0:T(8,128)(2,1)S(1)} %get-tuple-element.62), channel_id=1, source_target_pairs={{0,128},{32,160},{64,192},{96,224},{128,0},{160,32},{192,64},{224,... | collective-permute-start | bytes 196616 | tf_op jit(solution)/shard_map/side_in/ppermute | solution.py:307
  31.0 12.6 %collective-permute-start.5 = (bf16[2,64,256]{2,1,0:T(8,128)(2,1)S(1)}, bf16[2,64,256]{2,1,0:T(8,128)(2,1)S(1)}, u32[]{:S(2)}, u32[]{:S(2)}) collective-permute-start(bf16[2,64,256]{2,1,0:T(8,128)(2,1)S(1)} %get-tuple-element.63), channel_id=1, source_target_pairs={{0,160},{32,192},{64,224},{96,0},{128,32},{160,64},{192,96},{224,1... | collective-permute-start | bytes 196616 | tf_op jit(solution)/shard_map/side_in/ppermute | solution.py:307
  36.0 8.4 %collective-permute-start.6 = (bf16[2,64,256]{2,1,0:T(8,128)(2,1)S(1)}, bf16[2,64,256]{2,1,0:T(8,128)(2,1)S(1)}, u32[]{:S(2)}, u32[]{:S(2)}) collective-permute-start(bf16[2,64,256]{2,1,0:T(8,128)(2,1)S(1)} %get-tuple-element.64), channel_id=1, source_target_pairs={{0,192},{32,224},{64,0},{96,32},{128,64},{160,96},{192,128},{224,1... | collective-permute-start | bytes 196616 | tf_op jit(solution)/shard_map/side_in/ppermute | solution.py:307
  38.6 6.4 %collective-permute-start.7 = (bf16[2,64,256]{2,1,0:T(8,128)(2,1)S(1)}, bf16[2,64,256]{2,1,0:T(8,128)(2,1)S(1)}, u32[]{:S(2)}, u32[]{:S(2)}) collective-permute-start(bf16[2,64,256]{2,1,0:T(8,128)(2,1)S(1)} %get-tuple-element.65), channel_id=1, source_target_pairs={{0,224},{32,0},{64,32},{96,64},{128,96},{160,128},{192,160},{224,1... | collective-permute-start | bytes 196616 | tf_op jit(solution)/shard_map/side_in/ppermute | solution.py:307
  45.0 26.9 %copy-start = (bf16[8,2,64,256]{3,2,1,0:T(8,128)(2,1)}, bf16[8,2,64,256]{3,2,1,0:T(8,128)(2,1)S(1)}, u32[]{:S(2)}) copy-start(bf16[8,2,64,256]{3,2,1,0:T(8,128)(2,1)S(1)} %collect.3.x_ref) | copy-start | bytes 1572868
  45.1 33.9 %all-to-all-start.1 = ((bf16[8,2,2,64,256]{4,3,2,1,0:T(8,128)(2,1)}), bf16[8,2,2,64,256]{4,3,2,1,0:T(8,128)(2,1)S(1)}, u32[]{:S(2)}, u32[]{:S(2)}) async-start(bf16[8,2,2,64,256]{4,3,2,1,0:T(8,128)(2,1)} %bitcast.7.direct), calls=%async_computation.1 | async-start | bytes 2097152 | tf_op jit(solution)/shard_map/mirror/all_to_all | solution.py:348
  49.6 29.4 %collective-permute-start.8 = (bf16[8,2,2,64,256]{4,3,2,1,0:T(8,128)(2,1)}, bf16[8,2,2,64,256]{4,3,2,1,0:T(8,128)(2,1)S(1)}, u32[]{:S(2)}, u32[]{:S(2)}) collective-permute-start(bf16[8,2,2,64,256]{4,3,2,1,0:T(8,128)(2,1)} %bitcast.7.direct), channel_id=1, source_target_pairs={{0,8},{8,0},{1,9},{9,1},{2,10},{10,2},{3,11},{11,3},{4,12},{12,4},... | collective-permute-start | bytes 3145736 | tf_op jit(solution)/shard_map/ppermute | solution.py:312
  49.7 8.0 %collective-permute-start.9 = (bf16[2,64,256]{2,1,0:T(8,128)(2,1)S(1)}, bf16[2,64,256]{2,1,0:T(8,128)(2,1)S(1)}, u32[]{:S(2)}, u32[]{:S(2)}) collective-permute-start(bf16[2,64,256]{2,1,0:T(8,128)(2,1)S(1)} %get-tuple-element.70), channel_id=1, source_target_pairs={{0,1},{1,2},{2,3},{3,4},{4,5},{5,6},{6,7},{7,0},{8,9},{9,10},{10,1... | collective-permute-start | bytes 196616 | tf_op jit(solution)/shard_map/side_mirror/ppermute | solution.py:307
  52.7 8.6 %collective-permute-start.10 = (bf16[2,64,256]{2,1,0:T(8,128)(2,1)S(1)}, bf16[2,64,256]{2,1,0:T(8,128)(2,1)S(1)}, u32[]{:S(2)}, u32[]{:S(2)}) collective-permute-start(bf16[2,64,256]{2,1,0:T(8,128)(2,1)S(1)} %get-tuple-element.71), channel_id=1, source_target_pairs={{0,2},{1,3},{2,4},{3,5},{4,6},{5,7},{6,0},{7,1},{8,10},{9,11},{10,... | collective-permute-start | bytes 196616 | tf_op jit(solution)/shard_map/side_mirror/ppermute | solution.py:307
  54.2 9.2 %collective-permute-start.11 = (bf16[2,64,256]{2,1,0:T(8,128)(2,1)S(1)}, bf16[2,64,256]{2,1,0:T(8,128)(2,1)S(1)}, u32[]{:S(2)}, u32[]{:S(2)}) collective-permute-start(bf16[2,64,256]{2,1,0:T(8,128)(2,1)S(1)} %get-tuple-element.72), channel_id=1, source_target_pairs={{0,3},{1,4},{2,5},{3,6},{4,7},{5,0},{6,1},{7,2},{8,11},{9,12},{10,... | collective-permute-start | bytes 196616 | tf_op jit(solution)/shard_map/side_mirror/ppermute | solution.py:307
  54.9 9.1 %collective-permute-start.12 = (bf16[2,64,256]{2,1,0:T(8,128)(2,1)S(1)}, bf16[2,64,256]{2,1,0:T(8,128)(2,1)S(1)}, u32[]{:S(2)}, u32[]{:S(2)}) collective-permute-start(bf16[2,64,256]{2,1,0:T(8,128)(2,1)S(1)} %get-tuple-element.73), channel_id=1, source_target_pairs={{0,4},{1,5},{2,6},{3,7},{4,0},{5,1},{6,2},{7,3},{8,12},{9,13},{10,... | collective-permute-start | bytes 196616 | tf_op jit(solution)/shard_map/side_mirror/ppermute | solution.py:307
  57.7 7.8 %collective-permute-start.13 = (bf16[2,64,256]{2,1,0:T(8,128)(2,1)S(1)}, bf16[2,64,256]{2,1,0:T(8,128)(2,1)S(1)}, u32[]{:S(2)}, u32[]{:S(2)}) collective-permute-start(bf16[2,64,256]{2,1,0:T(8,128)(2,1)S(1)} %get-tuple-element.74), channel_id=1, source_target_pairs={{0,5},{1,6},{2,7},{3,0},{4,1},{5,2},{6,3},{7,4},{8,13},{9,14},{10,... | collective-permute-start | bytes 196616 | tf_op jit(solution)/shard_map/side_mirror/ppermute | solution.py:307
  61.3 4.9 %collective-permute-start.14 = (bf16[2,64,256]{2,1,0:T(8,128)(2,1)S(1)}, bf16[2,64,256]{2,1,0:T(8,128)(2,1)S(1)}, u32[]{:S(2)}, u32[]{:S(2)}) collective-permute-start(bf16[2,64,256]{2,1,0:T(8,128)(2,1)S(1)} %get-tuple-element.75), channel_id=1, source_target_pairs={{0,6},{1,7},{2,0},{3,1},{4,2},{5,3},{6,4},{7,5},{8,14},{9,15},{10,... | collective-permute-start | bytes 196616 | tf_op jit(solution)/shard_map/side_mirror/ppermute | solution.py:307
  63.3 5.8 %collective-permute-start.15 = (bf16[2,64,256]{2,1,0:T(8,128)(2,1)S(1)}, bf16[2,64,256]{2,1,0:T(8,128)(2,1)S(1)}, u32[]{:S(2)}, u32[]{:S(2)}) collective-permute-start(bf16[2,64,256]{2,1,0:T(8,128)(2,1)S(1)} %get-tuple-element.76), channel_id=1, source_target_pairs={{0,7},{1,0},{2,1},{3,2},{4,3},{5,4},{6,5},{7,6},{8,15},{9,8},{10,9... | collective-permute-start | bytes 196616 | tf_op jit(solution)/shard_map/side_mirror/ppermute | solution.py:307
  64.1 5.9 %collective-permute-start.17 = (bf16[8,2,64,256]{3,2,1,0:T(8,128)(2,1)S(1)}, bf16[8,2,64,256]{3,2,1,0:T(8,128)(2,1)S(1)}, u32[]{:S(2)}, u32[]{:S(2)}) collective-permute-start(bf16[8,2,64,256]{3,2,1,0:T(8,128)(2,1)S(1)} %collect.3.x_ref), channel_id=1, source_target_pairs={{0,8},{8,0},{1,9},{9,1},{2,10},{10,2},{3,11},{11,3},{4,12},{12,4},... | collective-permute-start | bytes 1572872 | tf_op jit(solution)/shard_map/side_mirror/ppermute | solution.py:312
  69.2 2.8 %copy-start.3 = (bf16[8,2,64,256]{3,2,1,0:T(8,128)(2,1)}, bf16[8,2,64,256]{3,2,1,0:T(8,128)(2,1)S(1)}, u32[]{:S(2)}) copy-start(bf16[8,2,64,256]{3,2,1,0:T(8,128)(2,1)S(1)} %collect.4) | copy-start | bytes 1572868
  69.2 2.0 %collective-permute-start.16 = (bf16[8,2,64,256]{3,2,1,0:T(8,128)(2,1)S(1)}, bf16[8,2,64,256]{3,2,1,0:T(8,128)(2,1)S(1)}, u32[]{:S(2)}, u32[]{:S(2)}) collective-permute-start(bf16[8,2,64,256]{3,2,1,0:T(8,128)(2,1)S(1)} %collect.4), channel_id=1, source_target_pairs={{0,8},{8,0},{1,9},{9,1},{2,10},{10,2},{3,11},{11,3},{4,12},{12,4},... | collective-permute-start | bytes 1572872 | tf_op jit(solution)/shard_map/side_mirror/ppermute | solution.py:312
  70.0 2.1 %copy-start.8 = (bf16[8,2,64,256]{3,2,1,0:T(8,128)(2,1)}, bf16[8,2,64,256]{3,2,1,0:T(8,128)(2,1)S(1)}, u32[]{:S(2)}) copy-start(bf16[8,2,64,256]{3,2,1,0:T(8,128)(2,1)S(1)} %collective-permute-done.17) | copy-start | bytes 1572868
  71.2 0.8 copy-start.9
  78.9 2.9 %copy-start.7 = (bf16[8,2,2,64,256]{4,3,2,1,0:T(8,128)(2,1)}, bf16[8,2,2,64,256]{4,3,2,1,0:T(8,128)(2,1)S(1)}, u32[]{:S(2)}) copy-start(bf16[8,2,2,64,256]{4,3,2,1,0:T(8,128)(2,1)S(1)} %collective-permute-done.8.direct_other) | copy-start | bytes 3145732
  79.0 2.9 %copy-start.5 = (bf16[8,2,2,64,256]{4,3,2,1,0:T(8,128)(2,1)}, bf16[8,2,2,64,256]{4,3,2,1,0:T(8,128)(2,1)S(1)}, u32[]{:S(2)}) copy-start(bf16[8,2,2,64,256]{4,3,2,1,0:T(8,128)(2,1)S(1)} %all-to-all-done.1.turned) | copy-start | bytes 3145732
  79.0 2.9 %collective-permute-start.18 = (bf16[8,2,2,64,256]{4,3,2,1,0:T(8,128)(2,1)S(1)}, bf16[8,2,2,64,256]{4,3,2,1,0:T(8,128)(2,1)}, u32[]{:S(2)}, u32[]{:S(2)}) collective-permute-start(bf16[8,2,2,64,256]{4,3,2,1,0:T(8,128)(2,1)S(1)} %all-to-all-done.1.turned), channel_id=1, source_target_pairs={{0,8},{8,0},{1,9},{9,1},{2,10},{10,2},{3,11},{11,3},{4,12},{12,4},... | collective-permute-start | bytes 3145736 | tf_op jit(solution)/shard_map/ppermute | solution.py:312
  79.9 17.9 %copy-start.1 = (bf16[8,1,256,128]{3,2,1,0:T(8,128)(2,1)S(1)}, bf16[8,1,256,128]{3,2,1,0:T(8,128)(2,1)}, u32[]{:S(2)}) copy-start(bf16[8,1,256,128]{3,2,1,0:T(8,128)(2,1)} %first_half_side.1.x_ref) | copy-start | bytes 1572868
  90.0 36.9 %all-to-all-start.2 = ((bf16[8,2,256,128]{3,2,1,0:T(8,128)(2,1)}), bf16[8,2,256,128]{3,2,1,0:T(8,128)(2,1)S(1)}, u32[]{:S(2)}, u32[]{:S(2)}) async-start(bf16[8,2,256,128]{3,2,1,0:T(8,128)(2,1)} %first_half.1), calls=%async_computation.2 | async-start | bytes 2097152 | tf_op jit(solution)/shard_map/partial/all_to_all | solution.py:364
  97.9 10.4 %collective-permute-start.19 = (bf16[1,256,128]{2,1,0:T(8,128)(2,1)S(1)}, bf16[1,256,128]{2,1,0:T(8,128)(2,1)S(1)}, u32[]{:S(2)}, u32[]{:S(2)}) collective-permute-start(bf16[1,256,128]{2,1,0:T(8,128)(2,1)S(1)} %get-tuple-element.82), channel_id=1, source_target_pairs={{0,1},{1,2},{2,3},{3,4},{4,5},{5,6},{6,7},{7,0},{8,9},{9,10},{10,1... | collective-permute-start | bytes 196616 | tf_op jit(solution)/shard_map/side_partial/ppermute | solution.py:307
  99.2 11.7 %collective-permute-start.20 = (bf16[1,256,128]{2,1,0:T(8,128)(2,1)S(1)}, bf16[1,256,128]{2,1,0:T(8,128)(2,1)S(1)}, u32[]{:S(2)}, u32[]{:S(2)}) collective-permute-start(bf16[1,256,128]{2,1,0:T(8,128)(2,1)S(1)} %get-tuple-element.83), channel_id=1, source_target_pairs={{0,2},{1,3},{2,4},{3,5},{4,6},{5,7},{6,0},{7,1},{8,10},{9,11},{10,... | collective-permute-start | bytes 196616 | tf_op jit(solution)/shard_map/side_partial/ppermute | solution.py:307
  100.4 10.9 %collective-permute-start.21 = (bf16[1,256,128]{2,1,0:T(8,128)(2,1)S(1)}, bf16[1,256,128]{2,1,0:T(8,128)(2,1)S(1)}, u32[]{:S(2)}, u32[]{:S(2)}) collective-permute-start(bf16[1,256,128]{2,1,0:T(8,128)(2,1)S(1)} %get-tuple-element.84), channel_id=1, source_target_pairs={{0,3},{1,4},{2,5},{3,6},{4,7},{5,0},{6,1},{7,2},{8,11},{9,12},{10,... | collective-permute-start | bytes 196616 | tf_op jit(solution)/shard_map/side_partial/ppermute | solution.py:307
  104.0 7.2 %collective-permute-start.22 = (bf16[1,256,128]{2,1,0:T(8,128)(2,1)S(1)}, bf16[1,256,128]{2,1,0:T(8,128)(2,1)S(1)}, u32[]{:S(2)}, u32[]{:S(2)}) collective-permute-start(bf16[1,256,128]{2,1,0:T(8,128)(2,1)S(1)} %get-tuple-element.85), channel_id=1, source_target_pairs={{0,4},{1,5},{2,6},{3,7},{4,0},{5,1},{6,2},{7,3},{8,12},{9,13},{10,... | collective-permute-start | bytes 196616 | tf_op jit(solution)/shard_map/side_partial/ppermute | solution.py:307
  105.3 6.9 %collective-permute-start.23 = (bf16[1,256,128]{2,1,0:T(8,128)(2,1)S(1)}, bf16[1,256,128]{2,1,0:T(8,128)(2,1)S(1)}, u32[]{:S(2)}, u32[]{:S(2)}) collective-permute-start(bf16[1,256,128]{2,1,0:T(8,128)(2,1)S(1)} %get-tuple-element.86), channel_id=1, source_target_pairs={{0,5},{1,6},{2,7},{3,0},{4,1},{5,2},{6,3},{7,4},{8,13},{9,14},{10,... | collective-permute-start | bytes 196616 | tf_op jit(solution)/shard_map/side_partial/ppermute | solution.py:307
  108.2 5.2 %collective-permute-start.24 = (bf16[1,256,128]{2,1,0:T(8,128)(2,1)S(1)}, bf16[1,256,128]{2,1,0:T(8,128)(2,1)S(1)}, u32[]{:S(2)}, u32[]{:S(2)}) collective-permute-start(bf16[1,256,128]{2,1,0:T(8,128)(2,1)S(1)} %get-tuple-element.87), channel_id=1, source_target_pairs={{0,6},{1,7},{2,0},{3,1},{4,2},{5,3},{6,4},{7,5},{8,14},{9,15},{10,... | collective-permute-start | bytes 196616 | tf_op jit(solution)/shard_map/side_partial/ppermute | solution.py:307
  110.9 5.8 %collective-permute-start.25 = (bf16[1,256,128]{2,1,0:T(8,128)(2,1)S(1)}, bf16[1,256,128]{2,1,0:T(8,128)(2,1)S(1)}, u32[]{:S(2)}, u32[]{:S(2)}) collective-permute-start(bf16[1,256,128]{2,1,0:T(8,128)(2,1)S(1)} %get-tuple-element.88), channel_id=1, source_target_pairs={{0,7},{1,0},{2,1},{3,2},{4,3},{5,4},{6,5},{7,6},{8,15},{9,8},{10,9... | collective-permute-start | bytes 196616 | tf_op jit(solution)/shard_map/side_partial/ppermute | solution.py:307
  116.7 2.0 %copy-start.2 = (bf16[8,1,256,128]{3,2,1,0:T(8,128)(2,1)}, bf16[8,1,256,128]{3,2,1,0:T(8,128)(2,1)S(1)}, u32[]{:S(2)}) copy-start(bf16[8,1,256,128]{3,2,1,0:T(8,128)(2,1)S(1)} %collect.5.t_ref) | copy-start | bytes 1572868
  116.7 2.0 %collective-permute-start.26 = (bf16[8,1,256,128]{3,2,1,0:T(8,128)(2,1)S(1)}, bf16[8,1,256,128]{3,2,1,0:T(8,128)(2,1)S(1)}, u32[]{:S(2)}, u32[]{:S(2)}) collective-permute-start(bf16[8,1,256,128]{3,2,1,0:T(8,128)(2,1)S(1)} %collect.5.t_ref), channel_id=1, source_target_pairs={{0,8},{8,0},{1,9},{9,1},{2,10},{10,2},{3,11},{11,3},{4,12},{12,4},... | collective-permute-start | bytes 1572872 | tf_op jit(solution)/shard_map/side_partial/ppermute | solution.py:312
  118.7 0.8 copy-start.10
  126.9 1.0 copy-start.6
  126.9 15.3 %copy-start.4 = (bf16[8,64,256]{2,1,0:T(8,128)(2,1)S(1)}, bf16[8,64,256]{2,1,0:T(8,128)(2,1)}, u32[]{:S(2)}) copy-start(bf16[8,64,256]{2,1,0:T(8,128)(2,1)} %get-tuple-element.94.keep) | copy-start | bytes 786436
  126.9 8.7 %collective-permute-start.27 = (bf16[8,64,256]{2,1,0:T(8,128)(2,1)}, bf16[8,64,256]{2,1,0:T(8,128)(2,1)S(1)}, u32[]{:S(2)}, u32[]{:S(2)}) collective-permute-start(bf16[8,64,256]{2,1,0:T(8,128)(2,1)} %get-tuple-element.92), channel_id=1, source_target_pairs={{0,16},{16,0},{1,17},{17,1},{2,18},{18,2},{3,19},{19,3},{4,20},{20... | collective-permute-start | bytes 786440 | tf_op jit(solution)/shard_map/ppermute | solution.py:312
  135.6 28.5 %all-to-all-start.3 = ((bf16[16,2,64,256]{3,2,1,0:T(8,128)(2,1)}), bf16[16,2,64,256]{3,2,1,0:T(8,128)(2,1)S(1)}, u32[]{:S(2)}, u32[]{:S(2)}) async-start(bf16[16,2,64,256]{3,2,1,0:T(8,128)(2,1)} %bitcast.20), calls=%async_computation.3 | async-start | bytes 2097152 | tf_op jit(solution)/shard_map/panels_out/all_to_all | solution.py:378
  142.8 10.5 %collective-permute-start.28 = (bf16[2,64,256]{2,1,0:T(8,128)(2,1)S(1)}, bf16[2,64,256]{2,1,0:T(8,128)(2,1)S(1)}, u32[]{:S(2)}, u32[]{:S(2)}) collective-permute-start(bf16[2,64,256]{2,1,0:T(8,128)(2,1)S(1)} %get-tuple-element.97), channel_id=1, source_target_pairs={{0,32},{32,64},{64,96},{96,128},{128,160},{160,192},{192,224},{224... | collective-permute-start | bytes 196616 | tf_op jit(solution)/shard_map/side_out/ppermute | solution.py:307
  143.4 13.4 %collective-permute-start.29 = (bf16[2,64,256]{2,1,0:T(8,128)(2,1)S(1)}, bf16[2,64,256]{2,1,0:T(8,128)(2,1)S(1)}, u32[]{:S(2)}, u32[]{:S(2)}) collective-permute-start(bf16[2,64,256]{2,1,0:T(8,128)(2,1)S(1)} %get-tuple-element.98), channel_id=1, source_target_pairs={{0,64},{32,96},{64,128},{96,160},{128,192},{160,224},{192,0},{224,... | collective-permute-start | bytes 196616 | tf_op jit(solution)/shard_map/side_out/ppermute | solution.py:307
  145.5 12.8 %collective-permute-start.30 = (bf16[2,64,256]{2,1,0:T(8,128)(2,1)S(1)}, bf16[2,64,256]{2,1,0:T(8,128)(2,1)S(1)}, u32[]{:S(2)}, u32[]{:S(2)}) collective-permute-start(bf16[2,64,256]{2,1,0:T(8,128)(2,1)S(1)} %get-tuple-element.99), channel_id=1, source_target_pairs={{0,96},{32,128},{64,160},{96,192},{128,224},{160,0},{192,32},{224,... | collective-permute-start | bytes 196616 | tf_op jit(solution)/shard_map/side_out/ppermute | solution.py:307
  148.2 10.1 %collective-permute-start.31 = (bf16[2,64,256]{2,1,0:T(8,128)(2,1)S(1)}, bf16[2,64,256]{2,1,0:T(8,128)(2,1)S(1)}, u32[]{:S(2)}, u32[]{:S(2)}) collective-permute-start(bf16[2,64,256]{2,1,0:T(8,128)(2,1)S(1)} %get-tuple-element.100), channel_id=1, source_target_pairs={{0,128},{32,160},{64,192},{96,224},{128,0},{160,32},{192,64},{224,... | collective-permute-start | bytes 196616 | tf_op jit(solution)/shard_map/side_out/ppermute | solution.py:307
  150.6 11.5 %collective-permute-start.32 = (bf16[2,64,256]{2,1,0:T(8,128)(2,1)S(1)}, bf16[2,64,256]{2,1,0:T(8,128)(2,1)S(1)}, u32[]{:S(2)}, u32[]{:S(2)}) collective-permute-start(bf16[2,64,256]{2,1,0:T(8,128)(2,1)S(1)} %get-tuple-element.101), channel_id=1, source_target_pairs={{0,160},{32,192},{64,224},{96,0},{128,32},{160,64},{192,96},{224,1... | collective-permute-start | bytes 196616 | tf_op jit(solution)/shard_map/side_out/ppermute | solution.py:307
  153.2 9.8 %collective-permute-start.33 = (bf16[2,64,256]{2,1,0:T(8,128)(2,1)S(1)}, bf16[2,64,256]{2,1,0:T(8,128)(2,1)S(1)}, u32[]{:S(2)}, u32[]{:S(2)}) collective-permute-start(bf16[2,64,256]{2,1,0:T(8,128)(2,1)S(1)} %get-tuple-element.102), channel_id=1, source_target_pairs={{0,192},{32,224},{64,0},{96,32},{128,64},{160,96},{192,128},{224,1... | collective-permute-start | bytes 196616 | tf_op jit(solution)/shard_map/side_out/ppermute | solution.py:307
  156.8 7.3 %collective-permute-start.34 = (bf16[2,64,256]{2,1,0:T(8,128)(2,1)S(1)}, bf16[2,64,256]{2,1,0:T(8,128)(2,1)S(1)}, u32[]{:S(2)}, u32[]{:S(2)}) collective-permute-start(bf16[2,64,256]{2,1,0:T(8,128)(2,1)S(1)} %get-tuple-element.103), channel_id=1, source_target_pairs={{0,224},{32,0},{64,32},{96,64},{128,96},{160,128},{192,160},{224,1... | collective-permute-start | bytes 196616 | tf_op jit(solution)/shard_map/side_out/ppermute | solution.py:307

commit v4 on v3

v4 whole, which is shorter than its diff:
```python
import jax
import jax.numpy as jnp
from jax import lax
from jax.experimental import pallas as pl
from jax.experimental.pallas import tpu as pltpu
from jax.sharding import Mesh, PartitionSpec as P

Z, YLO, CORE, X, YHI = 8, 2, 2, 4, 2
COLS = X * YHI
BLOCKS = 8
RING = 4
PLANE = ("x", "yhi", "ylo")
F32 = jnp.float32
BF16 = jnp.bfloat16
AT_Z, AT_YLO, AT_CORE, AT_X, AT_YHI = range(5)
WIDE = pltpu.CompilerParams(vmem_limit_bytes=56 * 2**20)
NARROW = pltpu.CompilerParams(vmem_limit_bytes=60 * 2**20)
SMALL = pltpu.CompilerParams(vmem_limit_bytes=8 * 2**20)
SCALARS = pl.BlockSpec(memory_space=pltpu.SMEM)
VMEM = pl.BlockSpec(memory_space=pltpu.VMEM)


def array(*shape):
    return jax.ShapeDtypeStruct(shape, BF16)


def aligned(start, size):
    return pl.ds(pl.multiple_of(start, size), size)


def transposed(block):
    size = block.shape[1]
    row = lax.broadcasted_iota(jnp.int32, (size, size), 0)
    column = lax.broadcasted_iota(jnp.int32, (size, size), 1)
    eye = (row == column).astype(F32).astype(BF16)
    return lax.dot_general(
        eye, block, (((1,), (1,)), ((), ())), preferred_element_type=F32
    ).astype(BF16)


def pick_kernel(place, c_ref, out_ref):
    block = c_ref.shape[1] // BLOCKS
    lanes = block // CORE
    half = lanes // 2
    for core in range(CORE):
        @pl.when(place[AT_CORE] == core)
        def _():
            for b in range(BLOCKS):
                pieces = []
                for y in range(YLO):
                    tile = c_ref[:, b * block + y * lanes:b * block + (y + 1) * lanes]
                    pieces.append(tile[:, core * half:(core + 1) * half])
                out_ref[:, b * lanes:(b + 1) * lanes] = jnp.concatenate(pieces, axis=1)


def pick_columns(place, orbitals):
    size = orbitals.shape[0]
    block = size // BLOCKS
    return pl.pallas_call(
        pick_kernel,
        out_shape=array(size, size // CORE),
        grid_spec=pltpu.PrefetchScalarGridSpec(
            num_scalar_prefetch=1,
            grid=(BLOCKS,),
            in_specs=[pl.BlockSpec((block, size), lambda g, s: (g, 0))],
            out_specs=pl.BlockSpec((block, size // CORE), lambda g, s: (g, 0)),
        ),
        name="pick_columns",
    )(place, orbitals)


def accumulate(total, product):
    step = pl.program_id(0)

    @pl.when(step == 0)
    def _():
        total[...] = product

    @pl.when(step > 0)
    def _():
        total[...] += product


def build_symmetric(mine, core, direct, direct_other, turned, turned_other, sym, turn):
    per_step, _, depth, rows, block = direct.shape
    step = pl.program_id(0)
    for u in range(per_step):
        b = step * per_step + u
        cols = slice(u * block, (u + 1) * block)

        @pl.when(b >= mine)
        def _():
            for k in range(depth):
                for y in range(YLO):
                    at = k * block + y * CORE * rows
                    sym[aligned(at + core * rows, rows), cols] = direct[u, y, k]
                    sym[aligned(at + (1 - core) * rows, rows), cols] = direct_other[u, y, k]

        @pl.when(b == mine)
        def _():
            row = lax.broadcasted_iota(jnp.int32, (block, block), 0)
            column = lax.broadcasted_iota(jnp.int32, (block, block), 1)
            for k in range(depth):
                upper = sym[k * block:(k + 1) * block, cols]
                sym[k * block:(k + 1) * block, cols] = jnp.where(row <= column, upper, transposed(upper))

        @pl.when(b < mine)
        def _():
            for k in range(depth):
                for y in range(YLO):
                    at = k * block + y * CORE * rows
                    turn[aligned(at + core * rows, rows), :] = turned[u, y, k]
                    turn[aligned(at + (1 - core) * rows, rows), :] = turned_other[u, y, k]
            for k in range(depth):
                sym[k * block:(k + 1) * block, cols] = transposed(turn[k * block:(k + 1) * block])


def last_step():
    return pl.program_id(0) == pl.num_programs(0) - 1


def first_main_kernel(place, direct, direct_other, turned, turned_other, c_ref, t_ref, sym, turn, total):
    build_symmetric(place[AT_Z], place[AT_CORE], direct, direct_other, turned, turned_other, sym, turn)
    accumulate(total, jnp.dot(sym[...], c_ref[...], preferred_element_type=F32))

    @pl.when(last_step())
    def _():
        count, depth, block, lanes = t_ref.shape
        for part in range(count):
            for k in range(depth):
                t_ref[part, k] = total[k * block:(k + 1) * block, part * lanes:(part + 1) * lanes].astype(BF16)


def first_side_kernel(place, direct, direct_other, turned, turned_other, c_ref, keep, send, sym, turn, total):
    mine, yhi = place[AT_X] * YHI + place[AT_YHI], place[AT_YHI]
    build_symmetric(mine, place[AT_CORE], direct, direct_other, turned, turned_other, sym, turn)
    accumulate(total, jnp.dot(sym[...], c_ref[...], preferred_element_type=F32))

    @pl.when(last_step())
    def _():
        lanes = keep.shape[2]
        for x in range(X):
            keep[x] = total[:, aligned((x * YHI + yhi) * lanes, lanes)].astype(BF16)
            send[x] = total[:, aligned((x * YHI + 1 - yhi) * lanes, lanes)].astype(BF16)


def first_half(kernel, outs, place, direct, direct_other, turned, turned_other, picked, name):
    _, _, depth, rows, block = direct.shape
    size, width = picked.shape
    per_step = 2
    piece = pl.BlockSpec((per_step, YLO, depth, rows, block), lambda g, s: (g, 0, 0, 0, 0))
    return pl.pallas_call(
        kernel,
        out_shape=outs,
        grid_spec=pltpu.PrefetchScalarGridSpec(
            num_scalar_prefetch=1,
            grid=(BLOCKS // per_step,),
            in_specs=[piece, piece, piece, piece,
                      pl.BlockSpec((per_step * block, width), lambda g, s: (g, 0))],
            out_specs=[pl.BlockSpec(out.shape, lambda g, s, n=len(out.shape): (0,) * n) for out in outs],
            scratch_shapes=[pltpu.VMEM((depth * block, per_step * block), BF16),
                            pltpu.VMEM((depth * block, block), BF16),
                            pltpu.VMEM((depth * block, width), F32)],
        ),
        compiler_params=NARROW,
        name=name,
    )(place, direct, direct_other, turned, turned_other, picked)


def second_main_kernel(t_ref, c_ref, out_ref, left, total):
    per_step, depth, block, lanes = t_ref.shape
    rows = lanes // YLO
    for u in range(per_step):
        for k in range(depth):
            left[k * lanes:(k + 1) * lanes, u * block:(u + 1) * block] = transposed(t_ref[u, k])
    accumulate(total, jnp.dot(left[...], c_ref[...], preferred_element_type=F32))

    @pl.when(last_step())
    def _():
        for c in range(COLS):
            for y in range(YLO):
                for k in range(depth):
                    at = k * lanes + y * rows
                    out_ref[c, y, k] = total[at:at + rows, c * block:(c + 1) * block].astype(BF16)


def second_main(partial_value, orbitals):
    _, depth, block, lanes = partial_value.shape
    size = orbitals.shape[0]
    per_step = 2
    out = (COLS, YLO, depth, lanes // YLO, block)
    return pl.pallas_call(
        second_main_kernel,
        out_shape=array(*out),
        grid=(BLOCKS // per_step,),
        in_specs=[pl.BlockSpec((per_step, depth, block, lanes), lambda g: (g, 0, 0, 0)),
                  pl.BlockSpec((per_step * block, size), lambda g: (g, 0))],
        out_specs=pl.BlockSpec(out, lambda g: (0, 0, 0, 0, 0)),
        scratch_shapes=[pltpu.VMEM((depth * lanes, per_step * block), BF16),
                        pltpu.VMEM((depth * lanes, size), F32)],
        compiler_params=WIDE,
        name="second_main",
    )(partial_value, orbitals)


def second_side_kernel(place, t_ref, other_ref, c_ref, *rest):
    out_refs = rest[:RING]
    left, total, final = rest[RING:]
    per_step, block, lanes = t_ref.shape
    rows = lanes // YLO
    core = place[AT_CORE]
    for u in range(per_step):
        cols = slice(u * block, (u + 1) * block)
        own = transposed(t_ref[u])
        other = transposed(other_ref[u])
        for y in range(YLO):
            at = y * CORE * rows
            left[aligned(at + core * rows, rows), cols] = own[y * rows:(y + 1) * rows]
            left[aligned(at + (1 - core) * rows, rows), cols] = other[y * rows:(y + 1) * rows]
    accumulate(total, jnp.dot(left[...], c_ref[...], preferred_element_type=F32))

    @pl.when(last_step())
    def _():
        for part in range(total.shape[1] // block):
            cols = slice(part * block, (part + 1) * block)
            final[cols] = transposed(total[:, cols].astype(BF16))
        for a, b, out_ref in steps(out_refs):
            z_low, ylo = near(place, a, b)
            for z_high in range(RING):
                out_ref[z_high] = final[aligned(((z_high * 2 + z_low) * YLO + ylo) * rows, rows)]


def second_side(place, own, other, picked):
    _, block, lanes = own.shape
    size, width = picked.shape
    per_step = 2
    piece = pl.BlockSpec((per_step, block, lanes), lambda g, s: (g, 0, 0))
    out = array(RING, lanes // YLO, block)
    return pl.pallas_call(
        second_side_kernel,
        out_shape=[out] * RING,
        grid_spec=pltpu.PrefetchScalarGridSpec(
            num_scalar_prefetch=1,
            grid=(BLOCKS // per_step,),
            in_specs=[piece, piece, pl.BlockSpec((per_step * block, width), lambda g, s: (g, 0))],
            out_specs=[pl.BlockSpec(out.shape, lambda g, s: (0, 0, 0))] * RING,
            scratch_shapes=[pltpu.VMEM((block, per_step * block), BF16),
                            pltpu.VMEM((block, width), F32),
                            pltpu.VMEM((width, block), BF16)],
        ),
        compiler_params=NARROW,
        name="second_side",
    )(place, own, other, picked)


def steps(refs):
    return [(a, b, refs[2 * a + b]) for a in range(2) for b in range(2)]


def near(place, a, b):
    z_low, ylo = place[AT_Z] % 2, place[AT_YLO]
    return (1 - z_low if a else z_low), (1 - ylo if b else ylo)


def small_call(kernel, outs, name, place, *values):
    return pl.pallas_call(
        kernel,
        out_shape=outs,
        in_specs=[SCALARS] + [VMEM] * len(values),
        out_specs=jax.tree.map(lambda _: VMEM, outs),
        compiler_params=SMALL,
        name=name,
    )(place, *values)


def split_near_kernel(place, x_ref, *out_refs):
    for a, b, out_ref in steps(out_refs):
        z_low, ylo = near(place, a, b)
        for z_high in range(RING):
            out_ref[z_high] = x_ref[ylo * Z + z_high * 2 + z_low]


def split_near(place, half_panel, count):
    pairs, rows, block = half_panel.shape
    out = array(RING, rows, block)
    return pl.pallas_call(
        split_near_kernel,
        out_shape=[out] * RING,
        grid_spec=pltpu.PrefetchScalarGridSpec(
            num_scalar_prefetch=1,
            grid=(1,),
            in_specs=[pl.BlockSpec((count, rows, block), lambda g, s: (pairs // count - 1, 0, 0))],
            out_specs=[pl.BlockSpec(out.shape, lambda g, s: (0, 0, 0))] * RING,
        ),
        compiler_params=SMALL,
        name="split_near",
    )(place, half_panel)


def split_far_kernel(place, *refs):
    in_refs, out_refs = refs[:RING], refs[RING:]
    z_high = place[AT_Z] // 2
    for d in range(RING):
        for s in range(RING):
            out_refs[d][s] = in_refs[s][(z_high + d) % RING]


def collect_z_kernel(place, *refs):
    out_ref = refs[RING]
    z_high = place[AT_Z] // 2
    for d in range(RING):
        for a, b, s in steps(range(RING)):
            z_low, ylo = near(place, a, b)
            out_ref[(z_high + RING - d) % RING * 2 + z_low, ylo] = refs[d][s]


def finish_kernel(place, *refs):
    main_ref, out_ref = refs[RING:]
    main = main_ref.shape[0]
    z_high = place[AT_Z] // 2
    out_ref[:main] = main_ref[...]
    for d in range(RING):
        for a, b, s in steps(range(RING)):
            z_low, ylo = near(place, a, b)
            out_ref[main + ylo * Z + (z_high + RING - d) % RING * 2 + z_low] = refs[d][s]


def split_yhi_kernel(place, x_ref, keep, send):
    yhi = place[AT_YHI]
    for x in range(X):
        keep[x] = x_ref[x * YHI + yhi]
        send[x] = x_ref[x * YHI + 1 - yhi]


def split_x_kernel(place, keep, got, *out_refs):
    x, yhi = place[AT_X], place[AT_YHI]
    for d in range(RING):
        out_refs[d][yhi] = keep[(x + d) % X]
        out_refs[d][1 - yhi] = got[(x + d) % X]


def collect_x_kernel(place, *refs):
    out_ref = refs[RING]
    for d in range(RING):
        for y in range(YHI):
            out_ref[(place[AT_X] + RING - d) % X * YHI + y] = refs[d][y]


def swap(value, axis):
    return lax.ppermute(value, axis, [(0, 1), (1, 0)])


def near_exchange(parts):
    out = []
    for a, b, part in steps(parts):
        if a or b:
            pairs = [(z * YLO + y, (z ^ a) * YLO + (y ^ b)) for z in range(Z) for y in range(YLO)]
            part = lax.ppermute(part, ("z", "ylo"), pairs)
        out.append(part)
    return out


def far_exchange(place, parts):
    rows, block = parts[0].shape[1:]
    parts = small_call(split_far_kernel, [array(RING, rows, block)] * RING, "split_far", place, *parts)
    return [parts[0]] + [
        lax.ppermute(parts[d], "z", [(z, (z + 2 * d) % Z) for z in range(Z)]) for d in range(1, RING)
    ]


def x_exchange(place, keep, send):
    got = swap(send, "yhi")
    shape = keep.shape[1:]
    parts = small_call(split_x_kernel, [array(YHI, *shape)] * RING, "split_x", place, keep, got)
    parts = [parts[0]] + [
        lax.ppermute(parts[d], "x", [(x, (x + d) % X) for x in range(X)]) for d in range(1, RING)
    ]
    return small_call(collect_x_kernel, array(BLOCKS, *shape), "collect_x", place, *parts)


def per_device(half_panel, orbitals):
    pairs, rows, block = half_panel.shape
    side_pairs = Z * YLO
    main_pairs = pairs - side_pairs
    depth = main_pairs // (COLS * YLO)
    lanes = block // CORE
    place = jnp.stack([lax.axis_index(name) for name in ("z", "ylo", "core", "x", "yhi")]).astype(jnp.int32)

    def deep(value):
        return value.reshape(BLOCKS, YLO, 1, rows, block)

    together = lax.optimization_barrier

    with jax.named_scope("side_in"):
        near_parts = near_exchange(split_near(place, half_panel, side_pairs))
    picked = pick_columns(place, orbitals)
    own = half_panel[:main_pairs].reshape(COLS * YLO, depth, rows, block)
    own, near_parts, picked = together((own, near_parts, picked))

    with jax.named_scope("panels_in"):
        own = lax.all_to_all(own, PLANE, 0, 0, tiled=True)
        own = own.reshape(COLS, YLO, depth, rows, block)
    with jax.named_scope("side_in"):
        side_own = small_call(
            collect_z_kernel, array(Z, YLO, rows, block), "collect_z", place, *far_exchange(place, near_parts)
        )
    own, side_own, picked = together((own, side_own, picked))

    with jax.named_scope("mirror"):
        own_low = lax.all_to_all(own, "z", 0, 0, tiled=True)
    other = swap(own, "core")
    with jax.named_scope("side_mirror"):
        side_other = swap(side_own, "core")
        half = array(X, YLO, rows, block)
        keep, send = small_call(split_yhi_kernel, [half, half], "split_yhi", place, side_own)
        side_low = x_exchange(place, keep, send)
        side_other_low = swap(side_low, "core")
        half = array(X, block, lanes)
        keep, send = first_half(
            first_side_kernel, [half, half], place, deep(side_low), deep(side_other_low),
            deep(side_own), deep(side_other), picked, "first_side"
        )
    own_low, other, keep, send = together((own_low, other, keep, send))

    other_low = swap(own_low, "core")
    partial_value, = first_half(
        first_main_kernel, [array(Z, depth, block, lanes)], place, own, other, own_low, other_low,
        picked, "first_main"
    )
    with jax.named_scope("partial"):
        partial_value = lax.all_to_all(partial_value, "z", 0, 0, tiled=True)
    with jax.named_scope("side_partial"):
        side_partial = x_exchange(place, keep, send)
        near_parts = second_side(place, side_partial, swap(side_partial, "core"), picked)
    partial_value, near_parts = together((partial_value, near_parts))

    near_parts = near_exchange(near_parts)
    result = second_main(partial_value, orbitals)
    result, near_parts = together((result, near_parts))

    with jax.named_scope("panels_out"):
        result = result.reshape(COLS * YLO, depth, rows, block)
        result = lax.all_to_all(result, PLANE, 0, 0, tiled=True)
        result = result.reshape(main_pairs, rows, block)
    with jax.named_scope("side_out"):
        parts = far_exchange(place, near_parts)
    return small_call(finish_kernel, array(pairs, rows, block), "finish", place, *parts, result)


def solution(mesh):
    fine = Mesh(mesh.devices.reshape(Z, YLO, CORE, X, YHI), ("z", "ylo", "core", "x", "yhi"))
    spec = P(None, ("z", "ylo", "core"), ("x", "yhi"))
    return jax.shard_map(
        per_device, mesh=fine, in_specs=(spec, P()), out_specs=spec, check_vma=False
    )
```

time: 166 us -> 173 us (1.042)
  waiting for transfers between devices: 26.6 us -> 45.9 us
  starting transfers between devices: 90.4 us -> 73.1 us
  Pallas kernels: 40.5 us -> 45.7 us
  other arithmetic: 2.13 us -> 0 us
    ppermute x28 -> x18, starting transfers between devices: 61.7 us -> 38.2 us  [the longest x6 21.2 us: far_exchange(): lax.ppermute(parts[d], 'z', [(z, (z + 2 * d) % Z) for z in range(Z)])]
    ppermute x7, waiting for transfers between devices: 4.4 us -> 20 us  [swap(): return lax.ppermute(value, axis, [(0, 1), (1, 0)])]
    pallas_call x13 -> x15, Pallas kernels: 40.5 us -> 45.7 us  [the longest x2 15.2 us: first_half(): pl.pallas_call(kernel, out_shape=outs, grid_spec=pltpu.PrefetchScalarGrid...]
    ppermute x7, starting transfers between devices: 2.64 us -> 7 us  [swap(): return lax.ppermute(value, axis, [(0, 1), (1, 0)])]
    ppermute x28 -> x18, waiting for transfers between devices: 21.7 us -> 25.9 us  [the longest x6 16.3 us: far_exchange(): lax.ppermute(parts[d], 'z', [(z, (z + 2 * d) % Z) for z in range(Z)])]
    unnamed x22 -> x38, local copies, waits for them, and re-layouts: 2.04 us -> 4.28 us
    another operation x4 -> x0, other arithmetic: 2.13 us -> none  [scalars(): return jnp.stack(values).astype(jnp.int32)]
  transfers between devices with their start and end apart: 39 -> 29, of which waited for: 16 -> 16; matrix products, arithmetic and copies ran while one was open for 3% -> 1% of each run, Pallas kernels for 19% -> 20%
where the time goes in v4:
time: 173 us; the launch traced here: 172 us
  starting transfers between devices  73.1 us (42%)
  waiting for transfers between devices  45.9 us (27%)
  Pallas kernels  45.7 us (26%)
  local copies, waits for them, and re-layouts  6.67 us (4%)
    ppermute x6, starting transfers between devices, far_exchange(): lax.ppermute(parts[d], 'z', [(z, (z + 2 * d) % Z) for z in range(Z)])  21.2 us
    ppermute x7, waiting for transfers between devices, swap(): return lax.ppermute(value, axis, [(0, 1), (1, 0)])  20 us
    ppermute x6, waiting for transfers between devices, far_exchange(): lax.ppermute(parts[d], 'z', [(z, (z + 2 * d) % Z) for z in range(Z)])  16.3 us
    pallas_call x2, Pallas kernels, first_half(): pl.pallas_call(kernel, out_shape=outs, grid_spec=pltpu.PrefetchScalarGrid...  15.2 us
    ppermute x6, starting transfers between devices, x_exchange(): lax.ppermute(parts[d], 'x', [(x, (x + d) % X) for x in range(X)])  9.87 us
    ppermute x6, waiting for transfers between devices, x_exchange(): lax.ppermute(parts[d], 'x', [(x, (x + d) % X) for x in range(X)])  9.63 us
    pallas_call x1, Pallas kernels, pick_columns(): pl.pallas_call(pick_kernel, out_shape=array(size, size // CORE), grid_spe...  8.86 us
    all_to_all x1, starting transfers between devices, per_device(): partial_value = lax.all_to_all(partial_value, 'z', 0, 0, tiled=True)  7.86 us
  transfers between devices with their start and end apart: 29, of which 16 were waited for; matrix products, arithmetic and copies ran while one was open for 1% of the time, Pallas kernels for 20%

profile of v4, /device:TPU:2, one launch (start us, length us, event | category | flops | bytes accessed | tf_op | source)
XLA Modules:
  0.0 171.7 jit_solution(2440444344595281488)
XLA Ops:
  0.0 0.1 stack.23.place
  0.1 1.4 copy-done.1
  1.5 0.6 split_near.1
  2.1 1.7 collective-permute-start
  3.7 1.9 %collective-permute-start.1 = (bf16[4,64,256]{2,1,0:T(8,128)(2,1)S(1)}, bf16[4,64,256]{2,1,0:T(8,128)(2,1)S(1)}, u32[]{:S(2)}, u32[]{:S(2)}) collective-permute-start(bf16[4,64,256]{2,1,0:T(8,128)(2,1)S(1)} %get-tuple-element.58), channel_id=1, source_target_pairs={{0,32},{16,48},{32,0},{48,16},{64,96},{80,112},{96,64},{112,80},{1... | collective-permute-start | bytes 393224 | tf_op jit(solution)/shard_map/side_in/ppermute | solution.py:358
  5.7 2.3 %slice.3 = bf16[32,64,256]{2,1,0:T(8,128)(2,1)} slice(bf16[48,64,256]{2,1,0:T(8,128)(2,1)} %x_ref.1), slice={[0:32], [0:64], [0:256]} | slice | bytes 2097152 | tf_op jit(solution)/shard_map/slice | solution.py:397
  8.0 8.9 %pick_columns.1.c_ref = bf16[2048,1024]{1,0:T(8,128)(2,1)} custom-call(s32[5]{0:T(128)} %copy-done.6, bf16[2048,2048]{1,0:T(8,128)(2,1)} %c_ref.3), custom_call_target="tpu_custom_call" | custom-call | tf_op jit(solution)/shard_map/pick_columns/pallas_call | solution.py:59
  16.9 7.5 %all-to-all-start = ((bf16[16,2,64,256]{3,2,1,0:T(8,128)(2,1)}), bf16[16,2,64,256]{3,2,1,0:T(8,128)(2,1)}, u32[]{:S(2)}, u32[]{:S(2)}) async-start(bf16[16,2,64,256]{3,2,1,0:T(8,128)(2,1)} %bitcast.5), calls=%async_computation | async-start | bytes 2097152 | tf_op jit(solution)/shard_map/panels_in/all_to_all | solution.py:401
  24.3 0.6 copy-done.7
  24.9 0.6 split_far.2
  25.5 3.3 %collective-permute-start.3 = (bf16[4,64,256]{2,1,0:T(8,128)(2,1)S(1)}, bf16[4,64,256]{2,1,0:T(8,128)(2,1)S(1)}, u32[]{:S(2)}, u32[]{:S(2)}) collective-permute-start(bf16[4,64,256]{2,1,0:T(8,128)(2,1)S(1)} %get-tuple-element.66), channel_id=1, source_target_pairs={{0,64},{32,96},{64,128},{96,160},{128,192},{160,224},{192,0},{224,... | collective-permute-start | bytes 393224 | tf_op jit(solution)/shard_map/side_in/ppermute | solution.py:367
  28.9 5.4 %collective-permute-start.4 = (bf16[4,64,256]{2,1,0:T(8,128)(2,1)S(1)}, bf16[4,64,256]{2,1,0:T(8,128)(2,1)S(1)}, u32[]{:S(2)}, u32[]{:S(2)}) collective-permute-start(bf16[4,64,256]{2,1,0:T(8,128)(2,1)S(1)} %get-tuple-element.67), channel_id=1, source_target_pairs={{0,128},{32,160},{64,192},{96,224},{128,0},{160,32},{192,64},{224,... | collective-permute-start | bytes 393224 | tf_op jit(solution)/shard_map/side_in/ppermute | solution.py:367
  34.3 2.7 %collective-permute-start.5 = (bf16[4,64,256]{2,1,0:T(8,128)(2,1)S(1)}, bf16[4,64,256]{2,1,0:T(8,128)(2,1)S(1)}, u32[]{:S(2)}, u32[]{:S(2)}) collective-permute-start(bf16[4,64,256]{2,1,0:T(8,128)(2,1)S(1)} %get-tuple-element.68), channel_id=1, source_target_pairs={{0,192},{32,224},{64,0},{96,32},{128,64},{160,96},{192,128},{224,1... | collective-permute-start | bytes 393224 | tf_op jit(solution)/shard_map/side_in/ppermute | solution.py:367
  37.0 5.6 %collective-permute-done.4.refs_2_ = bf16[4,64,256]{2,1,0:T(8,128)(2,1)S(1)} collective-permute-done((bf16[4,64,256]{2,1,0:T(8,128)(2,1)S(1)}, bf16[4,64,256]{2,1,0:T(8,128)(2,1)S(1)}, u32[]{:S(2)}, u32[]{:S(2)}) %collective-permute-start.4) | collective-permute-done | bytes 131104 | tf_op jit(solution)/shard_map/side_in/ppermute | solution.py:367
  42.5 2.5 %collective-permute-done.5.refs_3_ = bf16[4,64,256]{2,1,0:T(8,128)(2,1)S(1)} collective-permute-done((bf16[4,64,256]{2,1,0:T(8,128)(2,1)S(1)}, bf16[4,64,256]{2,1,0:T(8,128)(2,1)S(1)}, u32[]{:S(2)}, u32[]{:S(2)}) %collective-permute-start.5) | collective-permute-done | bytes 131104 | tf_op jit(solution)/shard_map/side_in/ppermute | solution.py:367
  45.0 0.6 copy-done.8
  45.7 0.6 collect_z.1.x_ref
  46.3 5.5 %all-to-all-start.1 = ((bf16[8,2,2,64,256]{4,3,2,1,0:T(8,128)(2,1)}), bf16[8,2,2,64,256]{4,3,2,1,0:T(8,128)(2,1)S(1)}, u32[]{:S(2)}, u32[]{:S(2)}) async-start(bf16[8,2,2,64,256]{4,3,2,1,0:T(8,128)(2,1)} %bitcast.6.direct), calls=%async_computation.1 | async-start | bytes 2097152 | tf_op jit(solution)/shard_map/mirror/all_to_all | solution.py:410
  51.8 0.6 split_yhi.1
  52.4 3.1 %collective-permute-start.7 = (bf16[4,2,64,256]{3,2,1,0:T(8,128)(2,1)S(1)}, bf16[4,2,64,256]{3,2,1,0:T(8,128)(2,1)S(1)}, u32[]{:S(2)}, u32[]{:S(2)}) collective-permute-start(bf16[4,2,64,256]{3,2,1,0:T(8,128)(2,1)S(1)} %get-tuple-element.73), channel_id=1, source_target_pairs={{0,1},{1,0},{2,3},{3,2},{4,5},{5,4},{6,7},{7,6},{8,9},{9,8},{10,11... | collective-permute-start | bytes 786440 | tf_op jit(solution)/shard_map/side_mirror/ppermute | solution.py:350
  55.5 7.2 %collective-permute-done.7.got = bf16[4,2,64,256]{3,2,1,0:T(8,128)(2,1)S(1)} collective-permute-done((bf16[4,2,64,256]{3,2,1,0:T(8,128)(2,1)S(1)}, bf16[4,2,64,256]{3,2,1,0:T(8,128)(2,1)S(1)}, u32[]{:S(2)}, u32[]{:S(2)}) %collective-permute-start.7) | collective-permute-done | bytes 262176 | tf_op jit(solution)/shard_map/side_mirror/ppermute | solution.py:350
  62.7 0.6 split_x.2
  63.3 1.5 collective-permute-start.8
  64.8 1.0 collective-permute-start.9
  65.9 2.2 %collective-permute-start.10 = (bf16[2,2,64,256]{3,2,1,0:T(8,128)(2,1)S(1)}, bf16[2,2,64,256]{3,2,1,0:T(8,128)(2,1)S(1)}, u32[]{:S(2)}, u32[]{:S(2)}) collective-permute-start(bf16[2,2,64,256]{3,2,1,0:T(8,128)(2,1)S(1)} %get-tuple-element.77), channel_id=1, source_target_pairs={{0,6},{2,0},{4,2},{6,4},{1,7},{3,1},{5,3},{7,5},{8,14},{10,8},{12,... | collective-permute-start | bytes 393224 | tf_op jit(solution)/shard_map/side_mirror/ppermute | solution.py:376
  68.1 0.8 collective-permute-done.8.refs_1_
  68.9 3.8 %collective-permute-done.9.refs_2_ = bf16[2,2,64,256]{3,2,1,0:T(8,128)(2,1)S(1)} collective-permute-done((bf16[2,2,64,256]{3,2,1,0:T(8,128)(2,1)S(1)}, bf16[2,2,64,256]{3,2,1,0:T(8,128)(2,1)S(1)}, u32[]{:S(2)}, u32[]{:S(2)}) %collective-permute-start.9) | collective-permute-done | bytes 131104 | tf_op jit(solution)/shard_map/side_mirror/ppermute | solution.py:376
  72.7 0.6 collective-permute-done.10.refs_3_
  73.3 0.6 collect_x.2
  73.9 0.1 collective-permute-start.11
  74.0 1.9 %collective-permute-done.11 = bf16[8,2,64,256]{3,2,1,0:T(8,128)(2,1)S(1)} collective-permute-done((bf16[8,2,64,256]{3,2,1,0:T(8,128)(2,1)S(1)}, bf16[8,2,64,256]{3,2,1,0:T(8,128)(2,1)S(1)}, u32[]{:S(2)}, u32[]{:S(2)}) %collective-permute-start.11) | collective-permute-done | bytes 524320 | tf_op jit(solution)/shard_map/side_mirror/ppermute | solution.py:350
  75.9 0.8 copy-done.16
  76.7 7.0 %first_side.1 = (bf16[4,256,128]{2,1,0:T(8,128)(2,1)}, bf16[4,256,128]{2,1,0:T(8,128)(2,1)}) custom-call(s32[5]{0:T(128)} %copy-done.6, bf16[8,2,1,64,256]{4,3,2,1,0:T(8,128)(2,1)} %bitcast.15, bf16[8,2,1,64,256]{4,3,2,1,0:T(8,128)(2,1)} %bitcast.18, bf16[8,2,1,64,256]{4,3,2,1,0:T(8,128)(2,1)} %bitcast.13, bf16[8,2,1,64,256]{4,3,2,1,0:T(8,128)(2,1)} %bitcast.17, ...), custom_call_target="tpu_custom_call" | custom-call | tf_op jit(solution)/shard_map/side_mirror/first_side/pallas_call | solution.py:152
  83.7 0.4 collective-permute-start.13
  84.1 2.7 %collective-permute-done.13.turned_other = bf16[8,2,2,64,256]{4,3,2,1,0:T(8,128)(2,1)} collective-permute-done((bf16[8,2,2,64,256]{4,3,2,1,0:T(8,128)(2,1)S(1)}, bf16[8,2,2,64,256]{4,3,2,1,0:T(8,128)(2,1)}, u32[]{:S(2)}, u32[]{:S(2)}) %collective-permute-start.13) | collective-permute-done | bytes 1048608 | tf_op jit(solution)/shard_map/ppermute | solution.py:350
  86.8 8.1 %first_main.1 = bf16[8,2,256,128]{3,2,1,0:T(8,128)(2,1)} custom-call(s32[5]{0:T(128)} %copy-done.6, bf16[8,2,2,64,256]{4,3,2,1,0:T(8,128)(2,1)} %bitcast.6.direct, bf16[8,2,2,64,256]{4,3,2,1,0:T(8,128)(2,1)} %copy-done.14, bf16[8,2,2,64,256]{4,3,2,1,0:T(8,128)(2,1)} %copy-done.12, bf16[8,2,2,64,256]{4,3,2,1,0:T(8,128)(2,1)} %collective-permute-done.13.turned_other, ...), custom_call_target="tpu_custom_call" | custom-call | tf_op jit(solution)/shard_map/first_main/pallas_call | solution.py:152
  94.9 7.9 %all-to-all-start.2 = ((bf16[8,2,256,128]{3,2,1,0:T(8,128)(2,1)}), bf16[8,2,256,128]{3,2,1,0:T(8,128)(2,1)S(1)}, u32[]{:S(2)}, u32[]{:S(2)}) async-start(bf16[8,2,256,128]{3,2,1,0:T(8,128)(2,1)} %first_main.1), calls=%async_computation.2 | async-start | bytes 2097152 | tf_op jit(solution)/shard_map/partial/all_to_all | solution.py:431
  102.8 3.4 %collective-permute-start.14 = (bf16[4,256,128]{2,1,0:T(8,128)(2,1)S(1)}, bf16[4,256,128]{2,1,0:T(8,128)(2,1)S(1)}, u32[]{:S(2)}, u32[]{:S(2)}) collective-permute-start(bf16[4,256,128]{2,1,0:T(8,128)(2,1)S(1)} %copy-done.18), channel_id=1, source_target_pairs={{0,1},{1,0},{2,3},{3,2},{4,5},{5,4},{6,7},{7,6},{8,9},{9,8},{10,11... | collective-permute-start | bytes 786440 | tf_op jit(solution)/shard_map/side_partial/ppermute | solution.py:350
  106.2 6.3 %collective-permute-done.14.got = bf16[4,256,128]{2,1,0:T(8,128)(2,1)S(1)} collective-permute-done((bf16[4,256,128]{2,1,0:T(8,128)(2,1)S(1)}, bf16[4,256,128]{2,1,0:T(8,128)(2,1)S(1)}, u32[]{:S(2)}, u32[]{:S(2)}) %collective-permute-start.14) | collective-permute-done | bytes 262176 | tf_op jit(solution)/shard_map/side_partial/ppermute | solution.py:350
  112.5 0.6 split_x.3
  113.1 1.6 collective-permute-start.15
  114.7 1.0 collective-permute-start.16
  115.7 2.5 %collective-permute-start.17 = (bf16[2,256,128]{2,1,0:T(8,128)(2,1)S(1)}, bf16[2,256,128]{2,1,0:T(8,128)(2,1)S(1)}, u32[]{:S(2)}, u32[]{:S(2)}) collective-permute-start(bf16[2,256,128]{2,1,0:T(8,128)(2,1)S(1)} %get-tuple-element.88), channel_id=1, source_target_pairs={{0,6},{2,0},{4,2},{6,4},{1,7},{3,1},{5,3},{7,5},{8,14},{10,8},{12,... | collective-permute-start | bytes 393224 | tf_op jit(solution)/shard_map/side_partial/ppermute | solution.py:376
  118.2 0.6 collective-permute-done.15.refs_1_
  118.8 3.1 %collective-permute-done.16.refs_2_ = bf16[2,256,128]{2,1,0:T(8,128)(2,1)S(1)} collective-permute-done((bf16[2,256,128]{2,1,0:T(8,128)(2,1)S(1)}, bf16[2,256,128]{2,1,0:T(8,128)(2,1)S(1)}, u32[]{:S(2)}, u32[]{:S(2)}) %collective-permute-start.16) | collective-permute-done | bytes 131104 | tf_op jit(solution)/shard_map/side_partial/ppermute | solution.py:376
  121.9 0.8 collective-permute-done.17.refs_3_
  122.7 0.6 collect_x.3.t_ref
  123.3 0.1 collective-permute-start.18
  123.4 1.9 %collective-permute-done.18.other_ref = bf16[8,256,128]{2,1,0:T(8,128)(2,1)S(1)} collective-permute-done((bf16[8,256,128]{2,1,0:T(8,128)(2,1)S(1)}, bf16[8,256,128]{2,1,0:T(8,128)(2,1)S(1)}, u32[]{:S(2)}, u32[]{:S(2)}) %collective-permute-start.18) | collective-permute-done | bytes 524320 | tf_op jit(solution)/shard_map/side_partial/ppermute | solution.py:350
  125.3 0.8 copy-done.17
  126.1 6.9 %second_side.1 = (bf16[4,64,256]{2,1,0:T(8,128)(2,1)}, bf16[4,64,256]{2,1,0:T(8,128)(2,1)}, bf16[4,64,256]{2,1,0:T(8,128)(2,1)}, bf16[4,64,256]{2,1,0:T(8,128)(2,1)}) custom-call(s32[5]{0:T(128)} %copy-done.6, bf16[8,256,128]{2,1,0:T(8,128)(2,1)} %copy-done.3, bf16[8,256,128]{2,1,0:T(8,128)(2,1)} %copy-done.17, bf16[2048,1024]{1,0:T(8,128)(2,1)} %pick_columns.1.c_ref), custom_call_target="tpu_custom_call" | custom-call | tf_op jit(solution)/shard_map/side_partial/second_side/pallas_call | solution.py:239
  132.9 1.5 collective-permute-start.19
  134.5 1.3 collective-permute-start.20
  135.8 0.7 collective-permute-start.21
  136.5 7.7 %second_main.1 = bf16[8,2,2,64,256]{4,3,2,1,0:T(8,128)(2,1)} custom-call(bf16[8,2,256,128]{3,2,1,0:T(8,128)(2,1)} %copy-done.13, bf16[2048,2048]{1,0:T(8,128)(2,1)} %c_ref.3), custom_call_target="tpu_custom_call" | custom-call | tf_op jit(solution)/shard_map/second_main/pallas_call | solution.py:192
  144.3 7.0 %all-to-all-start.3 = ((bf16[16,2,64,256]{3,2,1,0:T(8,128)(2,1)}), bf16[16,2,64,256]{3,2,1,0:T(8,128)(2,1)S(1)}, u32[]{:S(2)}, u32[]{:S(2)}) async-start(bf16[16,2,64,256]{3,2,1,0:T(8,128)(2,1)} %bitcast.16), calls=%async_computation.3 | async-start | bytes 2097152 | tf_op jit(solution)/shard_map/panels_out/all_to_all | solution.py:443
  151.3 0.6 split_far.3
  151.9 2.6 %collective-permute-start.22 = (bf16[4,64,256]{2,1,0:T(8,128)(2,1)S(1)}, bf16[4,64,256]{2,1,0:T(8,128)(2,1)S(1)}, u32[]{:S(2)}, u32[]{:S(2)}) collective-permute-start(bf16[4,64,256]{2,1,0:T(8,128)(2,1)S(1)} %get-tuple-element.103), channel_id=1, source_target_pairs={{0,64},{32,96},{64,128},{96,160},{128,192},{160,224},{192,0},{224,... | collective-permute-start | bytes 393224 | tf_op jit(solution)/shard_map/side_out/ppermute | solution.py:367
  154.5 3.6 %collective-permute-start.23 = (bf16[4,64,256]{2,1,0:T(8,128)(2,1)S(1)}, bf16[4,64,256]{2,1,0:T(8,128)(2,1)S(1)}, u32[]{:S(2)}, u32[]{:S(2)}) collective-permute-start(bf16[4,64,256]{2,1,0:T(8,128)(2,1)S(1)} %get-tuple-element.104), channel_id=1, source_target_pairs={{0,128},{32,160},{64,192},{96,224},{128,0},{160,32},{192,64},{224,... | collective-permute-start | bytes 393224 | tf_op jit(solution)/shard_map/side_out/ppermute | solution.py:367
  158.1 3.6 %collective-permute-start.24 = (bf16[4,64,256]{2,1,0:T(8,128)(2,1)S(1)}, bf16[4,64,256]{2,1,0:T(8,128)(2,1)S(1)}, u32[]{:S(2)}, u32[]{:S(2)}) collective-permute-start(bf16[4,64,256]{2,1,0:T(8,128)(2,1)S(1)} %get-tuple-element.105), channel_id=1, source_target_pairs={{0,192},{32,224},{64,0},{96,32},{128,64},{160,96},{192,128},{224,1... | collective-permute-start | bytes 393224 | tf_op jit(solution)/shard_map/side_out/ppermute | solution.py:367
  161.7 0.3 collective-permute-done.22.refs_1_
  162.0 4.7 %collective-permute-done.23.refs_2_ = bf16[4,64,256]{2,1,0:T(8,128)(2,1)S(1)} collective-permute-done((bf16[4,64,256]{2,1,0:T(8,128)(2,1)S(1)}, bf16[4,64,256]{2,1,0:T(8,128)(2,1)S(1)}, u32[]{:S(2)}, u32[]{:S(2)}) %collective-permute-start.23) | collective-permute-done | bytes 131104 | tf_op jit(solution)/shard_map/side_out/ppermute | solution.py:367
  166.7 3.2 %collective-permute-done.24.refs_3_ = bf16[4,64,256]{2,1,0:T(8,128)(2,1)S(1)} collective-permute-done((bf16[4,64,256]{2,1,0:T(8,128)(2,1)S(1)}, bf16[4,64,256]{2,1,0:T(8,128)(2,1)S(1)}, u32[]{:S(2)}, u32[]{:S(2)}) %collective-permute-start.24) | collective-permute-done | bytes 131104 | tf_op jit(solution)/shard_map/side_out/ppermute | solution.py:367
  169.9 1.8 %finish.1 = bf16[48,64,256]{2,1,0:T(8,128)(2,1)} custom-call(s32[5]{0:T(128)S(1)} %copy-done.11, bf16[4,64,256]{2,1,0:T(8,128)(2,1)S(1)} %get-tuple-element.102.refs_0_, bf16[4,64,256]{2,1,0:T(8,128)(2,1)S(1)} %collective-permute-done.22.refs_1_, bf16[4,64,256]{2,1,0:T(8,128)(2,1)S(1)} %collective-permute-done.23.refs_2_, ...), custom_call_target="tpu_custom_call" | custom-call | tf_op jit(solution)/shard_map/finish/pallas_call | solution.py:266
  (49 shorter events, 0.1 us)
Async XLA Ops:
  0.1 1.4 copy-start.1
  1.5 6.5 %copy-start.6 = (s32[5]{0:T(128)}, s32[5]{0:T(128)S(1)}, u32[]{:S(2)}) copy-start(s32[5]{0:T(128)S(1)} %stack.23.place) | copy-start | bytes 64
  2.1 14.8 %collective-permute-start = (bf16[4,64,256]{2,1,0:T(8,128)(2,1)S(1)}, bf16[4,64,256]{2,1,0:T(8,128)(2,1)S(1)}, u32[]{:S(2)}, u32[]{:S(2)}) collective-permute-start(bf16[4,64,256]{2,1,0:T(8,128)(2,1)S(1)} %get-tuple-element.57), channel_id=1, source_target_pairs={{0,16},{16,0},{32,48},{48,32},{64,80},{80,64},{96,112},{112,96},{1... | collective-permute-start | bytes 393224 | tf_op jit(solution)/shard_map/side_in/ppermute | solution.py:358
  3.7 13.1 %collective-permute-start.1 = (bf16[4,64,256]{2,1,0:T(8,128)(2,1)S(1)}, bf16[4,64,256]{2,1,0:T(8,128)(2,1)S(1)}, u32[]{:S(2)}, u32[]{:S(2)}) collective-permute-start(bf16[4,64,256]{2,1,0:T(8,128)(2,1)S(1)} %get-tuple-element.58), channel_id=1, source_target_pairs={{0,32},{16,48},{32,0},{48,16},{64,96},{80,112},{96,64},{112,80},{1... | collective-permute-start | bytes 393224 | tf_op jit(solution)/shard_map/side_in/ppermute | solution.py:358
  5.7 11.2 %collective-permute-start.2 = (bf16[4,64,256]{2,1,0:T(8,128)(2,1)S(1)}, bf16[4,64,256]{2,1,0:T(8,128)(2,1)S(1)}, u32[]{:S(2)}, u32[]{:S(2)}) collective-permute-start(bf16[4,64,256]{2,1,0:T(8,128)(2,1)S(1)} %get-tuple-element.59), channel_id=1, source_target_pairs={{0,48},{16,32},{32,16},{48,0},{64,112},{80,96},{96,80},{112,64},{1... | collective-permute-start | bytes 393224 | tf_op jit(solution)/shard_map/side_in/ppermute | solution.py:358
  16.8 35.0 %copy-start.9 = (s32[5]{0:T(128)S(1)}, s32[5]{0:T(128)}, u32[]{:S(2)}) copy-start(s32[5]{0:T(128)} %copy-done.6) | copy-start | bytes 64
  16.9 29.4 %all-to-all-start = ((bf16[16,2,64,256]{3,2,1,0:T(8,128)(2,1)}), bf16[16,2,64,256]{3,2,1,0:T(8,128)(2,1)}, u32[]{:S(2)}, u32[]{:S(2)}) async-start(bf16[16,2,64,256]{3,2,1,0:T(8,128)(2,1)} %bitcast.5), calls=%async_computation | async-start | bytes 2097152 | tf_op jit(solution)/shard_map/panels_in/all_to_all | solution.py:401
  24.3 0.6 copy-start.7
  25.5 11.4 %collective-permute-start.3 = (bf16[4,64,256]{2,1,0:T(8,128)(2,1)S(1)}, bf16[4,64,256]{2,1,0:T(8,128)(2,1)S(1)}, u32[]{:S(2)}, u32[]{:S(2)}) collective-permute-start(bf16[4,64,256]{2,1,0:T(8,128)(2,1)S(1)} %get-tuple-element.66), channel_id=1, source_target_pairs={{0,64},{32,96},{64,128},{96,160},{128,192},{160,224},{192,0},{224,... | collective-permute-start | bytes 393224 | tf_op jit(solution)/shard_map/side_in/ppermute | solution.py:367
  28.9 13.6 %collective-permute-start.4 = (bf16[4,64,256]{2,1,0:T(8,128)(2,1)S(1)}, bf16[4,64,256]{2,1,0:T(8,128)(2,1)S(1)}, u32[]{:S(2)}, u32[]{:S(2)}) collective-permute-start(bf16[4,64,256]{2,1,0:T(8,128)(2,1)S(1)} %get-tuple-element.67), channel_id=1, source_target_pairs={{0,128},{32,160},{64,192},{96,224},{128,0},{160,32},{192,64},{224,... | collective-permute-start | bytes 393224 | tf_op jit(solution)/shard_map/side_in/ppermute | solution.py:367
  34.3 10.8 %collective-permute-start.5 = (bf16[4,64,256]{2,1,0:T(8,128)(2,1)S(1)}, bf16[4,64,256]{2,1,0:T(8,128)(2,1)S(1)}, u32[]{:S(2)}, u32[]{:S(2)}) collective-permute-start(bf16[4,64,256]{2,1,0:T(8,128)(2,1)S(1)} %get-tuple-element.68), channel_id=1, source_target_pairs={{0,192},{32,224},{64,0},{96,32},{128,64},{160,96},{192,128},{224,1... | collective-permute-start | bytes 393224 | tf_op jit(solution)/shard_map/side_in/ppermute | solution.py:367
  45.0 0.6 copy-start.8
  46.3 30.4 %copy-start = (bf16[8,2,64,256]{3,2,1,0:T(8,128)(2,1)}, bf16[8,2,64,256]{3,2,1,0:T(8,128)(2,1)S(1)}, u32[]{:S(2)}) copy-start(bf16[8,2,64,256]{3,2,1,0:T(8,128)(2,1)S(1)} %collect_z.1.x_ref) | copy-start | bytes 1572868
  46.3 37.4 %all-to-all-start.1 = ((bf16[8,2,2,64,256]{4,3,2,1,0:T(8,128)(2,1)}), bf16[8,2,2,64,256]{4,3,2,1,0:T(8,128)(2,1)S(1)}, u32[]{:S(2)}, u32[]{:S(2)}) async-start(bf16[8,2,2,64,256]{4,3,2,1,0:T(8,128)(2,1)} %bitcast.6.direct), calls=%async_computation.1 | async-start | bytes 2097152 | tf_op jit(solution)/shard_map/mirror/all_to_all | solution.py:410
  51.8 31.9 %collective-permute-start.6 = (bf16[8,2,2,64,256]{4,3,2,1,0:T(8,128)(2,1)}, bf16[8,2,2,64,256]{4,3,2,1,0:T(8,128)(2,1)S(1)}, u32[]{:S(2)}, u32[]{:S(2)}) collective-permute-start(bf16[8,2,2,64,256]{4,3,2,1,0:T(8,128)(2,1)} %bitcast.6.direct), channel_id=1, source_target_pairs={{0,8},{8,0},{1,9},{9,1},{2,10},{10,2},{3,11},{11,3},{4,12},{12,4},... | collective-permute-start | bytes 3145736 | tf_op jit(solution)/shard_map/ppermute | solution.py:350
  52.4 10.3 %collective-permute-start.7 = (bf16[4,2,64,256]{3,2,1,0:T(8,128)(2,1)S(1)}, bf16[4,2,64,256]{3,2,1,0:T(8,128)(2,1)S(1)}, u32[]{:S(2)}, u32[]{:S(2)}) collective-permute-start(bf16[4,2,64,256]{3,2,1,0:T(8,128)(2,1)S(1)} %get-tuple-element.73), channel_id=1, source_target_pairs={{0,1},{1,0},{2,3},{3,2},{4,5},{5,4},{6,7},{7,6},{8,9},{9,8},{10,11... | collective-permute-start | bytes 786440 | tf_op jit(solution)/shard_map/side_mirror/ppermute | solution.py:350
  63.3 5.6 %collective-permute-start.8 = (bf16[2,2,64,256]{3,2,1,0:T(8,128)(2,1)S(1)}, bf16[2,2,64,256]{3,2,1,0:T(8,128)(2,1)S(1)}, u32[]{:S(2)}, u32[]{:S(2)}) collective-permute-start(bf16[2,2,64,256]{3,2,1,0:T(8,128)(2,1)S(1)} %get-tuple-element.75), channel_id=1, source_target_pairs={{0,2},{2,4},{4,6},{6,0},{1,3},{3,5},{5,7},{7,1},{8,10},{10,12},{12... | collective-permute-start | bytes 393224 | tf_op jit(solution)/shard_map/side_mirror/ppermute | solution.py:376
  64.8 7.8 %collective-permute-start.9 = (bf16[2,2,64,256]{3,2,1,0:T(8,128)(2,1)S(1)}, bf16[2,2,64,256]{3,2,1,0:T(8,128)(2,1)S(1)}, u32[]{:S(2)}, u32[]{:S(2)}) collective-permute-start(bf16[2,2,64,256]{3,2,1,0:T(8,128)(2,1)S(1)} %get-tuple-element.76), channel_id=1, source_target_pairs={{0,4},{2,6},{4,0},{6,2},{1,5},{3,7},{5,1},{7,3},{8,12},{10,14},{12... | collective-permute-start | bytes 393224 | tf_op jit(solution)/shard_map/side_mirror/ppermute | solution.py:376
  65.9 7.4 %collective-permute-start.10 = (bf16[2,2,64,256]{3,2,1,0:T(8,128)(2,1)S(1)}, bf16[2,2,64,256]{3,2,1,0:T(8,128)(2,1)S(1)}, u32[]{:S(2)}, u32[]{:S(2)}) collective-permute-start(bf16[2,2,64,256]{3,2,1,0:T(8,128)(2,1)S(1)} %get-tuple-element.77), channel_id=1, source_target_pairs={{0,6},{2,0},{4,2},{6,4},{1,7},{3,1},{5,3},{7,5},{8,14},{10,8},{12,... | collective-permute-start | bytes 393224 | tf_op jit(solution)/shard_map/side_mirror/ppermute | solution.py:376
  68.1 5.9 %collective-permute-start.12 = (bf16[8,2,64,256]{3,2,1,0:T(8,128)(2,1)S(1)}, bf16[8,2,64,256]{3,2,1,0:T(8,128)(2,1)S(1)}, u32[]{:S(2)}, u32[]{:S(2)}) collective-permute-start(bf16[8,2,64,256]{3,2,1,0:T(8,128)(2,1)S(1)} %collect_z.1.x_ref), channel_id=1, source_target_pairs={{0,8},{8,0},{1,9},{9,1},{2,10},{10,2},{3,11},{11,3},{4,12},{12,4},... | collective-permute-start | bytes 1572872 | tf_op jit(solution)/shard_map/side_mirror/ppermute | solution.py:350
  73.8 2.8 %copy-start.2 = (bf16[8,2,64,256]{3,2,1,0:T(8,128)(2,1)}, bf16[8,2,64,256]{3,2,1,0:T(8,128)(2,1)S(1)}, u32[]{:S(2)}) copy-start(bf16[8,2,64,256]{3,2,1,0:T(8,128)(2,1)S(1)} %collect_x.2) | copy-start | bytes 1572868
  73.9 2.0 %collective-permute-start.11 = (bf16[8,2,64,256]{3,2,1,0:T(8,128)(2,1)S(1)}, bf16[8,2,64,256]{3,2,1,0:T(8,128)(2,1)S(1)}, u32[]{:S(2)}, u32[]{:S(2)}) collective-permute-start(bf16[8,2,64,256]{3,2,1,0:T(8,128)(2,1)S(1)} %collect_x.2), channel_id=1, source_target_pairs={{0,8},{8,0},{1,9},{9,1},{2,10},{10,2},{3,11},{11,3},{4,12},{12,4},... | collective-permute-start | bytes 1572872 | tf_op jit(solution)/shard_map/side_mirror/ppermute | solution.py:350
  74.0 2.7 %copy-start.15 = (bf16[8,2,64,256]{3,2,1,0:T(8,128)(2,1)}, bf16[8,2,64,256]{3,2,1,0:T(8,128)(2,1)S(1)}, u32[]{:S(2)}) copy-start(bf16[8,2,64,256]{3,2,1,0:T(8,128)(2,1)S(1)} %collective-permute-done.12) | copy-start | bytes 1572868
  75.9 0.8 copy-start.16
  83.7 3.1 %copy-start.14 = (bf16[8,2,2,64,256]{4,3,2,1,0:T(8,128)(2,1)}, bf16[8,2,2,64,256]{4,3,2,1,0:T(8,128)(2,1)S(1)}, u32[]{:S(2)}) copy-start(bf16[8,2,2,64,256]{4,3,2,1,0:T(8,128)(2,1)S(1)} %collective-permute-done.6.direct_other) | copy-start | bytes 3145732
  83.7 3.1 %copy-start.12 = (bf16[8,2,2,64,256]{4,3,2,1,0:T(8,128)(2,1)}, bf16[8,2,2,64,256]{4,3,2,1,0:T(8,128)(2,1)S(1)}, u32[]{:S(2)}) copy-start(bf16[8,2,2,64,256]{4,3,2,1,0:T(8,128)(2,1)S(1)} %all-to-all-done.1.turned) | copy-start | bytes 3145732
  83.7 19.1 %copy-start.18 = (bf16[4,256,128]{2,1,0:T(8,128)(2,1)S(1)}, bf16[4,256,128]{2,1,0:T(8,128)(2,1)}, u32[]{:S(2)}) copy-start(bf16[4,256,128]{2,1,0:T(8,128)(2,1)} %get-tuple-element.84) | copy-start | bytes 786436
  83.7 28.8 %copy-start.4 = (bf16[4,256,128]{2,1,0:T(8,128)(2,1)S(1)}, bf16[4,256,128]{2,1,0:T(8,128)(2,1)}, u32[]{:S(2)}) copy-start(bf16[4,256,128]{2,1,0:T(8,128)(2,1)} %get-tuple-element.83.keep) | copy-start | bytes 786436
  83.7 28.8 %copy-start.10 = (s32[5]{0:T(128)S(1)}, s32[5]{0:T(128)}, u32[]{:S(2)}) copy-start(s32[5]{0:T(128)} %copy-done.6) | copy-start | bytes 64
  83.7 3.1 %collective-permute-start.13 = (bf16[8,2,2,64,256]{4,3,2,1,0:T(8,128)(2,1)S(1)}, bf16[8,2,2,64,256]{4,3,2,1,0:T(8,128)(2,1)}, u32[]{:S(2)}, u32[]{:S(2)}) collective-permute-start(bf16[8,2,2,64,256]{4,3,2,1,0:T(8,128)(2,1)S(1)} %all-to-all-done.1.turned), channel_id=1, source_target_pairs={{0,8},{8,0},{1,9},{9,1},{2,10},{10,2},{3,11},{11,3},{4,12},{12,4},... | collective-permute-start | bytes 3145736 | tf_op jit(solution)/shard_map/ppermute | solution.py:350
  94.9 38.0 %all-to-all-start.2 = ((bf16[8,2,256,128]{3,2,1,0:T(8,128)(2,1)}), bf16[8,2,256,128]{3,2,1,0:T(8,128)(2,1)S(1)}, u32[]{:S(2)}, u32[]{:S(2)}) async-start(bf16[8,2,256,128]{3,2,1,0:T(8,128)(2,1)} %first_main.1), calls=%async_computation.2 | async-start | bytes 2097152 | tf_op jit(solution)/shard_map/partial/all_to_all | solution.py:431
  102.8 9.7 %collective-permute-start.14 = (bf16[4,256,128]{2,1,0:T(8,128)(2,1)S(1)}, bf16[4,256,128]{2,1,0:T(8,128)(2,1)S(1)}, u32[]{:S(2)}, u32[]{:S(2)}) collective-permute-start(bf16[4,256,128]{2,1,0:T(8,128)(2,1)S(1)} %copy-done.18), channel_id=1, source_target_pairs={{0,1},{1,0},{2,3},{3,2},{4,5},{5,4},{6,7},{7,6},{8,9},{9,8},{10,11... | collective-permute-start | bytes 786440 | tf_op jit(solution)/shard_map/side_partial/ppermute | solution.py:350
  113.1 5.7 %collective-permute-start.15 = (bf16[2,256,128]{2,1,0:T(8,128)(2,1)S(1)}, bf16[2,256,128]{2,1,0:T(8,128)(2,1)S(1)}, u32[]{:S(2)}, u32[]{:S(2)}) collective-permute-start(bf16[2,256,128]{2,1,0:T(8,128)(2,1)S(1)} %get-tuple-element.86), channel_id=1, source_target_pairs={{0,2},{2,4},{4,6},{6,0},{1,3},{3,5},{5,7},{7,1},{8,10},{10,12},{12... | collective-permute-start | bytes 393224 | tf_op jit(solution)/shard_map/side_partial/ppermute | solution.py:376
  114.7 7.2 %collective-permute-start.16 = (bf16[2,256,128]{2,1,0:T(8,128)(2,1)S(1)}, bf16[2,256,128]{2,1,0:T(8,128)(2,1)S(1)}, u32[]{:S(2)}, u32[]{:S(2)}) collective-permute-start(bf16[2,256,128]{2,1,0:T(8,128)(2,1)S(1)} %get-tuple-element.87), channel_id=1, source_target_pairs={{0,4},{2,6},{4,0},{6,2},{1,5},{3,7},{5,1},{7,3},{8,12},{10,14},{12... | collective-permute-start | bytes 393224 | tf_op jit(solution)/shard_map/side_partial/ppermute | solution.py:376
  115.7 7.0 %collective-permute-start.17 = (bf16[2,256,128]{2,1,0:T(8,128)(2,1)S(1)}, bf16[2,256,128]{2,1,0:T(8,128)(2,1)S(1)}, u32[]{:S(2)}, u32[]{:S(2)}) collective-permute-start(bf16[2,256,128]{2,1,0:T(8,128)(2,1)S(1)} %get-tuple-element.88), channel_id=1, source_target_pairs={{0,6},{2,0},{4,2},{6,4},{1,7},{3,1},{5,3},{7,5},{8,14},{10,8},{12,... | collective-permute-start | bytes 393224 | tf_op jit(solution)/shard_map/side_partial/ppermute | solution.py:376
  123.3 2.0 %copy-start.3 = (bf16[8,256,128]{2,1,0:T(8,128)(2,1)}, bf16[8,256,128]{2,1,0:T(8,128)(2,1)S(1)}, u32[]{:S(2)}) copy-start(bf16[8,256,128]{2,1,0:T(8,128)(2,1)S(1)} %collect_x.3.t_ref) | copy-start | bytes 1572868
  123.3 2.0 %collective-permute-start.18 = (bf16[8,256,128]{2,1,0:T(8,128)(2,1)S(1)}, bf16[8,256,128]{2,1,0:T(8,128)(2,1)S(1)}, u32[]{:S(2)}, u32[]{:S(2)}) collective-permute-start(bf16[8,256,128]{2,1,0:T(8,128)(2,1)S(1)} %collect_x.3.t_ref), channel_id=1, source_target_pairs={{0,8},{8,0},{1,9},{9,1},{2,10},{10,2},{3,11},{11,3},{4,12},{12,4},... | collective-permute-start | bytes 1572872 | tf_op jit(solution)/shard_map/side_partial/ppermute | solution.py:350
  125.3 0.8 copy-start.17
  132.9 3.6 %copy-start.13 = (bf16[8,2,256,128]{3,2,1,0:T(8,128)(2,1)}, bf16[8,2,256,128]{3,2,1,0:T(8,128)(2,1)S(1)}, u32[]{:S(2)}) copy-start(bf16[8,2,256,128]{3,2,1,0:T(8,128)(2,1)S(1)} %all-to-all-done.2.t_ref) | copy-start | bytes 3145732
  132.9 18.4 %copy-start.5 = (bf16[4,64,256]{2,1,0:T(8,128)(2,1)S(1)}, bf16[4,64,256]{2,1,0:T(8,128)(2,1)}, u32[]{:S(2)}) copy-start(bf16[4,64,256]{2,1,0:T(8,128)(2,1)} %get-tuple-element.98.refs_0_) | copy-start | bytes 393220
  132.9 18.4 %copy-start.11 = (s32[5]{0:T(128)S(1)}, s32[5]{0:T(128)}, u32[]{:S(2)}) copy-start(s32[5]{0:T(128)} %copy-done.6) | copy-start | bytes 64
  132.9 11.3 %collective-permute-start.19 = (bf16[4,64,256]{2,1,0:T(8,128)(2,1)}, bf16[4,64,256]{2,1,0:T(8,128)(2,1)S(1)}, u32[]{:S(2)}, u32[]{:S(2)}) collective-permute-start(bf16[4,64,256]{2,1,0:T(8,128)(2,1)} %get-tuple-element.95), channel_id=1, source_target_pairs={{0,16},{16,0},{32,48},{48,32},{64,80},{80,64},{96,112},{112,96},{1... | collective-permute-start | bytes 393224 | tf_op jit(solution)/shard_map/ppermute | solution.py:358
  134.5 9.8 %collective-permute-start.20 = (bf16[4,64,256]{2,1,0:T(8,128)(2,1)}, bf16[4,64,256]{2,1,0:T(8,128)(2,1)S(1)}, u32[]{:S(2)}, u32[]{:S(2)}) collective-permute-start(bf16[4,64,256]{2,1,0:T(8,128)(2,1)} %get-tuple-element.96), channel_id=1, source_target_pairs={{0,32},{16,48},{32,0},{48,16},{64,96},{80,112},{96,64},{112,80},{1... | collective-permute-start | bytes 393224 | tf_op jit(solution)/shard_map/ppermute | solution.py:358
  135.8 8.5 %collective-permute-start.21 = (bf16[4,64,256]{2,1,0:T(8,128)(2,1)}, bf16[4,64,256]{2,1,0:T(8,128)(2,1)S(1)}, u32[]{:S(2)}, u32[]{:S(2)}) collective-permute-start(bf16[4,64,256]{2,1,0:T(8,128)(2,1)} %get-tuple-element.97), channel_id=1, source_target_pairs={{0,48},{16,32},{32,16},{48,0},{64,112},{80,96},{96,80},{112,64},{1... | collective-permute-start | bytes 393224 | tf_op jit(solution)/shard_map/ppermute | solution.py:358
  144.3 25.6 %all-to-all-start.3 = ((bf16[16,2,64,256]{3,2,1,0:T(8,128)(2,1)}), bf16[16,2,64,256]{3,2,1,0:T(8,128)(2,1)S(1)}, u32[]{:S(2)}, u32[]{:S(2)}) async-start(bf16[16,2,64,256]{3,2,1,0:T(8,128)(2,1)} %bitcast.16), calls=%async_computation.3 | async-start | bytes 2097152 | tf_op jit(solution)/shard_map/panels_out/all_to_all | solution.py:443
  151.9 10.1 %collective-permute-start.22 = (bf16[4,64,256]{2,1,0:T(8,128)(2,1)S(1)}, bf16[4,64,256]{2,1,0:T(8,128)(2,1)S(1)}, u32[]{:S(2)}, u32[]{:S(2)}) collective-permute-start(bf16[4,64,256]{2,1,0:T(8,128)(2,1)S(1)} %get-tuple-element.103), channel_id=1, source_target_pairs={{0,64},{32,96},{64,128},{96,160},{128,192},{160,224},{192,0},{224,... | collective-permute-start | bytes 393224 | tf_op jit(solution)/shard_map/side_out/ppermute | solution.py:367
  154.5 12.2 %collective-permute-start.23 = (bf16[4,64,256]{2,1,0:T(8,128)(2,1)S(1)}, bf16[4,64,256]{2,1,0:T(8,128)(2,1)S(1)}, u32[]{:S(2)}, u32[]{:S(2)}) collective-permute-start(bf16[4,64,256]{2,1,0:T(8,128)(2,1)S(1)} %get-tuple-element.104), channel_id=1, source_target_pairs={{0,128},{32,160},{64,192},{96,224},{128,0},{160,32},{192,64},{224,... | collective-permute-start | bytes 393224 | tf_op jit(solution)/shard_map/side_out/ppermute | solution.py:367
  158.1 11.8 %collective-permute-start.24 = (bf16[4,64,256]{2,1,0:T(8,128)(2,1)S(1)}, bf16[4,64,256]{2,1,0:T(8,128)(2,1)S(1)}, u32[]{:S(2)}, u32[]{:S(2)}) collective-permute-start(bf16[4,64,256]{2,1,0:T(8,128)(2,1)S(1)} %get-tuple-element.105), channel_id=1, source_target_pairs={{0,192},{32,224},{64,0},{96,32},{128,64},{160,96},{192,128},{224,1... | collective-permute-start | bytes 393224 | tf_op jit(solution)/shard_map/side_out/ppermute | solution.py:367
